TPU v7x, 32 devices: a whole 2x2x4 slice. The times are simulated.
32 devices in a mesh: tm: 8 (over z, y), head: 4 (over x, core).
Axes of the slice: x: 2, y: 2, z: 4, core: 2. Of those that a mesh axis runs over, the one named last changes fastest.
Arguments:
- query_rows: bfloat16 [4096, 1536], P('tm', 'head'), may hold values from -5 to 5
- key_rows: bfloat16 [4096, 1536], P('tm', 'head'), may hold values from -5 to 5
- value_rows: bfloat16 [4096, 1536], P('tm', 'head'), may hold values from -6 to 6
- output_weight: bfloat16 [1536, 1536], P('head'), may hold values from -0.15625 to 0.15625
- output_grad: bfloat16 [4096, 1536], P('tm', 'head'), may hold values from -6 to 6
- anchor: int32 [8], replicated, may hold values from 0 to 7, as said below
Outputs:
- layer_output: bfloat16 [4096, 1536], P('tm', 'head')
- query_grad: bfloat16 [4096, 1536], P('tm', 'head')
- key_grad: bfloat16 [4096, 1536], P('tm', 'head')
- value_grad: bfloat16 [4096, 1536], P('tm', 'head')
- weight_grad: float32 [1536, 1536], P('head')
Inputs may be any that keep to these rules, and one draw needn't show every extreme that they name: anchor[0] = 0; anchor[f] is f or anchor[f - 1]; f - anchor[f] is below 4; the segment that starts at frame 8 // 2 - 2 has exactly 4 frames.
All inputs are finite; a program needn't handle non-finite values.
Results may differ from a plain program's by a relative error of at most 0.0083.
Values may be sent and summed in bfloat16 or wider, within the bound.
No kernel may reach another device: no remote copies, remote signals or barrier semaphores. Data moves between devices by JAX's collectives and lax.ppermute only.
A program may use at most 128 MiB of HBM per device.

v0:
```python
import jax
import jax.numpy as jnp
from jax import lax
from jax.sharding import PartitionSpec as P

HEAD_DIM = 128


def from_behind(array, axis, by):
    length = lax.axis_size(axis)
    pairs = [(i, i + by) for i in range(length) if 0 <= i + by < length]
    return lax.ppermute(array, axis, pairs)


def split_heads(array, head_size):
    return array.reshape(array.shape[0], array.shape[1] // head_size, head_size)


def local(query_rows, key_rows, value_rows, output_weight, output_grad, anchor):
    head_size = HEAD_DIM
    scaling = head_size ** (-0.5)
    row_count, col_count = query_rows.shape
    frame_count = anchor.shape[0]
    position = lax.axis_index("tm")
    frame_ids = jnp.arange(frame_count, dtype=jnp.int32)
    anchor_of = jnp.sum(jnp.where(frame_ids == position, anchor, 0))
    is_start = anchor_of == position
    next_anchor = jnp.sum(jnp.where(frame_ids == position + 1, anchor, 0))
    next_start = next_anchor == position + 1
    segment_most = min(8, lax.axis_size("tm") // 2)
    neighbour = from_behind((key_rows, value_rows), "tm", 1)
    prev_keys = jnp.where(is_start, key_rows, neighbour[0])
    prev_values = jnp.where(is_start, value_rows, neighbour[1])
    anchor_keys = prev_keys
    anchor_values = prev_values
    for repeat in range(segment_most - 2):
        fetched = from_behind((anchor_keys, anchor_values), "tm", 1)
        anchor_keys = jnp.where(is_start, key_rows, fetched[0])
        anchor_values = jnp.where(is_start, value_rows, fetched[1])
    key_heads = split_heads(jnp.concatenate([anchor_keys, prev_keys, key_rows], 0), head_size)
    value_heads = split_heads(
        jnp.concatenate([anchor_values, prev_values, value_rows], 0), head_size
    )
    query_heads = split_heads(query_rows, head_size)
    scores = (
        jnp.einsum("qhd,khd->hqk", query_heads, key_heads, preferred_element_type=jnp.float32)
        * scaling
    )
    highest = jnp.max(scores, axis=-1, keepdims=True)
    raw_weights = jnp.exp(scores - highest)
    probabilities = raw_weights / jnp.sum(raw_weights, axis=-1, keepdims=True)
    rounded = probabilities.astype(jnp.bfloat16)
    attended = jnp.einsum("hqk,khd->qhd", rounded, value_heads, preferred_element_type=jnp.float32)
    attended = attended.astype(jnp.bfloat16).reshape(row_count, col_count)
    partial_value = jnp.dot(attended, output_weight, preferred_element_type=jnp.float32)
    layer_output = lax.psum_scatter(partial_value, "head", scatter_dimension=1, tiled=True).astype(
        jnp.bfloat16
    )
    grad_full = lax.all_gather(output_grad, "head", axis=1, tiled=True)
    attended_grad = lax.dot_general(
        grad_full, output_weight, (((1,), (1,)), ((), ())), preferred_element_type=jnp.float32
    ).astype(jnp.bfloat16)
    weight_term = lax.dot_general(
        attended, grad_full, (((0,), (0,)), ((), ())), preferred_element_type=jnp.float32
    )
    weight_grad = lax.psum(weight_term, "tm")
    grad_heads = split_heads(attended_grad, head_size)
    value_blocks = jnp.einsum(
        "hqk,qhd->khd", rounded, grad_heads, preferred_element_type=jnp.float32
    )
    value_blocks = value_blocks.reshape(3 * row_count, col_count)
    prob_grad = jnp.einsum(
        "qhd,khd->hqk", grad_heads, value_heads, preferred_element_type=jnp.float32
    )
    row_delta = jnp.sum(probabilities * prob_grad, axis=-1, keepdims=True)
    score_grad = (probabilities * (prob_grad - row_delta) * scaling).astype(jnp.bfloat16)
    query_grad = jnp.einsum(
        "hqk,khd->qhd", score_grad, key_heads, preferred_element_type=jnp.float32
    )
    query_grad = query_grad.astype(jnp.bfloat16).reshape(row_count, col_count)
    key_blocks = jnp.einsum(
        "hqk,qhd->khd", score_grad, query_heads, preferred_element_type=jnp.float32
    )
    key_blocks = key_blocks.reshape(3 * row_count, col_count)
    key_anchor = key_blocks[:row_count]
    key_previous = key_blocks[row_count : 2 * row_count]
    value_anchor = value_blocks[:row_count]
    value_previous = value_blocks[row_count : 2 * row_count]
    key_total = key_blocks[2 * row_count :] + jnp.where(is_start, key_anchor + key_previous, 0.0)
    value_total = value_blocks[2 * row_count :] + jnp.where(
        is_start, value_anchor + value_previous, 0.0
    )
    returned = from_behind(
        (jnp.where(is_start, 0.0, key_previous), jnp.where(is_start, 0.0, value_previous)), "tm", -1
    )
    key_total = key_total + returned[0]
    value_total = value_total + returned[1]
    key_send = jnp.where(is_start, 0.0, key_anchor)
    value_send = jnp.where(is_start, 0.0, value_anchor)
    key_running = key_send
    value_running = value_send
    key_passed = jnp.zeros_like(key_send)
    value_passed = jnp.zeros_like(value_send)
    for repeat in range(segment_most - 1):
        arrived = from_behind((key_running, value_running), "tm", -1)
        key_passed = jnp.where(next_start, 0.0, arrived[0])
        value_passed = jnp.where(next_start, 0.0, arrived[1])
        key_running = jnp.where(is_start, 0.0, key_send + key_passed)
        value_running = jnp.where(is_start, 0.0, value_send + value_passed)
    key_total = key_total + jnp.where(is_start, key_passed, 0.0)
    value_total = value_total + jnp.where(is_start, value_passed, 0.0)
    return (
        layer_output,
        query_grad,
        key_total.astype(jnp.bfloat16),
        value_total.astype(jnp.bfloat16),
        weight_grad,
    )


def solution(mesh):
    in_specs = (
        P("tm", "head"),
        P("tm", "head"),
        P("tm", "head"),
        P("head", None),
        P("tm", "head"),
        P(),
    )
    out_specs = (
        P("tm", "head"),
        P("tm", "head"),
        P("tm", "head"),
        P("tm", "head"),
        P("head", None),
    )
    return jax.shard_map(local, mesh=mesh, in_specs=in_specs, out_specs=out_specs, check_vma=False)
```

profile of v0, /device:TPU:12, one launch (start us, length us, event | category | flops | bytes accessed | tf_op | source)
XLA Modules:
  0.0 324.0 jit_solution(2364208206808198318)
XLA Ops:
  7.2 1.3 copy.37
  8.5 3.4 %collective-permute-start = (bf16[512,384]{0,1:T(8,128)(2,1)S(1)}, bf16[512,384]{0,1:T(8,128)(2,1)S(1)}, u32[]{:S(2)}, u32[]{:S(2)}) collective-permute-start(bf16[512,384]{0,1:T(8,128)(2,1)S(1)} %copy.37), channel_id=1, source_target_pairs={{0,4},{4,8},{8,12},{12,16},{16,20},{20,24},{24,28},{1,5},{5,9},{9,... | collective-permute-start | bytes 1179656 | tf_op jit(solution)/shard_map/ppermute | solution.py:12
  13.1 3.4 %collective-permute-start.3 = (bf16[512,384]{0,1:T(8,128)(2,1)S(1)}, bf16[512,384]{0,1:T(8,128)(2,1)S(1)}, u32[]{:S(2)}, u32[]{:S(2)}) collective-permute-start(bf16[512,384]{0,1:T(8,128)(2,1)S(1)} %copy.42), channel_id=1, source_target_pairs={{0,4},{4,8},{8,12},{12,16},{16,20},{20,24},{24,28},{1,5},{5,9},{9,... | collective-permute-start | bytes 1179656 | tf_op jit(solution)/shard_map/ppermute | solution.py:12
  16.6 1.3 fusion.36
  18.5 3.9 %collective-permute-done = bf16[512,384]{0,1:T(8,128)(2,1)S(1)} collective-permute-done((bf16[512,384]{0,1:T(8,128)(2,1)S(1)}, bf16[512,384]{0,1:T(8,128)(2,1)S(1)}, u32[]{:S(2)}, u32[]{:S(2)}) %collective-permute-start) | collective-permute-done | bytes 393248 | tf_op jit(solution)/shard_map/ppermute | solution.py:12
  22.5 4.3 %collective-permute-start.1 = (bf16[512,384]{0,1:T(8,128)(2,1)S(1)}, bf16[512,384]{0,1:T(8,128)(2,1)S(1)}, u32[]{:S(2)}, u32[]{:S(2)}) collective-permute-start(bf16[512,384]{0,1:T(8,128)(2,1)S(1)} %broadcast_select_fusion.5), channel_id=1, source_target_pairs={{0,4},{4,8},{8,12},{12,16},{16,20},{20,24},{24,28},{1,5},{5,9},{9,... | collective-permute-start | bytes 1179656 | tf_op jit(solution)/shard_map/ppermute | solution.py:12
  26.8 4.0 %collective-permute-done.3 = bf16[512,384]{0,1:T(8,128)(2,1)S(1)} collective-permute-done((bf16[512,384]{0,1:T(8,128)(2,1)S(1)}, bf16[512,384]{0,1:T(8,128)(2,1)S(1)}, u32[]{:S(2)}, u32[]{:S(2)}) %collective-permute-start.3) | collective-permute-done | bytes 393248 | tf_op jit(solution)/shard_map/ppermute | solution.py:12
  30.9 4.3 %collective-permute-start.4 = (bf16[512,384]{0,1:T(8,128)(2,1)S(1)}, bf16[512,384]{0,1:T(8,128)(2,1)}, u32[]{:S(2)}, u32[]{:S(2)}) collective-permute-start(bf16[512,384]{0,1:T(8,128)(2,1)S(1)} %broadcast_select_fusion.2), channel_id=1, source_target_pairs={{0,4},{4,8},{8,12},{12,16},{16,20},{20,24},{24,28},{1,5},{5,9},{9,... | collective-permute-start | bytes 1179656 | tf_op jit(solution)/shard_map/ppermute | solution.py:12
  35.2 4.0 %collective-permute-done.1 = bf16[512,384]{0,1:T(8,128)(2,1)S(1)} collective-permute-done((bf16[512,384]{0,1:T(8,128)(2,1)S(1)}, bf16[512,384]{0,1:T(8,128)(2,1)S(1)}, u32[]{:S(2)}, u32[]{:S(2)}) %collective-permute-start.1) | collective-permute-done | bytes 393248 | tf_op jit(solution)/shard_map/ppermute | solution.py:12
  39.3 4.3 %collective-permute-start.2 = (bf16[512,384]{0,1:T(8,128)(2,1)S(1)}, bf16[512,384]{0,1:T(8,128)(2,1)S(1)}, u32[]{:S(2)}, u32[]{:S(2)}) collective-permute-start(bf16[512,384]{0,1:T(8,128)(2,1)S(1)} %broadcast_select_fusion.4), channel_id=1, source_target_pairs={{0,4},{4,8},{8,12},{12,16},{16,20},{20,24},{24,28},{1,5},{5,9},{9,... | collective-permute-start | bytes 1179656 | tf_op jit(solution)/shard_map/ppermute | solution.py:12
  44.7 3.1 collective-permute-done.4
  48.9 4.3 %collective-permute-start.5 = (bf16[512,384]{0,1:T(8,128)(2,1)S(1)}, bf16[512,384]{0,1:T(8,128)(2,1)S(1)}, u32[]{:S(2)}, u32[]{:S(2)}) collective-permute-start(bf16[512,384]{0,1:T(8,128)(2,1)S(1)} %broadcast_select_fusion.1), channel_id=1, source_target_pairs={{0,4},{4,8},{8,12},{12,16},{16,20},{20,24},{24,28},{1,5},{5,9},{9,... | collective-permute-start | bytes 1179656 | tf_op jit(solution)/shard_map/ppermute | solution.py:12
  53.2 2.9 collective-permute-done.2
  57.3 6.2 %collective-permute-done.5 = bf16[512,384]{0,1:T(8,128)(2,1)S(1)} collective-permute-done((bf16[512,384]{0,1:T(8,128)(2,1)S(1)}, bf16[512,384]{0,1:T(8,128)(2,1)S(1)}, u32[]{:S(2)}, u32[]{:S(2)}) %collective-permute-start.5) | collective-permute-done | bytes 393248 | tf_op jit(solution)/shard_map/ppermute | solution.py:12
  64.7 8.4 %fusion.42 = (f32[3,512]{1,0:T(4,128)S(1)}, f32[3,512,1536]{1,2,0:T(8,128)}) fusion(bf16[1536,3,128]{0,2,1:T(8,128)(2,1)} %bitcast.67, bf16[512,3,128]{0,2,1:T(8,128)(2,1)} %bitcast.73), kind=kOutput, calls=%fused_computation.56 | convolution fusion | flops 611059200 | bytes 11016192 | tf_op jit(solution)/shard_map/sub | solution.py:50
  73.1 4.5 %fusion.23 = bf16[3,128,512]{2,1,0:T(8,128)(2,1)S(1)} fusion(bf16[1536,3,128]{0,2,1:T(8,128)(2,1)S(1)} %bitcast.63, f32[3,512,1536]{1,2,0:T(8,128)} %get-tuple-element.24, f32[3,512]{1,0:T(4,128)S(1)} %get-tuple-element.23), kind=kOutput, calls=%fused_computation.19 | convolution fusion | flops 608894976 | bytes 11016192 | tf_op jit(solution)/shard_map/hqk,khd->qhd/dot_general | solution.py:53
  77.6 2.7 fusion.43
  80.4 2.2 convolution_convert_fusion
  82.6 5.1 %fusion.44 = f32[3,512,1536]{1,2,0:T(8,128)} fusion(bf16[512,3,128]{0,2,1:T(8,128)(2,1)S(1)} %bitcast.71, bf16[1536,3,128]{0,2,1:T(8,128)(2,1)S(1)} %bitcast.64), kind=kOutput, calls=%fused_computation.58 | convolution fusion | flops 603979776 | bytes 11010048 | tf_op jit(solution)/shard_map/qhd,khd->hqk/dot_general | solution.py:72
  87.7 16.6 %fusion.17 = f32[1536,3,128]{0,2,1:T(8,128)} fusion(bf16[512,3,128]{0,2,1:T(8,128)(2,1)S(1)} %bitcast.74, f32[3,512,1536]{1,2,0:T(8,128)} %fusion.44, f32[3,512,1536]{1,2,0:T(8,128)} %get-tuple-element.24, f32[3,512]{1,0:T(4,128)S(1)} %get-tuple-element.23), kind=kOutput, calls=%fused_computation.14 | convolution fusion | flops 620497920 | bytes 21633024 | tf_op jit(solution)/shard_map/hqk,qhd->khd/dot_general | solution.py:81
  104.3 3.2 slice_select_fusion.3
  107.4 3.3 %collective-permute-start.7 = (f32[512,384]{0,1:T(8,128)S(1)}, f32[512,384]{0,1:T(8,128)}, u32[]{:S(2)}, u32[]{:S(2)}) collective-permute-start(f32[512,384]{0,1:T(8,128)S(1)} %bitcast.62), channel_id=1, source_target_pairs={{4,0},{8,4},{12,8},{16,12},{20,16},{24,20},{28,24},{5,1},{9,5},{13... | collective-permute-start | bytes 2359304 | tf_op jit(solution)/shard_map/ppermute | solution.py:12
  110.7 5.4 %convolution_bitcast_fusion = f32[1536,3,128]{0,2,1:T(8,128)S(1)} fusion(bf16[512,3,128]{0,2,1:T(8,128)(2,1)S(1)} %bitcast.72, f32[3,512,1536]{1,2,0:T(8,128)} %get-tuple-element.24, f32[3,512]{1,0:T(4,128)S(1)} %get-tuple-element.23), kind=kOutput, calls=%fused_computation.15 | convolution fusion | flops 608698368 | bytes 12195840 | tf_op jit(solution)/shard_map/hqk,qhd->khd/dot_general | solution.py:68
  116.1 1.5 slice_select_fusion.1
  117.6 2.6 collective-permute-start.11
  120.9 9.9 %collective-permute-done.7 = f32[512,384]{0,1:T(8,128)} collective-permute-done((f32[512,384]{0,1:T(8,128)S(1)}, f32[512,384]{0,1:T(8,128)}, u32[]{:S(2)}, u32[]{:S(2)}) %collective-permute-start.7) | collective-permute-done | bytes 786464 | tf_op jit(solution)/shard_map/ppermute | solution.py:12
  130.8 2.2 add_select_fusion.3
  133.0 2.4 collective-permute-start.8
  135.4 3.6 %fusion.45 = f32[384,1536]{1,0:T(8,128)} fusion(bf16[512,384]{0,1:T(8,128)(2,1)S(1)} %bitcast.66, bf16[512,1536]{1,0:T(8,128)(2,1)} %all-gather.2.cloned.1.call-done), kind=kOutput, calls=%fused_computation.59 | convolution fusion | flops 603979776 | bytes 4325376 | tf_op jit(solution)/shard_map/dot_general | solution.py:63
  139.0 8.6 %collective-permute-done.11 = f32[512,384]{0,1:T(8,128)} collective-permute-done((f32[512,384]{0,1:T(8,128)S(1)}, f32[512,384]{0,1:T(8,128)}, u32[]{:S(2)}, u32[]{:S(2)}) %collective-permute-start.11) | collective-permute-done | bytes 786464 | tf_op jit(solution)/shard_map/ppermute | solution.py:12
  148.9 2.4 collective-permute-start.12
  151.3 2.2 collective-permute-start.6
  153.6 32.0 %collective-permute-done.8 = f32[512,384]{0,1:T(8,128)} collective-permute-done((f32[512,384]{0,1:T(8,128)}, f32[512,384]{0,1:T(8,128)}, u32[]{:S(2)}, u32[]{:S(2)}) %collective-permute-start.8) | collective-permute-done | bytes 786464 | tf_op jit(solution)/shard_map/ppermute | solution.py:12
  185.5 2.2 add_select_fusion.2
  187.7 4.7 %collective-permute-start.9 = (f32[512,384]{0,1:T(8,128)}, f32[512,384]{0,1:T(8,128)S(1)}, u32[]{:S(2)}, u32[]{:S(2)}) collective-permute-start(f32[512,384]{0,1:T(8,128)} %add_select_fusion.2), channel_id=1, source_target_pairs={{4,0},{8,4},{12,8},{16,12},{20,16},{24,20},{28,24},{5,1},{9,5},{13... | collective-permute-start | bytes 2359304 | tf_op jit(solution)/shard_map/ppermute | solution.py:12
  192.4 4.2 %collective-permute-start.10 = (f32[512,384]{0,1:T(8,128)}, f32[512,384]{0,1:T(8,128)}, u32[]{:S(2)}, u32[]{:S(2)}) collective-permute-start(f32[512,384]{0,1:T(8,128)} %bitcast.69), channel_id=1, source_target_pairs={{4,0},{8,4},{12,8},{16,12},{20,16},{24,20},{28,24},{5,1},{9,5},{13... | collective-permute-start | bytes 2359304 | tf_op jit(solution)/shard_map/ppermute | solution.py:12
  196.6 10.0 %collective-permute-done.12 = f32[512,384]{0,1:T(8,128)S(1)} collective-permute-done((f32[512,384]{0,1:T(8,128)S(1)}, f32[512,384]{0,1:T(8,128)S(1)}, u32[]{:S(2)}, u32[]{:S(2)}) %collective-permute-start.12) | collective-permute-done | bytes 786464 | tf_op jit(solution)/shard_map/ppermute | solution.py:12
  207.7 2.0 collective-permute-start.13
  209.7 14.6 %fusion.26 = bf16[3,128,512]{2,1,0:T(8,128)(2,1)} fusion(bf16[1536,3,128]{0,2,1:T(8,128)(2,1)} %bitcast.68, f32[3,512,1536]{1,2,0:T(8,128)} %fusion.44, f32[3,512,1536]{1,2,0:T(8,128)} %get-tuple-element.24, f32[3,512]{1,0:T(4,128)S(1)} %get-tuple-element.23), kind=kOutput, calls=%fused_computation.20 | convolution fusion | flops 620694528 | bytes 20453376 | tf_op jit(solution)/shard_map/hqk,khd->qhd/dot_general | solution.py:77
  224.3 2.0 copy.55
  226.3 3.5 %collective-permute-done.6 = f32[512,384]{0,1:T(8,128)} collective-permute-done((f32[512,384]{0,1:T(8,128)}, f32[512,384]{0,1:T(8,128)}, u32[]{:S(2)}, u32[]{:S(2)}) %collective-permute-start.6) | collective-permute-done | bytes 786464 | tf_op jit(solution)/shard_map/ppermute | solution.py:12
  229.8 23.1 %collective-permute-done.9 = f32[512,384]{0,1:T(8,128)S(1)} collective-permute-done((f32[512,384]{0,1:T(8,128)}, f32[512,384]{0,1:T(8,128)S(1)}, u32[]{:S(2)}, u32[]{:S(2)}) %collective-permute-start.9) | collective-permute-done | bytes 786464 | tf_op jit(solution)/shard_map/ppermute | solution.py:12
  253.8 1.6 fusion.34
  256.3 27.1 %collective-permute-done.10 = f32[512,384]{0,1:T(8,128)} collective-permute-done((f32[512,384]{0,1:T(8,128)}, f32[512,384]{0,1:T(8,128)}, u32[]{:S(2)}, u32[]{:S(2)}) %collective-permute-start.10) | collective-permute-done | bytes 786464 | tf_op jit(solution)/shard_map/ppermute | solution.py:12
  283.4 26.5 %collective-permute-done.13 = f32[512,384]{0,1:T(8,128)} collective-permute-done((f32[512,384]{0,1:T(8,128)}, f32[512,384]{0,1:T(8,128)}, u32[]{:S(2)}, u32[]{:S(2)}) %collective-permute-start.13) | collective-permute-done | bytes 786464 | tf_op jit(solution)/shard_map/ppermute | solution.py:12
  309.9 1.6 fusion.32
  312.4 1.9 convert_element_type.33
  314.3 3.2 copy.68
  (37 shorter events, 10.9 us)
Async XLA Ops:
  7.2 70.4 %copy-start = (bf16[384,1536]{1,0:T(8,128)(2,1)S(1)}, bf16[384,1536]{1,0:T(8,128)(2,1)}, u32[]{:S(2)}) copy-start(bf16[384,1536]{1,0:T(8,128)(2,1)} %param.9) | copy-start | bytes 3538948
  7.2 36.6 %copy-start.5 = (bf16[512,384]{1,0:T(8,128)(2,1)S(1)}, bf16[512,384]{1,0:T(8,128)(2,1)}, u32[]{:S(2)}) copy-start(bf16[512,384]{1,0:T(8,128)(2,1)} %param.6) | copy-start | bytes 1179652
  7.2 73.2 %all-gather.2.cloned.1.call-start = ((), (), s32[]{:S(2)}) async-start(), calls=%async_computation.2 | async-start | bytes 1966080 | tf_op jit(solution)/shard_map/all_gather | solution.py:59
  8.5 13.9 %collective-permute-start = (bf16[512,384]{0,1:T(8,128)(2,1)S(1)}, bf16[512,384]{0,1:T(8,128)(2,1)S(1)}, u32[]{:S(2)}, u32[]{:S(2)}) collective-permute-start(bf16[512,384]{0,1:T(8,128)(2,1)S(1)} %copy.37), channel_id=1, source_target_pairs={{0,4},{4,8},{8,12},{12,16},{16,20},{20,24},{24,28},{1,5},{5,9},{9,... | collective-permute-start | bytes 1179656 | tf_op jit(solution)/shard_map/ppermute | solution.py:12
  13.1 17.7 %collective-permute-start.3 = (bf16[512,384]{0,1:T(8,128)(2,1)S(1)}, bf16[512,384]{0,1:T(8,128)(2,1)S(1)}, u32[]{:S(2)}, u32[]{:S(2)}) collective-permute-start(bf16[512,384]{0,1:T(8,128)(2,1)S(1)} %copy.42), channel_id=1, source_target_pairs={{0,4},{4,8},{8,12},{12,16},{16,20},{20,24},{24,28},{1,5},{5,9},{9,... | collective-permute-start | bytes 1179656 | tf_op jit(solution)/shard_map/ppermute | solution.py:12
  22.5 8.4 %copy-start.3 = (bf16[512,384]{0,1:T(8,128)(2,1)}, bf16[512,384]{0,1:T(8,128)(2,1)S(1)}, u32[]{:S(2)}) copy-start(bf16[512,384]{0,1:T(8,128)(2,1)S(1)} %broadcast_select_fusion.5) | copy-start | bytes 1179652
  22.5 16.8 %collective-permute-start.1 = (bf16[512,384]{0,1:T(8,128)(2,1)S(1)}, bf16[512,384]{0,1:T(8,128)(2,1)S(1)}, u32[]{:S(2)}, u32[]{:S(2)}) collective-permute-start(bf16[512,384]{0,1:T(8,128)(2,1)S(1)} %broadcast_select_fusion.5), channel_id=1, source_target_pairs={{0,4},{4,8},{8,12},{12,16},{16,20},{20,24},{24,28},{1,5},{5,9},{9,... | collective-permute-start | bytes 1179656 | tf_op jit(solution)/shard_map/ppermute | solution.py:12
  30.9 16.9 %collective-permute-start.4 = (bf16[512,384]{0,1:T(8,128)(2,1)S(1)}, bf16[512,384]{0,1:T(8,128)(2,1)}, u32[]{:S(2)}, u32[]{:S(2)}) collective-permute-start(bf16[512,384]{0,1:T(8,128)(2,1)S(1)} %broadcast_select_fusion.2), channel_id=1, source_target_pairs={{0,4},{4,8},{8,12},{12,16},{16,20},{20,24},{24,28},{1,5},{5,9},{9,... | collective-permute-start | bytes 1179656 | tf_op jit(solution)/shard_map/ppermute | solution.py:12
  39.3 16.8 %collective-permute-start.2 = (bf16[512,384]{0,1:T(8,128)(2,1)S(1)}, bf16[512,384]{0,1:T(8,128)(2,1)S(1)}, u32[]{:S(2)}, u32[]{:S(2)}) collective-permute-start(bf16[512,384]{0,1:T(8,128)(2,1)S(1)} %broadcast_select_fusion.4), channel_id=1, source_target_pairs={{0,4},{4,8},{8,12},{12,16},{16,20},{20,24},{24,28},{1,5},{5,9},{9,... | collective-permute-start | bytes 1179656 | tf_op jit(solution)/shard_map/ppermute | solution.py:12
  43.7 268.7 %reduce-scatter.2.cloned.1.call-start = ((), (), s32[]{:S(2)}) async-start(), calls=%async_computation.1 | async-start | bytes 3932160 | tf_op jit(solution)/shard_map/reduce_scatter | solution.py:56
  48.9 14.6 %collective-permute-start.5 = (bf16[512,384]{0,1:T(8,128)(2,1)S(1)}, bf16[512,384]{0,1:T(8,128)(2,1)S(1)}, u32[]{:S(2)}, u32[]{:S(2)}) collective-permute-start(bf16[512,384]{0,1:T(8,128)(2,1)S(1)} %broadcast_select_fusion.1), channel_id=1, source_target_pairs={{0,4},{4,8},{8,12},{12,16},{16,20},{20,24},{24,28},{1,5},{5,9},{9,... | collective-permute-start | bytes 1179656 | tf_op jit(solution)/shard_map/ppermute | solution.py:12
  80.3 234.0 %all-reduce.2.cloned.1.call-start = ((), (), s32[]{:S(2)}) async-start(), calls=%async_computation.3 | async-start | bytes 4718592 | tf_op jit(solution)/shard_map/psum | solution.py:66
  82.6 5.1 %copy-start.6 = (bf16[512,384]{0,1:T(8,128)(2,1)S(1)}, bf16[512,384]{0,1:T(8,128)(2,1)}, u32[]{:S(2)}) copy-start(bf16[512,384]{0,1:T(8,128)(2,1)} %copy.44) | copy-start | bytes 1179652
  107.4 23.4 %collective-permute-start.7 = (f32[512,384]{0,1:T(8,128)S(1)}, f32[512,384]{0,1:T(8,128)}, u32[]{:S(2)}, u32[]{:S(2)}) collective-permute-start(f32[512,384]{0,1:T(8,128)S(1)} %bitcast.62), channel_id=1, source_target_pairs={{4,0},{8,4},{12,8},{16,12},{20,16},{24,20},{28,24},{5,1},{9,5},{13... | collective-permute-start | bytes 2359304 | tf_op jit(solution)/shard_map/ppermute | solution.py:12
  117.6 30.0 %collective-permute-start.11 = (f32[512,384]{0,1:T(8,128)S(1)}, f32[512,384]{0,1:T(8,128)}, u32[]{:S(2)}, u32[]{:S(2)}) collective-permute-start(f32[512,384]{0,1:T(8,128)S(1)} %bitcast.61), channel_id=1, source_target_pairs={{4,0},{8,4},{12,8},{16,12},{20,16},{24,20},{28,24},{5,1},{9,5},{13... | collective-permute-start | bytes 2359304 | tf_op jit(solution)/shard_map/ppermute | solution.py:12
  133.0 52.5 %collective-permute-start.8 = (f32[512,384]{0,1:T(8,128)}, f32[512,384]{0,1:T(8,128)}, u32[]{:S(2)}, u32[]{:S(2)}) collective-permute-start(f32[512,384]{0,1:T(8,128)} %add_select_fusion.3), channel_id=1, source_target_pairs={{4,0},{8,4},{12,8},{16,12},{20,16},{24,20},{28,24},{5,1},{9,5},{13... | collective-permute-start | bytes 2359304 | tf_op jit(solution)/shard_map/ppermute | solution.py:12
  148.9 57.7 %collective-permute-start.12 = (f32[512,384]{0,1:T(8,128)S(1)}, f32[512,384]{0,1:T(8,128)S(1)}, u32[]{:S(2)}, u32[]{:S(2)}) collective-permute-start(f32[512,384]{0,1:T(8,128)S(1)} %add_select_fusion.1), channel_id=1, source_target_pairs={{4,0},{8,4},{12,8},{16,12},{20,16},{24,20},{28,24},{5,1},{9,5},{13... | collective-permute-start | bytes 2359304 | tf_op jit(solution)/shard_map/ppermute | solution.py:12
  151.3 78.5 %collective-permute-start.6 = (f32[512,384]{0,1:T(8,128)}, f32[512,384]{0,1:T(8,128)}, u32[]{:S(2)}, u32[]{:S(2)}) collective-permute-start(f32[512,384]{0,1:T(8,128)} %bitcast.70), channel_id=1, source_target_pairs={{4,0},{8,4},{12,8},{16,12},{20,16},{24,20},{28,24},{5,1},{9,5},{13... | collective-permute-start | bytes 2359304 | tf_op jit(solution)/shard_map/ppermute | solution.py:12
  187.7 65.2 %collective-permute-start.9 = (f32[512,384]{0,1:T(8,128)}, f32[512,384]{0,1:T(8,128)S(1)}, u32[]{:S(2)}, u32[]{:S(2)}) collective-permute-start(f32[512,384]{0,1:T(8,128)} %add_select_fusion.2), channel_id=1, source_target_pairs={{4,0},{8,4},{12,8},{16,12},{20,16},{24,20},{28,24},{5,1},{9,5},{13... | collective-permute-start | bytes 2359304 | tf_op jit(solution)/shard_map/ppermute | solution.py:12
  192.4 91.0 %collective-permute-start.10 = (f32[512,384]{0,1:T(8,128)}, f32[512,384]{0,1:T(8,128)}, u32[]{:S(2)}, u32[]{:S(2)}) collective-permute-start(f32[512,384]{0,1:T(8,128)} %bitcast.69), channel_id=1, source_target_pairs={{4,0},{8,4},{12,8},{16,12},{20,16},{24,20},{28,24},{5,1},{9,5},{13... | collective-permute-start | bytes 2359304 | tf_op jit(solution)/shard_map/ppermute | solution.py:12
  207.7 46.1 %copy-start.2 = (f32[512,3,128]{0,2,1:T(8,128)S(1)}, f32[512,3,128]{0,2,1:T(8,128)}, u32[]{:S(2)}) copy-start(f32[512,3,128]{0,2,1:T(8,128)} %get-tuple-element.22) | copy-start | bytes 2359300
  207.7 102.2 %collective-permute-start.13 = (f32[512,384]{0,1:T(8,128)}, f32[512,384]{0,1:T(8,128)}, u32[]{:S(2)}, u32[]{:S(2)}) collective-permute-start(f32[512,384]{0,1:T(8,128)} %add_select_fusion), channel_id=1, source_target_pairs={{4,0},{8,4},{12,8},{16,12},{20,16},{24,20},{28,24},{5,1},{9,5},{13... | collective-permute-start | bytes 2359304 | tf_op jit(solution)/shard_map/ppermute | solution.py:12
  224.3 85.5 %copy-start.1 = (f32[512,3,128]{0,2,1:T(8,128)S(1)}, f32[512,3,128]{0,2,1:T(8,128)}, u32[]{:S(2)}) copy-start(f32[512,3,128]{0,2,1:T(8,128)} %get-tuple-element.19) | copy-start | bytes 2359300
  252.9 0.9 copy-start.4
Sparse Core Ops, SparseCore 0:
  43.8 19.7 all-gather.1
  80.4 39.0 reduce-scatter.1
  139.1 148.7 all-reduce.1
where the time goes:
time: 325 us; the launch traced here: 324 us
  waiting for transfers between devices  165 us (51%)
  matrix products  63 us (19%)
  starting transfers between devices  48.1 us (15%)
  other arithmetic  21.3 us (7%)
  between operations  15.3 us (5%)
  local copies, waits for them, and re-layouts  11.4 us (4%)
    ppermute x14, waiting for transfers between devices, from_behind(): return lax.ppermute(array, axis, pairs)  165 us
    ppermute x14, starting transfers between devices, from_behind(): return lax.ppermute(array, axis, pairs)  48 us
    dot_general x1, matrix products, local(): jnp.einsum('hqk,qhd->khd', score_grad, query_heads, preferred_element_typ...  16.6 us
    dot_general x1, matrix products, local(): jnp.einsum('hqk,khd->qhd', score_grad, key_heads, preferred_element_type=...  14.6 us
    unnamed x21, local copies, waits for them, and re-layouts  11.4 us
    sub x1, matrix products, local(): raw_weights = jnp.exp(scores - highest)  8.44 us
  transfers between devices with their start and end apart: 17, of which 14 were waited for; matrix products, arithmetic and copies ran while one was open for 28% of the time, Pallas kernels for 0%

commit v1 on v0

v1 whole, which is shorter than its diff:
```python
import functools
import math

import jax
import jax.numpy as jnp
from jax import lax
from jax.experimental import pallas as pl
from jax.experimental.pallas import tpu as pltpu
from jax.sharding import PartitionSpec as P

HEAD_DIM = 128
BF16 = jnp.bfloat16
F32 = jnp.float32
SCALE = HEAD_DIM ** -0.5
SCALE_LOG2 = SCALE * math.log2(math.e)
Q_CHUNK = 256


def dot(a, b, dims):
    return lax.dot_general(a, b, (dims, ((), ())), preferred_element_type=F32)


def anchor_bounds(frames, seg):
    forced = frames // 2 - 2
    bounds = []
    for f in range(frames):
        if f < forced:
            bounds.append((max(0, f - seg + 1), f))
        elif f < forced + seg:
            bounds.append((forced, forced))
        else:
            bounds.append((max(forced + seg, f - seg + 1), f))
    return bounds


def vmem():
    return pl.BlockSpec(memory_space=pltpu.VMEM)


def smem():
    return pl.BlockSpec(memory_space=pltpu.SMEM)


def params():
    return pltpu.CompilerParams(vmem_limit_bytes=48 * 1024 * 1024)


def cotangent_kernel(own, across, beside, weight, out):
    head = lax.axis_index("head")
    width = own.shape[1]
    pieces = (own[...], beside[0], across[...], beside[1])
    total = None
    for m, piece in enumerate(pieces):
        start = pl.multiple_of((head ^ m) * width, 128)
        term = dot(piece, weight[:, pl.ds(start, width)], ((1,), (1,)))
        total = term if total is None else total + term
    out[...] = total.astype(BF16)


def gather_block(anchor, own, prev, far, extra_ref, kind):
    f = lax.axis_index("tm")
    a = anchor[f]
    mine = own[...]
    before = jnp.where(a < f, prev[kind], mine)
    distant = far[kind]
    if extra_ref is not None:
        distant = distant + extra_ref[...]
    first = jnp.where(f - a >= 2, distant, before)
    return first, before, mine


def forward_kernel(extra, anchor, q, k, v, prev, far, *rest):
    extra_k, extra_v = rest[:2] if extra else (None, None)
    grad, out, out_t, stats, keys, values = rest[2 if extra else 0 :]
    rows = q.shape[0]
    for block, part in enumerate(gather_block(anchor, k, prev, far, extra_k, 0)):
        keys[pl.ds(block * rows, rows), :] = part
    for block, part in enumerate(gather_block(anchor, v, prev, far, extra_v, 1)):
        values[pl.ds(block * rows, rows), :] = part
    for c in range(rows // Q_CHUNK):
        at = pl.ds(c * Q_CHUNK, Q_CHUNK)
        scores = dot(keys[...], q[at, :], ((1,), (1,)))
        highest = jnp.max(scores, axis=0, keepdims=True)
        raw = jnp.exp2((scores - highest) * SCALE_LOG2)
        total = jnp.sum(raw, axis=0, keepdims=True)
        attended = dot(values[...], raw.astype(BF16), ((0,), (0,))) / total
        out_t[:, at] = attended.astype(BF16)
        out[at, :] = attended.T.astype(BF16)
        delta = jnp.sum(attended * grad[at, :].astype(F32).T, axis=0, keepdims=True)
        stats[0, 0:1, at] = highest * SCALE_LOG2 + jnp.log2(total)
        stats[0, 1:2, at] = delta


def backward_kernel(extra, anchor, q, k, v, prev, far, *rest):
    extra_k, extra_v = rest[:2] if extra else (None, None)
    grad, stats, dq, own_grad, prev_grad, far_grad, keys, values, dk, dv = rest[2 if extra else 0 :]
    rows = q.shape[0]
    for block, part in enumerate(gather_block(anchor, k, prev, far, extra_k, 0)):
        keys[pl.ds(block * rows, rows), :] = part
    for block, part in enumerate(gather_block(anchor, v, prev, far, extra_v, 1)):
        values[pl.ds(block * rows, rows), :] = part
    for c in range(rows // Q_CHUNK):
        at = pl.ds(c * Q_CHUNK, Q_CHUNK)
        queries, cot = q[at, :], grad[at, :]
        scores = dot(keys[...], queries, ((1,), (1,)))
        prob = jnp.exp2(scores * SCALE_LOG2 - stats[0, 0:1, at])
        prob_grad = dot(values[...], cot, ((1,), (1,)))
        score_grad = (prob * (prob_grad - stats[0, 1:2, at])).astype(BF16)
        dv_term = dot(prob.astype(BF16), cot, ((1,), (0,)))
        dk_term = dot(score_grad, queries, ((1,), (0,)))
        if c == 0:
            dv[...] = dv_term
            dk[...] = dk_term
        else:
            dv[...] += dv_term
            dk[...] += dk_term
        dq_t = dot(keys[...], score_grad, ((0,), (0,))) * SCALE
        dq[at, :] = dq_t.T.astype(BF16)
    f = lax.axis_index("tm")
    a = anchor[f]
    for kind, (ref, factor) in enumerate(((dk, SCALE), (dv, None))):
        parts = [ref[pl.ds(block * rows, rows), :] for block in range(3)]
        if factor is not None:
            parts = [part * factor for part in parts]
        near = parts[1] + jnp.where(f - a >= 2, 0.0, parts[0])
        far_grad[kind] = jnp.where(f - a >= 2, parts[0], 0.0).astype(BF16)
        prev_grad[kind] = jnp.where(a < f, near, 0.0).astype(BF16)
        own_grad[kind] = parts[2] + jnp.where(a < f, 0.0, near)


def projection_kernel(attended_t, own, across, beside, keep, send, pieces):
    tm = lax.axis_index("tm")
    sel = (tm % 2) * 2 + (tm // 2) % 2
    pieces[0] = own[...]
    pieces[1] = beside[0]
    pieces[2] = across[...]
    pieces[3] = beside[1]
    for slot in range(4):
        term = dot(attended_t[...], pieces[slot ^ sel], ((1,), (0,)))
        if slot < 2:
            keep[slot] = term
        else:
            send[slot - 2] = term.astype(BF16)


def output_kernel(attended, weight, keep, send):
    head = lax.axis_index("head")
    width = weight.shape[0]
    for m in range(4):
        start = pl.multiple_of((head ^ m) * width, 128)
        part = dot(attended[...], weight[:, pl.ds(start, width)], ((1,), (0,)))
        if m % 2:
            send[m // 2] = part.astype(BF16)
        else:
            keep[m // 2] = part


def assemble_kernel(first, second, others, out):
    head = lax.axis_index("head")
    tm = lax.axis_index("tm")
    sel = (tm % 2) * 2 + (tm // 2) % 2
    width = first.shape[0]
    for slot in range(4):
        value = (first[...], second[...], others[0], others[1])[slot]
        start = pl.multiple_of((head ^ sel ^ slot) * width, 128)
        out[:, pl.ds(start, width)] = value.astype(out.dtype)


def swap(array, axis, bit):
    return lax.ppermute(array, axis, [(i, i ^ bit) for i in range(lax.axis_size(axis))])


def local(query_rows, key_rows, value_rows, output_weight, output_grad, anchor):
    rows, cols = query_rows.shape
    heads = cols // HEAD_DIM
    frames = lax.axis_size("tm")
    seg = min(8, frames // 2)
    bounds = anchor_bounds(frames, seg)
    position = lax.axis_index("tm")
    near_pairs = [(f - 1, f) for f in range(1, frames) if bounds[f][0] < f]
    far_frames = [f for f in range(frames) if f - bounds[f][0] >= 2]
    pair_plan = len(far_frames) == 2 and all(bounds[f][0] == bounds[f][1] for f in far_frames)

    def send(array, pairs):
        return lax.ppermute(array, "tm", pairs)

    def back(pairs):
        return [(b, a) for a, b in pairs]

    own_pair = jnp.stack([key_rows, value_rows])
    prev_pair = send(own_pair, near_pairs)
    if pair_plan:
        lower, upper = far_frames
        source = bounds[lower][0]
        far_pair = send(own_pair, [(source, lower)])
        extra = (send(key_rows, [(source, upper)]), send(prev_pair[1], [(source + 1, upper)]))
    else:
        own_anchor = jnp.sum(jnp.where(jnp.arange(frames) == position, anchor, 0))
        distance = position - own_anchor
        far_pair = jnp.where(distance == 0, own_pair, prev_pair)
        step = 2
        while step < seg:
            pairs = [(f - step, f) for f in range(step, frames) if f - bounds[f][0] >= step]
            far_pair = jnp.where(distance >= step, send(far_pair, pairs), far_pair)
            step *= 2
        extra = ()

    across = swap(output_grad, "head", 2)
    beside = swap(jnp.stack([output_grad, across]), "head", 1)
    attended_grad = pl.pallas_call(
        cotangent_kernel,
        out_shape=jax.ShapeDtypeStruct((rows, cols), BF16),
        in_specs=[vmem()] * 4,
        out_specs=vmem(),
        compiler_params=params(),
        name="cotangent",
    )(output_grad, across, beside, output_weight)

    by_head = pl.BlockSpec((rows, HEAD_DIM), lambda h: (0, h))
    pair_by_head = pl.BlockSpec((2, rows, HEAD_DIM), lambda h: (0, 0, h))
    stat_spec = pl.BlockSpec((1, 8, rows), lambda h: (h, 0, 0))
    sources = [smem(), by_head, by_head, by_head, pair_by_head, pair_by_head] + [by_head] * len(extra)
    blocks = [pltpu.VMEM((3 * rows, HEAD_DIM), BF16)] * 2
    gathered = (anchor, query_rows, key_rows, value_rows, prev_pair, far_pair, *extra)
    attended, attended_t, stats = pl.pallas_call(
        functools.partial(forward_kernel, bool(extra)),
        grid=(heads,),
        out_shape=(
            jax.ShapeDtypeStruct((rows, cols), BF16),
            jax.ShapeDtypeStruct((cols, rows), BF16),
            jax.ShapeDtypeStruct((heads, 8, rows), F32),
        ),
        in_specs=[*sources, by_head],
        out_specs=(by_head, pl.BlockSpec((HEAD_DIM, rows), lambda h: (h, 0)), stat_spec),
        scratch_shapes=blocks,
        compiler_params=params(),
        name="forward",
    )(*gathered, attended_grad)

    keep, away = pl.pallas_call(
        projection_kernel,
        out_shape=(
            jax.ShapeDtypeStruct((2, cols, cols), F32),
            jax.ShapeDtypeStruct((2, cols, cols), BF16),
        ),
        in_specs=[vmem()] * 4,
        out_specs=(vmem(), vmem()),
        scratch_shapes=[pltpu.VMEM((4, rows, cols), BF16)],
        compiler_params=params(),
        name="projection",
    )(attended_t, output_grad, across, beside)

    query_grad, own_grad, prev_grad, far_grad = pl.pallas_call(
        functools.partial(backward_kernel, bool(extra)),
        grid=(heads,),
        out_shape=(
            jax.ShapeDtypeStruct((rows, cols), BF16),
            jax.ShapeDtypeStruct((2, rows, cols), F32),
            jax.ShapeDtypeStruct((2, rows, cols), BF16),
            jax.ShapeDtypeStruct((2, rows, cols), BF16),
        ),
        in_specs=[*sources, by_head, stat_spec],
        out_specs=(by_head, pair_by_head, pair_by_head, pair_by_head),
        scratch_shapes=blocks + [pltpu.VMEM((3 * rows, HEAD_DIM), F32)] * 2,
        compiler_params=params(),
        name="backward",
    )(*gathered, attended_grad, stats)

    if frames == 8:
        half = keep + swap(away, "tm", 1).astype(F32)
        quarter = (half[0] + swap(half[1].astype(BF16), "tm", 2).astype(F32)).astype(BF16)
        first = (quarter.astype(F32) + swap(quarter, "tm", 4).astype(F32)).astype(BF16)
        second = swap(first, "tm", 2)
        others = swap(jnp.stack([first, second]), "tm", 1)
    else:
        first, second, others = keep[0], keep[1], away.astype(F32)
    weight_grad = pl.pallas_call(
        assemble_kernel,
        out_shape=jax.ShapeDtypeStruct((cols, 4 * cols), F32),
        in_specs=[vmem()] * 3,
        out_specs=vmem(),
        compiler_params=params(),
        name="assemble",
    )(first, second, others)
    if frames != 8:
        weight_grad = lax.psum(weight_grad, "tm")

    if pair_plan:
        crossing = send(
            jnp.where(position == lower, far_grad[1], far_grad[0]), [(lower, upper), (upper, lower)]
        )
        far_keys = (far_grad[0].astype(F32) + crossing.astype(F32)).astype(BF16)
        far_values = (far_grad[1].astype(F32) + crossing.astype(F32)).astype(BF16)
        from_far = jnp.stack(
            [send(far_keys, [(lower, source)]), send(far_values, [(upper, source)])]
        ).astype(F32)
        from_near = send(prev_grad, back(near_pairs)).astype(F32)
        totals = own_grad + from_near + from_far
    else:
        held = far_grad.astype(F32)
        while step > 2:
            step //= 2
            pairs = [(f, f - step) for f in range(step, frames) if f - bounds[f][0] >= step]
            leaving = jnp.where(distance >= step, held, 0.0)
            held = (held - leaving) + send(leaving.astype(BF16), pairs).astype(F32)
        to_prev = prev_grad.astype(F32) + jnp.where(distance == 1, held, 0.0)
        from_near = send(to_prev.astype(BF16), back(near_pairs)).astype(F32)
        totals = own_grad + from_near + jnp.where(distance == 0, held, 0.0)
    key_grad, value_grad = totals[0].astype(BF16), totals[1].astype(BF16)

    out_keep, out_send = pl.pallas_call(
        output_kernel,
        out_shape=(
            jax.ShapeDtypeStruct((2, rows, cols), F32),
            jax.ShapeDtypeStruct((2, rows, cols), BF16),
        ),
        in_specs=[vmem()] * 2,
        out_specs=(vmem(), vmem()),
        compiler_params=params(),
        name="output",
    )(attended, output_weight)
    pair_sum = out_keep + swap(out_send, "head", 1).astype(F32)
    layer_output = (pair_sum[0] + swap(pair_sum[1].astype(BF16), "head", 2).astype(F32)).astype(BF16)
    return layer_output, query_grad, key_grad, value_grad, weight_grad


def solution(mesh):
    in_specs = (
        P("tm", "head"),
        P("tm", "head"),
        P("tm", "head"),
        P("head", None),
        P("tm", "head"),
        P(),
    )
    out_specs = (
        P("tm", "head"),
        P("tm", "head"),
        P("tm", "head"),
        P("tm", "head"),
        P("head", None),
    )
    return jax.shard_map(local, mesh=mesh, in_specs=in_specs, out_specs=out_specs, check_vma=False)
```

time: 325 us -> 128 us (0.39)
  waiting for transfers between devices: 165 us -> 57 us
  matrix products: 63 us -> 0 us
  Pallas kernels: 0 us -> 22.1 us
  other arithmetic: 21.3 us -> 4.34 us
  between operations: 15.3 us -> 0.98 us
  starting transfers between devices: 48.1 us -> 35.7 us
  local copies, waits for them, and re-layouts: 11.4 us -> 7.57 us
    ppermute x14 -> x17, waiting for transfers between devices: 165 us -> 57 us  [the longest x9 37.4 us: swap(): lax.ppermute(array, axis, [(i, i ^ bit) for i in range(lax.axis_size(axis...]
    dot_general x8 -> x0, matrix products: 54.6 us -> none  [the longest x1 16.6 us: local(): jnp.einsum('hqk,qhd->khd', score_grad, query_heads, preferred_element_typ...]
    pallas_call x0 -> x6, Pallas kernels: none -> 22.1 us  [the longest x1 8.37 us: local(): pl.pallas_call(functools.partial(backward_kernel, bool(extra)), grid=(hea...]
    select_n x12 -> x1, other arithmetic: 12.6 us -> 0.05 us  [local(): jnp.where(position == lower, far_grad[1], far_grad[0])]
    ppermute x14 -> x17, starting transfers between devices: 48 us -> 35.7 us  [the longest x9 22.6 us: swap(): lax.ppermute(array, axis, [(i, i ^ bit) for i in range(lax.axis_size(axis...]
    sub x1 -> x0, matrix products: 8.44 us -> none  [local(): raw_weights = jnp.exp(scores - highest)]
    unnamed x21 -> x38, local copies, waits for them, and re-layouts: 11.4 us -> 6.49 us
    convert_element_type x3 -> x4, other arithmetic: 5.11 us -> 1.17 us  [the longest x1 0.82 us: local(): (pair_sum[0] + swap(pair_sum[1].astype(BF16), 'head', 2).astype(F32)).ast...]
  transfers between devices with their start and end apart: 17 -> 17, of which waited for: 14 -> 9; matrix products, arithmetic and copies ran while one was open for 28% -> 2% of each run, Pallas kernels for 0% -> 8%
where the time goes in v1:
time: 128 us
  waiting for transfers between devices  57 us (45%)
  starting transfers between devices  35.7 us (28%)
  Pallas kernels  22.1 us (17%)
  local copies, waits for them, and re-layouts  7.57 us (6%)
  other arithmetic  4.34 us (3%)
    ppermute x9, waiting for transfers between devices, swap(): lax.ppermute(array, axis, [(i, i ^ bit) for i in range(lax.axis_size(axis...  37.4 us
    ppermute x9, starting transfers between devices, swap(): lax.ppermute(array, axis, [(i, i ^ bit) for i in range(lax.axis_size(axis...  22.6 us
    ppermute x8, waiting for transfers between devices, send(): return lax.ppermute(array, 'tm', pairs)  19.7 us
    ppermute x8, starting transfers between devices, send(): return lax.ppermute(array, 'tm', pairs)  13.1 us
    pallas_call x1, Pallas kernels, local(): pl.pallas_call(functools.partial(backward_kernel, bool(extra)), grid=(hea...  8.37 us
    pallas_call x1, Pallas kernels, local(): pl.pallas_call(functools.partial(forward_kernel, bool(extra)), grid=(head...  7.96 us
    unnamed x38, local copies, waits for them, and re-layouts  6.49 us
  transfers between devices with their start and end apart: 17, of which 9 were waited for; matrix products, arithmetic and copies ran while one was open for 2% of the time, Pallas kernels for 8%

profile of v1, /device:TPU:12, one launch (start us, length us, event | category | flops | bytes accessed | tf_op | source)
XLA Modules:
  0.0 127.8 jit_solution(4220958075697411995)
XLA Ops:
  0.7 1.3 pad_maximum_fusion
  1.9 3.6 %collective-permute-start = (bf16[2,512,384]{2,1,0:T(8,128)(2,1)S(1)}, bf16[2,512,384]{2,1,0:T(8,128)(2,1)S(1)}, u32[]{:S(2)}, u32[]{:S(2)}) collective-permute-start(bf16[2,512,384]{2,1,0:T(8,128)(2,1)S(1)} %pad_maximum_fusion), channel_id=1, source_target_pairs={{0,4},{8,12},{12,16},{16,20},{24,28},{1,5},{9,13},{13,17},{17,21},... | collective-permute-start | bytes 2359304 | tf_op jit(solution)/shard_map/ppermute | solution.py:185
  5.5 1.6 %collective-permute-start.4 = (bf16[512,384]{1,0:T(8,128)(2,1)S(1)}, bf16[512,384]{1,0:T(8,128)(2,1)S(1)}, u32[]{:S(2)}, u32[]{:S(2)}) collective-permute-start(bf16[512,384]{1,0:T(8,128)(2,1)S(1)} %copy-done.3), channel_id=1, source_target_pairs={{0,2},{1,3},{2,0},{3,1},{4,6},{5,7},{6,4},{7,5},{8,10},{9,11},{10,... | collective-permute-start | bytes 1179656 | tf_op jit(solution)/shard_map/ppermute | solution.py:170
  7.1 9.1 %collective-permute-done.4.across = bf16[512,384]{1,0:T(8,128)(2,1)S(1)} collective-permute-done((bf16[512,384]{1,0:T(8,128)(2,1)S(1)}, bf16[512,384]{1,0:T(8,128)(2,1)S(1)}, u32[]{:S(2)}, u32[]{:S(2)}) %collective-permute-start.4) | collective-permute-done | bytes 393248 | tf_op jit(solution)/shard_map/ppermute | solution.py:170
  16.2 0.1 pad_maximum_fusion.1
  16.3 0.1 collective-permute-start.5
  16.3 0.7 collective-permute-start.1
  17.1 0.7 collective-permute-start.2
  17.8 5.5 %collective-permute-done.prev = bf16[2,512,384]{2,1,0:T(8,128)(2,1)S(1)} collective-permute-done((bf16[2,512,384]{2,1,0:T(8,128)(2,1)S(1)}, bf16[2,512,384]{2,1,0:T(8,128)(2,1)S(1)}, u32[]{:S(2)}, u32[]{:S(2)}) %collective-permute-start) | collective-permute-done | bytes 786464 | tf_op jit(solution)/shard_map/ppermute | solution.py:185
  23.3 3.6 %collective-permute-start.3 = (bf16[512,384]{1,0:T(8,128)(2,1)S(1)}, bf16[512,384]{1,0:T(8,128)(2,1)S(1)}, u32[]{:S(2)}, u32[]{:S(2)}) collective-permute-start(bf16[512,384]{1,0:T(8,128)(2,1)S(1)} %slice_bitcast_fusion.4), channel_id=1, source_target_pairs={{12,20},{13,21},{14,22},{15,23}} | collective-permute-start | bytes 1179656 | tf_op jit(solution)/shard_map/ppermute | solution.py:185
  27.0 1.1 cotangent.1.rest_2_
  28.2 6.2 %collective-permute-done.3.rest_1_ = bf16[512,384]{1,0:T(8,128)(2,1)S(1)} collective-permute-done((bf16[512,384]{1,0:T(8,128)(2,1)S(1)}, bf16[512,384]{1,0:T(8,128)(2,1)S(1)}, u32[]{:S(2)}, u32[]{:S(2)}) %collective-permute-start.3) | collective-permute-done | bytes 393248 | tf_op jit(solution)/shard_map/ppermute | solution.py:185
  34.4 8.0 %forward.1 = (bf16[512,384]{1,0:T(8,128)(2,1)S(1)}, bf16[384,512]{1,0:T(8,128)(2,1)S(1)}, f32[3,8,512]{2,1,0:T(8,128)S(1)}) custom-call(s32[8]{0:T(128)S(1)} %copy-done.17, bf16[512,384]{1,0:T(8,128)(2,1)S(1)} %copy-done.6, bf16[512,384]{1,0:T(8,128)(2,1)S(1)} %copy-done.1, bf16[512,384]{1,0:T(8,128)(2,1)S(1)} %copy-done.2, ...), custom_call_target="tpu_custom_call" | custom-call | tf_op jit(solution)/shard_map/forward/pallas_call | solution.py:225
  42.5 0.7 copy-done.13
  43.2 0.6 copy-done.15
  43.8 2.0 %projection.1 = (f32[2,384,384]{2,1,0:T(8,128)S(1)}, bf16[2,384,384]{2,1,0:T(8,128)(2,1)}) custom-call(bf16[384,512]{1,0:T(8,128)(2,1)S(1)} %get-tuple-element.24.attended_t, bf16[512,384]{1,0:T(8,128)(2,1)S(1)} %copy-done.3, bf16[512,384]{1,0:T(8,128)(2,1)S(1)} %collective-permute-done.4.across, bf16[2,512,384]{2,1,0:T(8,128)(2,1)S(1)} %collective-permute-done.5.beside), custom_call_target="tpu_custom_call" | custom-call | tf_op jit(solution)/shard_map/projection/pallas_call | solution.py:240
  45.8 1.0 copy-done.11
  46.8 11.8 %collective-permute-start.12 = (bf16[2,384,384]{2,1,0:T(8,128)(2,1)}, bf16[2,384,384]{2,1,0:T(8,128)(2,1)}, u32[]{:S(2)}, u32[]{:S(2)}) collective-permute-start(bf16[2,384,384]{2,1,0:T(8,128)(2,1)} %get-tuple-element.26), channel_id=1, source_target_pairs={{0,4},{4,0},{8,12},{12,8},{16,20},{20,16},{24,28},{28,24},{1,5},{5... | collective-permute-start | bytes 1769480 | tf_op jit(solution)/shard_map/ppermute | solution.py:170
  58.6 1.1 copy-done.5
  59.7 1.0 copy-done.8
  60.7 1.0 copy-done.10
  61.7 0.8 copy-done.16
  62.5 8.4 %backward.1 = (bf16[512,384]{1,0:T(8,128)(2,1)}, f32[2,512,384]{2,1,0:T(8,128)}, bf16[2,512,384]{2,1,0:T(8,128)(2,1)S(1)}, bf16[2,512,384]{2,1,0:T(8,128)(2,1)S(1)}) custom-call(s32[8]{0:T(128)S(1)} %copy-done.17, bf16[512,384]{1,0:T(8,128)(2,1)S(1)} %copy-done.6, bf16[512,384]{1,0:T(8,128)(2,1)S(1)} %copy-done.1, bf16[512,384]{1,0:T(8,128)(2,1)S(1)} %copy-done.2, ...), custom_call_target="tpu_custom_call" | custom-call | tf_op jit(solution)/shard_map/backward/pallas_call | solution.py:253
  70.9 1.2 collective-permute-done.12
  72.1 1.2 convert_add_fusion.1
  73.5 0.7 collective-permute-start.9
  74.2 0.1 copy-done.14
  74.3 1.1 output.1
  75.5 6.0 %collective-permute-done.13 = bf16[384,384]{1,0:T(8,128)(2,1)S(1)} collective-permute-done((bf16[384,384]{1,0:T(8,128)(2,1)S(1)}, bf16[384,384]{1,0:T(8,128)(2,1)S(1)}, u32[]{:S(2)}, u32[]{:S(2)}) %collective-permute-start.13) | collective-permute-done | bytes 294944 | tf_op jit(solution)/shard_map/ppermute | solution.py:170
  81.5 0.1 fusion.5
  81.6 3.1 %collective-permute-start.14 = (bf16[384,384]{1,0:T(8,128)(2,1)S(1)}, bf16[384,384]{1,0:T(8,128)(2,1)S(1)}, u32[]{:S(2)}, u32[]{:S(2)}) collective-permute-start(bf16[384,384]{1,0:T(8,128)(2,1)S(1)} %fusion.5), channel_id=1, source_target_pairs={{0,16},{4,20},{8,24},{12,28},{16,0},{20,4},{24,8},{28,12},{1,17},{... | collective-permute-start | bytes 884744 | tf_op jit(solution)/shard_map/ppermute | solution.py:170
  84.7 2.5 %collective-permute-start.8 = (bf16[2,512,384]{2,1,0:T(8,128)(2,1)S(1)}, bf16[2,512,384]{2,1,0:T(8,128)(2,1)S(1)}, u32[]{:S(2)}, u32[]{:S(2)}) collective-permute-start(bf16[2,512,384]{2,1,0:T(8,128)(2,1)S(1)} %get-tuple-element.22), channel_id=1, source_target_pairs={{4,0},{12,8},{16,12},{20,16},{28,24},{5,1},{13,9},{17,13},{21,17},... | collective-permute-start | bytes 2359304 | tf_op jit(solution)/shard_map/ppermute | solution.py:185
  87.2 0.2 fusion
  87.4 0.7 collective-permute-start.10
  88.1 0.7 collective-permute-start.11
  88.8 6.8 %collective-permute-done.14 = bf16[384,384]{1,0:T(8,128)(2,1)S(1)} collective-permute-done((bf16[384,384]{1,0:T(8,128)(2,1)S(1)}, bf16[384,384]{1,0:T(8,128)(2,1)S(1)}, u32[]{:S(2)}, u32[]{:S(2)}) %collective-permute-start.14) | collective-permute-done | bytes 294944 | tf_op jit(solution)/shard_map/ppermute | solution.py:170
  95.6 0.1 add_convert_fusion.1.first
  95.7 3.0 %collective-permute-start.15 = (bf16[384,384]{1,0:T(8,128)(2,1)S(1)}, bf16[384,384]{1,0:T(8,128)(2,1)S(1)}, u32[]{:S(2)}, u32[]{:S(2)}) collective-permute-start(bf16[384,384]{1,0:T(8,128)(2,1)S(1)} %add_convert_fusion.1.first), channel_id=1, source_target_pairs={{0,8},{4,12},{8,0},{12,4},{16,24},{20,28},{24,16},{28,20},{1,9},{5... | collective-permute-start | bytes 884744 | tf_op jit(solution)/shard_map/ppermute | solution.py:170
  98.7 0.2 convert_add_fusion
  99.0 1.6 %collective-permute-start.7 = (bf16[512,384]{1,0:T(8,128)(2,1)S(1)}, bf16[512,384]{1,0:T(8,128)(2,1)S(1)}, u32[]{:S(2)}, u32[]{:S(2)}) collective-permute-start(bf16[512,384]{1,0:T(8,128)(2,1)S(1)} %fusion.6), channel_id=1, source_target_pairs={{0,2},{1,3},{2,0},{3,1},{4,6},{5,7},{6,4},{7,5},{8,10},{9,11},{10,... | collective-permute-start | bytes 1179656 | tf_op jit(solution)/shard_map/ppermute | solution.py:170
  100.5 4.0 %collective-permute-done.15.second = bf16[384,384]{1,0:T(8,128)(2,1)S(1)} collective-permute-done((bf16[384,384]{1,0:T(8,128)(2,1)S(1)}, bf16[384,384]{1,0:T(8,128)(2,1)S(1)}, u32[]{:S(2)}, u32[]{:S(2)}) %collective-permute-start.15) | collective-permute-done | bytes 294944 | tf_op jit(solution)/shard_map/ppermute | solution.py:170
  104.6 1.4 %collective-permute-start.16 = (bf16[2,384,384]{2,1,0:T(8,128)(2,1)S(1)}, bf16[2,384,384]{2,1,0:T(8,128)(2,1)S(1)}, u32[]{:S(2)}, u32[]{:S(2)}) collective-permute-start(bf16[2,384,384]{2,1,0:T(8,128)(2,1)S(1)} %pad_maximum_fusion.2), channel_id=1, source_target_pairs={{0,4},{4,0},{8,12},{12,8},{16,20},{20,16},{24,28},{28,24},{1,5},{5... | collective-permute-start | bytes 1769480 | tf_op jit(solution)/shard_map/ppermute | solution.py:170
  106.0 7.9 %collective-permute-done.8 = bf16[2,512,384]{2,1,0:T(8,128)(2,1)S(1)} collective-permute-done((bf16[2,512,384]{2,1,0:T(8,128)(2,1)S(1)}, bf16[2,512,384]{2,1,0:T(8,128)(2,1)S(1)}, u32[]{:S(2)}, u32[]{:S(2)}) %collective-permute-start.8) | collective-permute-done | bytes 786464 | tf_op jit(solution)/shard_map/ppermute | solution.py:185
  113.9 0.3 add_convert_fusion
  114.2 1.0 slice_bitcast_fusion.2
  115.2 0.8 fusion.3
  116.0 10.2 %collective-permute-done.16.others = bf16[2,384,384]{2,1,0:T(8,128)(2,1)S(1)} collective-permute-done((bf16[2,384,384]{2,1,0:T(8,128)(2,1)S(1)}, bf16[2,384,384]{2,1,0:T(8,128)(2,1)S(1)}, u32[]{:S(2)}, u32[]{:S(2)}) %collective-permute-start.16) | collective-permute-done | bytes 589856 | tf_op jit(solution)/shard_map/ppermute | solution.py:170
  126.2 1.6 %assemble.1 = f32[384,1536]{1,0:T(8,128)} custom-call(bf16[384,384]{1,0:T(8,128)(2,1)S(1)} %add_convert_fusion.1.first, bf16[384,384]{1,0:T(8,128)(2,1)S(1)} %collective-permute-done.15.second, bf16[2,384,384]{2,1,0:T(8,128)(2,1)S(1)} %collective-permute-done.16.others), custom_call_target="tpu_custom_call" | custom-call | tf_op jit(solution)/shard_map/assemble/pallas_call | solution.py:277
  (45 shorter events, 0.5 us)
Async XLA Ops:
  0.6 4.9 %copy-start.3 = (bf16[512,384]{1,0:T(8,128)(2,1)S(1)}, bf16[512,384]{1,0:T(8,128)(2,1)}, u32[]{:S(2)}) copy-start(bf16[512,384]{1,0:T(8,128)(2,1)} %own.3) | copy-start | bytes 1179652
  0.6 16.4 %copy-start.1 = (bf16[512,384]{1,0:T(8,128)(2,1)S(1)}, bf16[512,384]{1,0:T(8,128)(2,1)}, u32[]{:S(2)}) copy-start(bf16[512,384]{1,0:T(8,128)(2,1)} %k.3) | copy-start | bytes 1179652
  1.9 25.1 %copy-start = (bf16[384,1536]{1,0:T(8,128)(2,1)S(1)}, bf16[384,1536]{1,0:T(8,128)(2,1)}, u32[]{:S(2)}) copy-start(bf16[384,1536]{1,0:T(8,128)(2,1)} %weight.3) | copy-start | bytes 3538948
  1.9 21.3 %collective-permute-start = (bf16[2,512,384]{2,1,0:T(8,128)(2,1)S(1)}, bf16[2,512,384]{2,1,0:T(8,128)(2,1)S(1)}, u32[]{:S(2)}, u32[]{:S(2)}) collective-permute-start(bf16[2,512,384]{2,1,0:T(8,128)(2,1)S(1)} %pad_maximum_fusion), channel_id=1, source_target_pairs={{0,4},{8,12},{12,16},{16,20},{24,28},{1,5},{9,13},{13,17},{17,21},... | collective-permute-start | bytes 2359304 | tf_op jit(solution)/shard_map/ppermute | solution.py:185
  5.5 10.6 %collective-permute-start.4 = (bf16[512,384]{1,0:T(8,128)(2,1)S(1)}, bf16[512,384]{1,0:T(8,128)(2,1)S(1)}, u32[]{:S(2)}, u32[]{:S(2)}) collective-permute-start(bf16[512,384]{1,0:T(8,128)(2,1)S(1)} %copy-done.3), channel_id=1, source_target_pairs={{0,2},{1,3},{2,0},{3,1},{4,6},{5,7},{6,4},{7,5},{8,10},{9,11},{10,... | collective-permute-start | bytes 1179656 | tf_op jit(solution)/shard_map/ppermute | solution.py:170
  16.3 10.7 %collective-permute-start.5 = (bf16[2,512,384]{2,1,0:T(8,128)(2,1)S(1)}, bf16[2,512,384]{2,1,0:T(8,128)(2,1)S(1)}, u32[]{:S(2)}, u32[]{:S(2)}) collective-permute-start(bf16[2,512,384]{2,1,0:T(8,128)(2,1)S(1)} %pad_maximum_fusion.1), channel_id=1, source_target_pairs={{0,1},{1,0},{2,3},{3,2},{4,5},{5,4},{6,7},{7,6},{8,9},{9,8},{10,11... | collective-permute-start | bytes 2359304 | tf_op jit(solution)/shard_map/ppermute | solution.py:170
  16.3 11.8 %collective-permute-start.1 = (bf16[2,512,384]{2,1,0:T(8,128)(2,1)S(1)}, bf16[2,512,384]{2,1,0:T(8,128)(2,1)S(1)}, u32[]{:S(2)}, u32[]{:S(2)}) collective-permute-start(bf16[2,512,384]{2,1,0:T(8,128)(2,1)S(1)} %pad_maximum_fusion), channel_id=1, source_target_pairs={{8,16},{9,17},{10,18},{11,19}} | collective-permute-start | bytes 2359304 | tf_op jit(solution)/shard_map/ppermute | solution.py:185
  17.1 11.1 %collective-permute-start.2 = (bf16[512,384]{1,0:T(8,128)(2,1)S(1)}, bf16[512,384]{1,0:T(8,128)(2,1)S(1)}, u32[]{:S(2)}, u32[]{:S(2)}) collective-permute-start(bf16[512,384]{1,0:T(8,128)(2,1)S(1)} %copy-done.1), channel_id=1, source_target_pairs={{8,20},{9,21},{10,22},{11,23}} | collective-permute-start | bytes 1179656 | tf_op jit(solution)/shard_map/ppermute | solution.py:185
  23.3 11.1 %copy-start.2 = (bf16[512,384]{1,0:T(8,128)(2,1)S(1)}, bf16[512,384]{1,0:T(8,128)(2,1)}, u32[]{:S(2)}) copy-start(bf16[512,384]{1,0:T(8,128)(2,1)} %v.3) | copy-start | bytes 1179652
  23.3 11.1 %copy-start.6 = (bf16[512,384]{1,0:T(8,128)(2,1)S(1)}, bf16[512,384]{1,0:T(8,128)(2,1)}, u32[]{:S(2)}) copy-start(bf16[512,384]{1,0:T(8,128)(2,1)} %q.3) | copy-start | bytes 1179652
  23.3 11.1 %copy-start.17 = (s32[8]{0:T(128)S(1)}, s32[8]{0:T(128)}, u32[]{:S(2)}) copy-start(s32[8]{0:T(128)} %anchor.3) | copy-start | bytes 100
  23.3 11.1 %collective-permute-start.3 = (bf16[512,384]{1,0:T(8,128)(2,1)S(1)}, bf16[512,384]{1,0:T(8,128)(2,1)S(1)}, u32[]{:S(2)}, u32[]{:S(2)}) collective-permute-start(bf16[512,384]{1,0:T(8,128)(2,1)S(1)} %slice_bitcast_fusion.4), channel_id=1, source_target_pairs={{12,20},{13,21},{14,22},{15,23}} | collective-permute-start | bytes 1179656 | tf_op jit(solution)/shard_map/ppermute | solution.py:185
  28.2 14.3 %copy-start.7 = (bf16[512,384]{1,0:T(8,128)(2,1)}, bf16[512,384]{1,0:T(8,128)(2,1)S(1)}, u32[]{:S(2)}) copy-start(bf16[512,384]{1,0:T(8,128)(2,1)S(1)} %collective-permute-done.2.rest_0_) | copy-start | bytes 1179652
  28.2 14.2 %copy-start.4 = (bf16[2,512,384]{2,1,0:T(8,128)(2,1)}, bf16[2,512,384]{2,1,0:T(8,128)(2,1)S(1)}, u32[]{:S(2)}) copy-start(bf16[2,512,384]{2,1,0:T(8,128)(2,1)S(1)} %collective-permute-done.1.far) | copy-start | bytes 2359300
  34.4 8.0 %copy-start.9 = (bf16[512,384]{1,0:T(8,128)(2,1)}, bf16[512,384]{1,0:T(8,128)(2,1)S(1)}, u32[]{:S(2)}) copy-start(bf16[512,384]{1,0:T(8,128)(2,1)S(1)} %collective-permute-done.3.rest_1_) | copy-start | bytes 1179652
  42.4 0.7 copy-start.13
  43.2 0.6 copy-start.15
  45.8 1.0 copy-start.11
  46.8 25.3 %collective-permute-start.12 = (bf16[2,384,384]{2,1,0:T(8,128)(2,1)}, bf16[2,384,384]{2,1,0:T(8,128)(2,1)}, u32[]{:S(2)}, u32[]{:S(2)}) collective-permute-start(bf16[2,384,384]{2,1,0:T(8,128)(2,1)} %get-tuple-element.26), channel_id=1, source_target_pairs={{0,4},{4,0},{8,12},{12,8},{16,20},{20,16},{24,28},{28,24},{1,5},{5... | collective-permute-start | bytes 1769480 | tf_op jit(solution)/shard_map/ppermute | solution.py:170
  58.6 1.1 copy-start.5
  59.7 1.0 copy-start.8
  60.7 1.0 copy-start.10
  61.7 0.8 copy-start.16
  62.5 9.6 %copy-start.12 = (f32[2,384,384]{2,1,0:T(8,128)S(1)}, f32[2,384,384]{2,1,0:T(8,128)}, u32[]{:S(2)}) copy-start(f32[2,384,384]{2,1,0:T(8,128)} %copy-done.11) | copy-start | bytes 3538948
  73.3 1.0 copy-start.14
  73.4 8.1 %collective-permute-start.13 = (bf16[384,384]{1,0:T(8,128)(2,1)S(1)}, bf16[384,384]{1,0:T(8,128)(2,1)S(1)}, u32[]{:S(2)}, u32[]{:S(2)}) collective-permute-start(bf16[384,384]{1,0:T(8,128)(2,1)S(1)} %fusion.7), channel_id=1, source_target_pairs={{0,8},{4,12},{8,0},{12,4},{16,24},{20,28},{24,16},{28,20},{1,9},{5... | collective-permute-start | bytes 884744 | tf_op jit(solution)/shard_map/ppermute | solution.py:170
  73.5 13.7 %collective-permute-start.9 = (bf16[512,384]{1,0:T(8,128)(2,1)S(1)}, bf16[512,384]{1,0:T(8,128)(2,1)S(1)}, u32[]{:S(2)}, u32[]{:S(2)}) collective-permute-start(bf16[512,384]{1,0:T(8,128)(2,1)S(1)} %select_bitcast_fusion), channel_id=1, source_target_pairs={{16,20},{20,16},{17,21},{21,17},{18,22},{22,18},{19,23},{23,19}} | collective-permute-start | bytes 1179656 | tf_op jit(solution)/shard_map/ppermute | solution.py:185
  75.5 23.2 %collective-permute-start.6 = (bf16[2,512,384]{2,1,0:T(8,128)(2,1)S(1)}, bf16[2,512,384]{2,1,0:T(8,128)(2,1)S(1)}, u32[]{:S(2)}, u32[]{:S(2)}) collective-permute-start(bf16[2,512,384]{2,1,0:T(8,128)(2,1)S(1)} %get-tuple-element.18), channel_id=1, source_target_pairs={{0,1},{1,0},{2,3},{3,2},{4,5},{5,4},{6,7},{7,6},{8,9},{9,8},{10,11... | collective-permute-start | bytes 2359304 | tf_op jit(solution)/shard_map/ppermute | solution.py:170
  81.6 14.1 %collective-permute-start.14 = (bf16[384,384]{1,0:T(8,128)(2,1)S(1)}, bf16[384,384]{1,0:T(8,128)(2,1)S(1)}, u32[]{:S(2)}, u32[]{:S(2)}) collective-permute-start(bf16[384,384]{1,0:T(8,128)(2,1)S(1)} %fusion.5), channel_id=1, source_target_pairs={{0,16},{4,20},{8,24},{12,28},{16,0},{20,4},{24,8},{28,12},{1,17},{... | collective-permute-start | bytes 884744 | tf_op jit(solution)/shard_map/ppermute | solution.py:170
  84.7 29.2 %collective-permute-start.8 = (bf16[2,512,384]{2,1,0:T(8,128)(2,1)S(1)}, bf16[2,512,384]{2,1,0:T(8,128)(2,1)S(1)}, u32[]{:S(2)}, u32[]{:S(2)}) collective-permute-start(bf16[2,512,384]{2,1,0:T(8,128)(2,1)S(1)} %get-tuple-element.22), channel_id=1, source_target_pairs={{4,0},{12,8},{16,12},{20,16},{28,24},{5,1},{13,9},{17,13},{21,17},... | collective-permute-start | bytes 2359304 | tf_op jit(solution)/shard_map/ppermute | solution.py:185
  87.4 18.6 %collective-permute-start.10 = (bf16[512,384]{1,0:T(8,128)(2,1)S(1)}, bf16[512,384]{1,0:T(8,128)(2,1)S(1)}, u32[]{:S(2)}, u32[]{:S(2)}) collective-permute-start(bf16[512,384]{1,0:T(8,128)(2,1)S(1)} %get-tuple-element.27), channel_id=1, source_target_pairs={{16,8},{17,9},{18,10},{19,11}} | collective-permute-start | bytes 1179656 | tf_op jit(solution)/shard_map/ppermute | solution.py:185
  88.1 17.9 %collective-permute-start.11 = (bf16[512,384]{1,0:T(8,128)(2,1)S(1)}, bf16[512,384]{1,0:T(8,128)(2,1)S(1)}, u32[]{:S(2)}, u32[]{:S(2)}) collective-permute-start(bf16[512,384]{1,0:T(8,128)(2,1)S(1)} %get-tuple-element.28), channel_id=1, source_target_pairs={{20,8},{21,9},{22,10},{23,11}} | collective-permute-start | bytes 1179656 | tf_op jit(solution)/shard_map/ppermute | solution.py:185
  95.7 8.8 %collective-permute-start.15 = (bf16[384,384]{1,0:T(8,128)(2,1)S(1)}, bf16[384,384]{1,0:T(8,128)(2,1)S(1)}, u32[]{:S(2)}, u32[]{:S(2)}) collective-permute-start(bf16[384,384]{1,0:T(8,128)(2,1)S(1)} %add_convert_fusion.1.first), channel_id=1, source_target_pairs={{0,8},{4,12},{8,0},{12,4},{16,24},{20,28},{24,16},{28,20},{1,9},{5... | collective-permute-start | bytes 884744 | tf_op jit(solution)/shard_map/ppermute | solution.py:170
  98.9 15.1 %copy-start.18 = (f32[2,512,384]{2,1,0:T(8,128)S(1)}, f32[2,512,384]{2,1,0:T(8,128)}, u32[]{:S(2)}) copy-start(f32[2,512,384]{2,1,0:T(8,128)} %get-tuple-element.21) | copy-start | bytes 4718596
  99.0 16.2 %collective-permute-start.7 = (bf16[512,384]{1,0:T(8,128)(2,1)S(1)}, bf16[512,384]{1,0:T(8,128)(2,1)S(1)}, u32[]{:S(2)}, u32[]{:S(2)}) collective-permute-start(bf16[512,384]{1,0:T(8,128)(2,1)S(1)} %fusion.6), channel_id=1, source_target_pairs={{0,2},{1,3},{2,0},{3,1},{4,6},{5,7},{6,4},{7,5},{8,10},{9,11},{10,... | collective-permute-start | bytes 1179656 | tf_op jit(solution)/shard_map/ppermute | solution.py:170
  104.6 21.6 %collective-permute-start.16 = (bf16[2,384,384]{2,1,0:T(8,128)(2,1)S(1)}, bf16[2,384,384]{2,1,0:T(8,128)(2,1)S(1)}, u32[]{:S(2)}, u32[]{:S(2)}) collective-permute-start(bf16[2,384,384]{2,1,0:T(8,128)(2,1)S(1)} %pad_maximum_fusion.2), channel_id=1, source_target_pairs={{0,4},{4,0},{8,12},{12,8},{16,20},{20,16},{24,28},{28,24},{1,5},{5... | collective-permute-start | bytes 1769480 | tf_op jit(solution)/shard_map/ppermute | solution.py:170

commit v2 on v1

--- a/solution.py
+++ b/solution.py
@@ -41,18 +41,17 @@
     return pl.BlockSpec(memory_space=pltpu.SMEM)
 
 
-def params():
-    return pltpu.CompilerParams(vmem_limit_bytes=48 * 1024 * 1024)
-
-
-def cotangent_kernel(own, across, beside, weight, out):
+def params(mebibytes):
+    return pltpu.CompilerParams(vmem_limit_bytes=mebibytes * 1024 * 1024)
+
+
+def cotangent_kernel(own, second, third, fourth, weight, out):
     head = lax.axis_index("head")
     width = own.shape[1]
-    pieces = (own[...], beside[0], across[...], beside[1])
     total = None
-    for m, piece in enumerate(pieces):
+    for m, piece in enumerate((own, second, third, fourth)):
         start = pl.multiple_of((head ^ m) * width, 128)
-        term = dot(piece, weight[:, pl.ds(start, width)], ((1,), (1,)))
+        term = dot(piece[...], weight[:, pl.ds(start, width)], ((1,), (1,)))
         total = term if total is None else total + term
     out[...] = total.astype(BF16)
 
@@ -128,13 +127,11 @@
         own_grad[kind] = parts[2] + jnp.where(a < f, 0.0, near)
 
 
-def projection_kernel(attended_t, own, across, beside, keep, send, pieces):
+def projection_kernel(attended_t, own, second, third, fourth, keep, send, pieces):
     tm = lax.axis_index("tm")
     sel = (tm % 2) * 2 + (tm // 2) % 2
-    pieces[0] = own[...]
-    pieces[1] = beside[0]
-    pieces[2] = across[...]
-    pieces[3] = beside[1]
+    for m, piece in enumerate((own, second, third, fourth)):
+        pieces[m] = piece[...]
     for slot in range(4):
         term = dot(attended_t[...], pieces[slot ^ sel], ((1,), (0,)))
         if slot < 2:
@@ -205,16 +202,15 @@
             step *= 2
         extra = ()
 
-    across = swap(output_grad, "head", 2)
-    beside = swap(jnp.stack([output_grad, across]), "head", 1)
+    others = tuple(swap(output_grad, "head", m) for m in (1, 2, 3))
     attended_grad = pl.pallas_call(
         cotangent_kernel,
         out_shape=jax.ShapeDtypeStruct((rows, cols), BF16),
-        in_specs=[vmem()] * 4,
+        in_specs=[vmem()] * 5,
         out_specs=vmem(),
-        compiler_params=params(),
+        compiler_params=params(8),
         name="cotangent",
-    )(output_grad, across, beside, output_weight)
+    )(output_grad, *others, output_weight)
 
     by_head = pl.BlockSpec((rows, HEAD_DIM), lambda h: (0, h))
     pair_by_head = pl.BlockSpec((2, rows, HEAD_DIM), lambda h: (0, 0, h))
@@ -233,7 +229,7 @@
         in_specs=[*sources, by_head],
         out_specs=(by_head, pl.BlockSpec((HEAD_DIM, rows), lambda h: (h, 0)), stat_spec),
         scratch_shapes=blocks,
-        compiler_params=params(),
+        compiler_params=params(24),
         name="forward",
     )(*gathered, attended_grad)
 
@@ -243,12 +239,12 @@
             jax.ShapeDtypeStruct((2, cols, cols), F32),
             jax.ShapeDtypeStruct((2, cols, cols), BF16),
         ),
-        in_specs=[vmem()] * 4,
+        in_specs=[vmem()] * 5,
         out_specs=(vmem(), vmem()),
         scratch_shapes=[pltpu.VMEM((4, rows, cols), BF16)],
-        compiler_params=params(),
+        compiler_params=params(8),
         name="projection",
-    )(attended_t, output_grad, across, beside)
+    )(attended_t, output_grad, *others)
 
     query_grad, own_grad, prev_grad, far_grad = pl.pallas_call(
         functools.partial(backward_kernel, bool(extra)),
@@ -262,7 +258,7 @@
         in_specs=[*sources, by_head, stat_spec],
         out_specs=(by_head, pair_by_head, pair_by_head, pair_by_head),
         scratch_shapes=blocks + [pltpu.VMEM((3 * rows, HEAD_DIM), F32)] * 2,
-        compiler_params=params(),
+        compiler_params=params(24),
         name="backward",
     )(*gathered, attended_grad, stats)
 
@@ -271,17 +267,17 @@
         quarter = (half[0] + swap(half[1].astype(BF16), "tm", 2).astype(F32)).astype(BF16)
         first = (quarter.astype(F32) + swap(quarter, "tm", 4).astype(F32)).astype(BF16)
         second = swap(first, "tm", 2)
-        others = swap(jnp.stack([first, second]), "tm", 1)
+        last = swap(jnp.stack([first, second]), "tm", 1)
     else:
-        first, second, others = keep[0], keep[1], away.astype(F32)
+        first, second, last = keep[0], keep[1], away.astype(F32)
     weight_grad = pl.pallas_call(
         assemble_kernel,
         out_shape=jax.ShapeDtypeStruct((cols, 4 * cols), F32),
         in_specs=[vmem()] * 3,
         out_specs=vmem(),
-        compiler_params=params(),
+        compiler_params=params(8),
         name="assemble",
-    )(first, second, others)
+    )(first, second, last)
     if frames != 8:
         weight_grad = lax.psum(weight_grad, "tm")
 
@@ -316,7 +312,7 @@
         ),
         in_specs=[vmem()] * 2,
         out_specs=(vmem(), vmem()),
-        compiler_params=params(),
+        compiler_params=params(8),
         name="output",
     )(attended, output_weight)
     pair_sum = out_keep + swap(out_send, "head", 1).astype(F32)

time: 128 us -> 119 us (0.930)
  starting transfers between devices: 35.7 us -> 22.8 us
  waiting for transfers between devices: 57 us -> 61.6 us
  local copies, waits for them, and re-layouts: 7.57 us -> 6.18 us
    ppermute x9 -> x10, starting transfers between devices: 22.6 us -> 9.79 us  [swap(): lax.ppermute(array, axis, [(i, i ^ bit) for i in range(lax.axis_size(axis...]
    ppermute x8, waiting for transfers between devices: 19.7 us -> 30 us  [send(): return lax.ppermute(array, 'tm', pairs)]
    ppermute x9 -> x10, waiting for transfers between devices: 37.4 us -> 31.6 us  [swap(): lax.ppermute(array, axis, [(i, i ^ bit) for i in range(lax.axis_size(axis...]
    unnamed x38 -> x36, local copies, waits for them, and re-layouts: 6.49 us -> 5.11 us
  transfers between devices with their start and end apart: 17 -> 18, of which waited for: 9 -> 8; matrix products, arithmetic and copies ran while one was open for 2% -> 2% of each run, Pallas kernels for 8% -> 9%
where the time goes in v2:
time: 119 us; the launch traced here: 118 us
  waiting for transfers between devices  61.6 us (52%)
  starting transfers between devices  22.8 us (19%)
  Pallas kernels  22.2 us (19%)
  local copies, waits for them, and re-layouts  6.18 us (5%)
  other arithmetic  4.29 us (4%)
    ppermute x10, waiting for transfers between devices, swap(): lax.ppermute(array, axis, [(i, i ^ bit) for i in range(lax.axis_size(axis...  31.6 us
    ppermute x8, waiting for transfers between devices, send(): return lax.ppermute(array, 'tm', pairs)  30 us
    ppermute x8, starting transfers between devices, send(): return lax.ppermute(array, 'tm', pairs)  13 us
    ppermute x10, starting transfers between devices, swap(): lax.ppermute(array, axis, [(i, i ^ bit) for i in range(lax.axis_size(axis...  9.79 us
    pallas_call x1, Pallas kernels, local(): pl.pallas_call(functools.partial(backward_kernel, bool(extra)), grid=(hea...  8.37 us
    pallas_call x1, Pallas kernels, local(): pl.pallas_call(functools.partial(forward_kernel, bool(extra)), grid=(head...  7.96 us
    unnamed x36, local copies, waits for them, and re-layouts  5.11 us
  transfers between devices with their start and end apart: 18, of which 8 were waited for; matrix products, arithmetic and copies ran while one was open for 2% of the time, Pallas kernels for 9%

profile of v2, /device:TPU:12, one launch (start us, length us, event | category | flops | bytes accessed | tf_op | source)
XLA Modules:
  0.0 118.1 jit_solution(14130270394046949408)
XLA Ops:
  0.7 1.3 %pad_maximum_fusion = bf16[2,512,384]{2,1,0:T(8,128)(2,1)S(1)} fusion(bf16[1,512,384]{2,1,0:T(8,128)(2,1)} %bitcast.37, bf16[1,512,384]{2,1,0:T(8,128)(2,1)} %bitcast.36), kind=kLoop, calls=%fused_computation.11 | loop fusion | flops 393216 | bytes 1572864 | tf_op jit(solution)/shard_map/stack | solution.py:187
  2.0 3.4 %collective-permute-start = (bf16[2,512,384]{2,1,0:T(8,128)(2,1)S(1)}, bf16[2,512,384]{2,1,0:T(8,128)(2,1)S(1)}, u32[]{:S(2)}, u32[]{:S(2)}) collective-permute-start(bf16[2,512,384]{2,1,0:T(8,128)(2,1)S(1)} %pad_maximum_fusion), channel_id=1, source_target_pairs={{0,4},{8,12},{12,16},{16,20},{24,28},{1,5},{9,13},{13,17},{17,21},... | collective-permute-start | bytes 2359304 | tf_op jit(solution)/shard_map/ppermute | solution.py:182
  5.5 0.7 collective-permute-start.6
  6.2 0.7 collective-permute-start.1
  6.9 0.7 collective-permute-start.2
  7.6 0.9 collective-permute-start.5
  8.5 14.7 %collective-permute-done.prev = bf16[2,512,384]{2,1,0:T(8,128)(2,1)S(1)} collective-permute-done((bf16[2,512,384]{2,1,0:T(8,128)(2,1)S(1)}, bf16[2,512,384]{2,1,0:T(8,128)(2,1)S(1)}, u32[]{:S(2)}, u32[]{:S(2)}) %collective-permute-start) | collective-permute-done | bytes 786464 | tf_op jit(solution)/shard_map/ppermute | solution.py:182
  23.3 3.6 %collective-permute-start.3 = (bf16[512,384]{1,0:T(8,128)(2,1)S(1)}, bf16[512,384]{1,0:T(8,128)(2,1)S(1)}, u32[]{:S(2)}, u32[]{:S(2)}) collective-permute-start(bf16[512,384]{1,0:T(8,128)(2,1)S(1)} %slice_bitcast_fusion.4), channel_id=1, source_target_pairs={{12,20},{13,21},{14,22},{15,23}} | collective-permute-start | bytes 1179656 | tf_op jit(solution)/shard_map/ppermute | solution.py:182
  27.0 1.1 cotangent.1.rest_2_
  28.1 7.8 %collective-permute-done.3.rest_1_ = bf16[512,384]{1,0:T(8,128)(2,1)S(1)} collective-permute-done((bf16[512,384]{1,0:T(8,128)(2,1)S(1)}, bf16[512,384]{1,0:T(8,128)(2,1)S(1)}, u32[]{:S(2)}, u32[]{:S(2)}) %collective-permute-start.3) | collective-permute-done | bytes 393248 | tf_op jit(solution)/shard_map/ppermute | solution.py:182
  35.9 8.0 %forward.1 = (bf16[512,384]{1,0:T(8,128)(2,1)S(1)}, bf16[384,512]{1,0:T(8,128)(2,1)S(1)}, f32[3,8,512]{2,1,0:T(8,128)S(1)}) custom-call(s32[8]{0:T(128)S(1)} %copy-done.17, bf16[512,384]{1,0:T(8,128)(2,1)S(1)} %copy-done.5, bf16[512,384]{1,0:T(8,128)(2,1)S(1)} %copy-done.1, bf16[512,384]{1,0:T(8,128)(2,1)S(1)} %copy-done.2, ...), custom_call_target="tpu_custom_call" | custom-call | tf_op jit(solution)/shard_map/forward/pallas_call | solution.py:221
  44.0 2.0 %projection.1 = (f32[2,384,384]{2,1,0:T(8,128)S(1)}, bf16[2,384,384]{2,1,0:T(8,128)(2,1)}) custom-call(bf16[384,512]{1,0:T(8,128)(2,1)S(1)} %get-tuple-element.24.attended_t, bf16[512,384]{1,0:T(8,128)(2,1)S(1)} %copy-done.10, bf16[512,384]{1,0:T(8,128)(2,1)S(1)} %collective-permute-done.4.second, bf16[512,384]{1,0:T(8,128)(2,1)S(1)} %collective-permute-done.5.third, ...), custom_call_target="tpu_custom_call" | custom-call | tf_op jit(solution)/shard_map/projection/pallas_call | solution.py:236
  45.9 1.0 copy-done.11
  47.0 0.6 collective-permute-start.13
  47.6 1.1 copy-done.4
  48.7 1.0 copy-done.7
  49.7 1.0 copy-done.9
  50.7 0.8 copy-done.16
  51.5 8.4 %backward.1 = (bf16[512,384]{1,0:T(8,128)(2,1)}, f32[2,512,384]{2,1,0:T(8,128)S(1)}, bf16[2,512,384]{2,1,0:T(8,128)(2,1)S(1)}, bf16[2,512,384]{2,1,0:T(8,128)(2,1)S(1)}) custom-call(s32[8]{0:T(128)S(1)} %copy-done.17, bf16[512,384]{1,0:T(8,128)(2,1)S(1)} %copy-done.5, bf16[512,384]{1,0:T(8,128)(2,1)S(1)} %copy-done.1, bf16[512,384]{1,0:T(8,128)(2,1)S(1)} %copy-done.2, ...), custom_call_target="tpu_custom_call" | custom-call | tf_op jit(solution)/shard_map/backward/pallas_call | solution.py:249
  59.9 2.4 %collective-permute-done.13 = bf16[2,384,384]{2,1,0:T(8,128)(2,1)} collective-permute-done((bf16[2,384,384]{2,1,0:T(8,128)(2,1)}, bf16[2,384,384]{2,1,0:T(8,128)(2,1)}, u32[]{:S(2)}, u32[]{:S(2)}) %collective-permute-start.13) | collective-permute-done | bytes 589856 | tf_op jit(solution)/shard_map/ppermute | solution.py:167
  62.2 1.2 %convert_add_fusion.1 = f32[2,384,384]{2,1,0:T(8,128)S(1)} fusion(f32[2,384,384]{2,1,0:T(8,128)S(1)} %copy-done.12, bf16[2,384,384]{2,1,0:T(8,128)(2,1)} %collective-permute-done.13), kind=kLoop, calls=%fused_computation.2 | loop fusion | flops 589824 | bytes 2949120 | tf_op jit(solution)/shard_map/add | solution.py:266
  63.5 0.1 collective-permute-start.14
  63.6 0.1 select_bitcast_fusion
  63.6 0.7 collective-permute-start.10
  64.3 0.1 copy-done.14
  64.4 1.1 output.1
  65.6 0.1 collective-permute-start.7
  65.7 5.7 %collective-permute-done.14 = bf16[384,384]{1,0:T(8,128)(2,1)S(1)} collective-permute-done((bf16[384,384]{1,0:T(8,128)(2,1)S(1)}, bf16[384,384]{1,0:T(8,128)(2,1)S(1)}, u32[]{:S(2)}, u32[]{:S(2)}) %collective-permute-start.14) | collective-permute-done | bytes 294944 | tf_op jit(solution)/shard_map/ppermute | solution.py:167
  71.3 0.1 fusion.5
  71.4 3.1 %collective-permute-start.15 = (bf16[384,384]{1,0:T(8,128)(2,1)S(1)}, bf16[384,384]{1,0:T(8,128)(2,1)S(1)}, u32[]{:S(2)}, u32[]{:S(2)}) collective-permute-start(bf16[384,384]{1,0:T(8,128)(2,1)S(1)} %fusion.5), channel_id=1, source_target_pairs={{0,16},{4,20},{8,24},{12,28},{16,0},{20,4},{24,8},{28,12},{1,17},{... | collective-permute-start | bytes 884744 | tf_op jit(solution)/shard_map/ppermute | solution.py:167
  74.5 2.5 %collective-permute-start.9 = (bf16[2,512,384]{2,1,0:T(8,128)(2,1)S(1)}, bf16[2,512,384]{2,1,0:T(8,128)(2,1)S(1)}, u32[]{:S(2)}, u32[]{:S(2)}) collective-permute-start(bf16[2,512,384]{2,1,0:T(8,128)(2,1)S(1)} %get-tuple-element.22), channel_id=1, source_target_pairs={{4,0},{12,8},{16,12},{20,16},{28,24},{5,1},{13,9},{17,13},{21,17},... | collective-permute-start | bytes 2359304 | tf_op jit(solution)/shard_map/ppermute | solution.py:182
  77.0 0.2 fusion
  77.2 0.7 collective-permute-start.11
  77.9 0.7 collective-permute-start.12
  78.6 7.3 %collective-permute-done.15 = bf16[384,384]{1,0:T(8,128)(2,1)S(1)} collective-permute-done((bf16[384,384]{1,0:T(8,128)(2,1)S(1)}, bf16[384,384]{1,0:T(8,128)(2,1)S(1)}, u32[]{:S(2)}, u32[]{:S(2)}) %collective-permute-start.15) | collective-permute-done | bytes 294944 | tf_op jit(solution)/shard_map/ppermute | solution.py:167
  85.9 0.1 add_convert_fusion.1.first
  86.0 2.4 %collective-permute-start.16 = (bf16[384,384]{1,0:T(8,128)(2,1)S(1)}, bf16[384,384]{1,0:T(8,128)(2,1)S(1)}, u32[]{:S(2)}, u32[]{:S(2)}) collective-permute-start(bf16[384,384]{1,0:T(8,128)(2,1)S(1)} %add_convert_fusion.1.first), channel_id=1, source_target_pairs={{0,8},{4,12},{8,0},{12,4},{16,24},{20,28},{24,16},{28,20},{1,9},{5... | collective-permute-start | bytes 884744 | tf_op jit(solution)/shard_map/ppermute | solution.py:167
  88.4 0.1 convert_add_fusion
  88.6 0.8 collective-permute-start.8
  89.4 5.9 %collective-permute-done.16.second = bf16[384,384]{1,0:T(8,128)(2,1)S(1)} collective-permute-done((bf16[384,384]{1,0:T(8,128)(2,1)S(1)}, bf16[384,384]{1,0:T(8,128)(2,1)S(1)}, u32[]{:S(2)}, u32[]{:S(2)}) %collective-permute-start.16) | collective-permute-done | bytes 294944 | tf_op jit(solution)/shard_map/ppermute | solution.py:167
  95.3 0.1 pad_maximum_fusion.1
  95.4 1.1 collective-permute-start.17
  96.5 7.6 %collective-permute-done.9 = bf16[2,512,384]{2,1,0:T(8,128)(2,1)S(1)} collective-permute-done((bf16[2,512,384]{2,1,0:T(8,128)(2,1)S(1)}, bf16[2,512,384]{2,1,0:T(8,128)(2,1)S(1)}, u32[]{:S(2)}, u32[]{:S(2)}) %collective-permute-start.9) | collective-permute-done | bytes 786464 | tf_op jit(solution)/shard_map/ppermute | solution.py:182
  104.0 0.3 add_convert_fusion
  104.3 1.0 slice_bitcast_fusion.2
  105.3 0.8 fusion.3
  106.1 10.4 %collective-permute-done.17.others = bf16[2,384,384]{2,1,0:T(8,128)(2,1)S(1)} collective-permute-done((bf16[2,384,384]{2,1,0:T(8,128)(2,1)S(1)}, bf16[2,384,384]{2,1,0:T(8,128)(2,1)S(1)}, u32[]{:S(2)}, u32[]{:S(2)}) %collective-permute-start.17) | collective-permute-done | bytes 589856 | tf_op jit(solution)/shard_map/ppermute | solution.py:167
  116.5 1.6 %assemble.1 = f32[384,1536]{1,0:T(8,128)} custom-call(bf16[384,384]{1,0:T(8,128)(2,1)S(1)} %add_convert_fusion.1.first, bf16[384,384]{1,0:T(8,128)(2,1)S(1)} %collective-permute-done.16.second, bf16[2,384,384]{2,1,0:T(8,128)(2,1)S(1)} %collective-permute-done.17.others), custom_call_target="tpu_custom_call" | custom-call | tf_op jit(solution)/shard_map/assemble/pallas_call | solution.py:273
  (44 shorter events, 0.2 us)
Async XLA Ops:
  0.6 6.2 %copy-start.1 = (bf16[512,384]{1,0:T(8,128)(2,1)S(1)}, bf16[512,384]{1,0:T(8,128)(2,1)}, u32[]{:S(2)}) copy-start(bf16[512,384]{1,0:T(8,128)(2,1)} %k.3) | copy-start | bytes 1179652
  0.6 4.8 %copy-start.10 = (bf16[512,384]{1,0:T(8,128)(2,1)S(1)}, bf16[512,384]{1,0:T(8,128)(2,1)}, u32[]{:S(2)}) copy-start(bf16[512,384]{1,0:T(8,128)(2,1)} %own.3) | copy-start | bytes 1179652
  0.7 26.3 %copy-start = (bf16[384,1536]{1,0:T(8,128)(2,1)S(1)}, bf16[384,1536]{1,0:T(8,128)(2,1)}, u32[]{:S(2)}) copy-start(bf16[384,1536]{1,0:T(8,128)(2,1)} %weight.3) | copy-start | bytes 3538948
  2.0 21.2 %collective-permute-start = (bf16[2,512,384]{2,1,0:T(8,128)(2,1)S(1)}, bf16[2,512,384]{2,1,0:T(8,128)(2,1)S(1)}, u32[]{:S(2)}, u32[]{:S(2)}) collective-permute-start(bf16[2,512,384]{2,1,0:T(8,128)(2,1)S(1)} %pad_maximum_fusion), channel_id=1, source_target_pairs={{0,4},{8,12},{12,16},{16,20},{24,28},{1,5},{9,13},{13,17},{17,21},... | collective-permute-start | bytes 2359304 | tf_op jit(solution)/shard_map/ppermute | solution.py:182
  5.5 17.8 %collective-permute-start.6 = (bf16[512,384]{1,0:T(8,128)(2,1)S(1)}, bf16[512,384]{1,0:T(8,128)(2,1)S(1)}, u32[]{:S(2)}, u32[]{:S(2)}) collective-permute-start(bf16[512,384]{1,0:T(8,128)(2,1)S(1)} %copy-done.10), channel_id=1, source_target_pairs={{0,3},{1,2},{2,1},{3,0},{4,7},{5,6},{6,5},{7,4},{8,11},{9,10},{10,... | collective-permute-start | bytes 1179656 | tf_op jit(solution)/shard_map/ppermute | solution.py:167
  6.2 22.0 %collective-permute-start.1 = (bf16[2,512,384]{2,1,0:T(8,128)(2,1)S(1)}, bf16[2,512,384]{2,1,0:T(8,128)(2,1)S(1)}, u32[]{:S(2)}, u32[]{:S(2)}) collective-permute-start(bf16[2,512,384]{2,1,0:T(8,128)(2,1)S(1)} %pad_maximum_fusion), channel_id=1, source_target_pairs={{8,16},{9,17},{10,18},{11,19}} | collective-permute-start | bytes 2359304 | tf_op jit(solution)/shard_map/ppermute | solution.py:182
  6.9 21.2 %collective-permute-start.2 = (bf16[512,384]{1,0:T(8,128)(2,1)S(1)}, bf16[512,384]{1,0:T(8,128)(2,1)S(1)}, u32[]{:S(2)}, u32[]{:S(2)}) collective-permute-start(bf16[512,384]{1,0:T(8,128)(2,1)S(1)} %copy-done.1), channel_id=1, source_target_pairs={{8,20},{9,21},{10,22},{11,23}} | collective-permute-start | bytes 1179656 | tf_op jit(solution)/shard_map/ppermute | solution.py:182
  7.6 19.3 %collective-permute-start.5 = (bf16[512,384]{1,0:T(8,128)(2,1)S(1)}, bf16[512,384]{1,0:T(8,128)(2,1)S(1)}, u32[]{:S(2)}, u32[]{:S(2)}) collective-permute-start(bf16[512,384]{1,0:T(8,128)(2,1)S(1)} %copy-done.10), channel_id=1, source_target_pairs={{0,2},{1,3},{2,0},{3,1},{4,6},{5,7},{6,4},{7,5},{8,10},{9,11},{10,... | collective-permute-start | bytes 1179656 | tf_op jit(solution)/shard_map/ppermute | solution.py:167
  23.2 3.8 %collective-permute-start.4 = (bf16[512,384]{1,0:T(8,128)(2,1)S(1)}, bf16[512,384]{1,0:T(8,128)(2,1)S(1)}, u32[]{:S(2)}, u32[]{:S(2)}) collective-permute-start(bf16[512,384]{1,0:T(8,128)(2,1)S(1)} %copy-done.10), channel_id=1, source_target_pairs={{0,1},{1,0},{2,3},{3,2},{4,5},{5,4},{6,7},{7,6},{8,9},{9,8},{10,11... | collective-permute-start | bytes 1179656 | tf_op jit(solution)/shard_map/ppermute | solution.py:167
  23.2 12.7 %copy-start.2 = (bf16[512,384]{1,0:T(8,128)(2,1)S(1)}, bf16[512,384]{1,0:T(8,128)(2,1)}, u32[]{:S(2)}) copy-start(bf16[512,384]{1,0:T(8,128)(2,1)} %v.3) | copy-start | bytes 1179652
  23.2 12.7 %copy-start.5 = (bf16[512,384]{1,0:T(8,128)(2,1)S(1)}, bf16[512,384]{1,0:T(8,128)(2,1)}, u32[]{:S(2)}) copy-start(bf16[512,384]{1,0:T(8,128)(2,1)} %q.3) | copy-start | bytes 1179652
  23.3 12.7 %copy-start.17 = (s32[8]{0:T(128)S(1)}, s32[8]{0:T(128)}, u32[]{:S(2)}) copy-start(s32[8]{0:T(128)} %anchor.3) | copy-start | bytes 100
  23.3 12.6 %collective-permute-start.3 = (bf16[512,384]{1,0:T(8,128)(2,1)S(1)}, bf16[512,384]{1,0:T(8,128)(2,1)S(1)}, u32[]{:S(2)}, u32[]{:S(2)}) collective-permute-start(bf16[512,384]{1,0:T(8,128)(2,1)S(1)} %slice_bitcast_fusion.4), channel_id=1, source_target_pairs={{12,20},{13,21},{14,22},{15,23}} | collective-permute-start | bytes 1179656 | tf_op jit(solution)/shard_map/ppermute | solution.py:182
  28.1 15.8 %copy-start.6 = (bf16[512,384]{1,0:T(8,128)(2,1)}, bf16[512,384]{1,0:T(8,128)(2,1)S(1)}, u32[]{:S(2)}) copy-start(bf16[512,384]{1,0:T(8,128)(2,1)S(1)} %collective-permute-done.2.rest_0_) | copy-start | bytes 1179652
  28.1 15.8 %copy-start.3 = (bf16[2,512,384]{2,1,0:T(8,128)(2,1)}, bf16[2,512,384]{2,1,0:T(8,128)(2,1)S(1)}, u32[]{:S(2)}) copy-start(bf16[2,512,384]{2,1,0:T(8,128)(2,1)S(1)} %collective-permute-done.1.far) | copy-start | bytes 2359300
  35.9 8.0 %copy-start.8 = (bf16[512,384]{1,0:T(8,128)(2,1)}, bf16[512,384]{1,0:T(8,128)(2,1)S(1)}, u32[]{:S(2)}) copy-start(bf16[512,384]{1,0:T(8,128)(2,1)S(1)} %collective-permute-done.3.rest_1_) | copy-start | bytes 1179652
  43.9 2.0 %copy-start.13 = (bf16[512,384]{1,0:T(8,128)(2,1)}, bf16[512,384]{1,0:T(8,128)(2,1)S(1)}, u32[]{:S(2)}) copy-start(bf16[512,384]{1,0:T(8,128)(2,1)S(1)} %get-tuple-element.16.attended) | copy-start | bytes 1179652
  43.9 3.0 %copy-start.15 = (f32[3,8,512]{2,1,0:T(8,128)}, f32[3,8,512]{2,1,0:T(8,128)S(1)}, u32[]{:S(2)}) copy-start(f32[3,8,512]{2,1,0:T(8,128)S(1)} %get-tuple-element.19.rest_3_) | copy-start | bytes 147460
  45.9 1.0 copy-start.11
  47.0 15.3 %collective-permute-start.13 = (bf16[2,384,384]{2,1,0:T(8,128)(2,1)}, bf16[2,384,384]{2,1,0:T(8,128)(2,1)}, u32[]{:S(2)}, u32[]{:S(2)}) collective-permute-start(bf16[2,384,384]{2,1,0:T(8,128)(2,1)} %get-tuple-element.26), channel_id=1, source_target_pairs={{0,4},{4,0},{8,12},{12,8},{16,20},{20,16},{24,28},{28,24},{1,5},{5... | collective-permute-start | bytes 1769480 | tf_op jit(solution)/shard_map/ppermute | solution.py:167
  47.6 1.1 copy-start.4
  48.7 1.0 copy-start.7
  49.7 1.0 copy-start.9
  50.7 0.8 copy-start.16
  51.5 10.7 %copy-start.12 = (f32[2,384,384]{2,1,0:T(8,128)S(1)}, f32[2,384,384]{2,1,0:T(8,128)}, u32[]{:S(2)}) copy-start(f32[2,384,384]{2,1,0:T(8,128)} %copy-done.11) | copy-start | bytes 3538948
  63.4 1.0 copy-start.14
  63.5 7.8 %collective-permute-start.14 = (bf16[384,384]{1,0:T(8,128)(2,1)S(1)}, bf16[384,384]{1,0:T(8,128)(2,1)S(1)}, u32[]{:S(2)}, u32[]{:S(2)}) collective-permute-start(bf16[384,384]{1,0:T(8,128)(2,1)S(1)} %fusion.7), channel_id=1, source_target_pairs={{0,8},{4,12},{8,0},{12,4},{16,24},{20,28},{24,16},{28,20},{1,9},{5... | collective-permute-start | bytes 884744 | tf_op jit(solution)/shard_map/ppermute | solution.py:167
  63.6 13.4 %collective-permute-start.10 = (bf16[512,384]{1,0:T(8,128)(2,1)S(1)}, bf16[512,384]{1,0:T(8,128)(2,1)S(1)}, u32[]{:S(2)}, u32[]{:S(2)}) collective-permute-start(bf16[512,384]{1,0:T(8,128)(2,1)S(1)} %select_bitcast_fusion), channel_id=1, source_target_pairs={{16,20},{20,16},{17,21},{21,17},{18,22},{22,18},{19,23},{23,19}} | collective-permute-start | bytes 1179656 | tf_op jit(solution)/shard_map/ppermute | solution.py:182
  65.6 22.8 %collective-permute-start.7 = (bf16[2,512,384]{2,1,0:T(8,128)(2,1)S(1)}, bf16[2,512,384]{2,1,0:T(8,128)(2,1)S(1)}, u32[]{:S(2)}, u32[]{:S(2)}) collective-permute-start(bf16[2,512,384]{2,1,0:T(8,128)(2,1)S(1)} %get-tuple-element.18), channel_id=1, source_target_pairs={{0,1},{1,0},{2,3},{3,2},{4,5},{5,4},{6,7},{7,6},{8,9},{9,8},{10,11... | collective-permute-start | bytes 2359304 | tf_op jit(solution)/shard_map/ppermute | solution.py:167
  71.4 14.5 %collective-permute-start.15 = (bf16[384,384]{1,0:T(8,128)(2,1)S(1)}, bf16[384,384]{1,0:T(8,128)(2,1)S(1)}, u32[]{:S(2)}, u32[]{:S(2)}) collective-permute-start(bf16[384,384]{1,0:T(8,128)(2,1)S(1)} %fusion.5), channel_id=1, source_target_pairs={{0,16},{4,20},{8,24},{12,28},{16,0},{20,4},{24,8},{28,12},{1,17},{... | collective-permute-start | bytes 884744 | tf_op jit(solution)/shard_map/ppermute | solution.py:167
  74.5 29.5 %collective-permute-start.9 = (bf16[2,512,384]{2,1,0:T(8,128)(2,1)S(1)}, bf16[2,512,384]{2,1,0:T(8,128)(2,1)S(1)}, u32[]{:S(2)}, u32[]{:S(2)}) collective-permute-start(bf16[2,512,384]{2,1,0:T(8,128)(2,1)S(1)} %get-tuple-element.22), channel_id=1, source_target_pairs={{4,0},{12,8},{16,12},{20,16},{28,24},{5,1},{13,9},{17,13},{21,17},... | collective-permute-start | bytes 2359304 | tf_op jit(solution)/shard_map/ppermute | solution.py:182
  77.2 19.2 %collective-permute-start.11 = (bf16[512,384]{1,0:T(8,128)(2,1)S(1)}, bf16[512,384]{1,0:T(8,128)(2,1)S(1)}, u32[]{:S(2)}, u32[]{:S(2)}) collective-permute-start(bf16[512,384]{1,0:T(8,128)(2,1)S(1)} %get-tuple-element.27), channel_id=1, source_target_pairs={{16,8},{17,9},{18,10},{19,11}} | collective-permute-start | bytes 1179656 | tf_op jit(solution)/shard_map/ppermute | solution.py:182
  77.9 18.5 %collective-permute-start.12 = (bf16[512,384]{1,0:T(8,128)(2,1)S(1)}, bf16[512,384]{1,0:T(8,128)(2,1)S(1)}, u32[]{:S(2)}, u32[]{:S(2)}) collective-permute-start(bf16[512,384]{1,0:T(8,128)(2,1)S(1)} %get-tuple-element.28), channel_id=1, source_target_pairs={{20,8},{21,9},{22,10},{23,11}} | collective-permute-start | bytes 1179656 | tf_op jit(solution)/shard_map/ppermute | solution.py:182
  86.0 9.4 %collective-permute-start.16 = (bf16[384,384]{1,0:T(8,128)(2,1)S(1)}, bf16[384,384]{1,0:T(8,128)(2,1)S(1)}, u32[]{:S(2)}, u32[]{:S(2)}) collective-permute-start(bf16[384,384]{1,0:T(8,128)(2,1)S(1)} %add_convert_fusion.1.first), channel_id=1, source_target_pairs={{0,8},{4,12},{8,0},{12,4},{16,24},{20,28},{24,16},{28,20},{1,9},{5... | collective-permute-start | bytes 884744 | tf_op jit(solution)/shard_map/ppermute | solution.py:167
  88.6 16.7 %collective-permute-start.8 = (bf16[512,384]{1,0:T(8,128)(2,1)S(1)}, bf16[512,384]{1,0:T(8,128)(2,1)S(1)}, u32[]{:S(2)}, u32[]{:S(2)}) collective-permute-start(bf16[512,384]{1,0:T(8,128)(2,1)S(1)} %fusion.6), channel_id=1, source_target_pairs={{0,2},{1,3},{2,0},{3,1},{4,6},{5,7},{6,4},{7,5},{8,10},{9,11},{10,... | collective-permute-start | bytes 1179656 | tf_op jit(solution)/shard_map/ppermute | solution.py:167
  95.4 21.1 %collective-permute-start.17 = (bf16[2,384,384]{2,1,0:T(8,128)(2,1)S(1)}, bf16[2,384,384]{2,1,0:T(8,128)(2,1)S(1)}, u32[]{:S(2)}, u32[]{:S(2)}) collective-permute-start(bf16[2,384,384]{2,1,0:T(8,128)(2,1)S(1)} %pad_maximum_fusion.1), channel_id=1, source_target_pairs={{0,4},{4,0},{8,12},{12,8},{16,20},{20,16},{24,28},{28,24},{1,5},{5... | collective-permute-start | bytes 1769480 | tf_op jit(solution)/shard_map/ppermute | solution.py:167

commit v3 on v2

v3 whole, which is shorter than its diff:
```python
import functools
import math

import jax
import jax.numpy as jnp
from jax import lax
from jax.experimental import pallas as pl
from jax.experimental.pallas import tpu as pltpu
from jax.sharding import PartitionSpec as P

HEAD_DIM = 128
BF16 = jnp.bfloat16
F32 = jnp.float32
SCALE = HEAD_DIM ** -0.5
SCALE_LOG2 = SCALE * math.log2(math.e)
Q_CHUNK = 256


def dot(a, b, dims):
    return lax.dot_general(a, b, (dims, ((), ())), preferred_element_type=F32)


def anchor_bounds(frames, seg):
    forced = frames // 2 - 2
    bounds = []
    for f in range(frames):
        if f < forced:
            bounds.append((max(0, f - seg + 1), f))
        elif f < forced + seg:
            bounds.append((forced, forced))
        else:
            bounds.append((max(forced + seg, f - seg + 1), f))
    return bounds


def vmem():
    return pl.BlockSpec(memory_space=pltpu.VMEM)


def smem():
    return pl.BlockSpec(memory_space=pltpu.SMEM)


def params(mebibytes):
    return pltpu.CompilerParams(vmem_limit_bytes=mebibytes * 1024 * 1024)


def cotangent_kernel(own, second, third, fourth, weight, out):
    head = lax.axis_index("head")
    width = own.shape[1]
    total = None
    for m, piece in enumerate((own, second, third, fourth)):
        start = pl.multiple_of((head ^ m) * width, 128)
        term = dot(piece[...], weight[:, pl.ds(start, width)], ((1,), (1,)))
        total = term if total is None else total + term
    out[...] = total.astype(BF16)


def earlier(anchor, own, prev):
    f = lax.axis_index("tm")
    return jnp.where(anchor[f] < f, prev, own[...])


def furthest(anchor, own, prev, far):
    f = lax.axis_index("tm")
    distant = far[0]
    for more in far[1:]:
        distant = distant + more
    return jnp.where(f - anchor[f] >= 2, distant, earlier(anchor, own, prev))


def distant_pair(far):
    return [far[0][0], *[x[...] for x in far[1:2]]], [far[0][1], *[x[...] for x in far[2:3]]]


def near_kernel(anchor, q, k, v, prev, part, stats, keys, values):
    rows = q.shape[0]
    keys[:rows, :] = earlier(anchor, k, prev[0])
    keys[rows:, :] = k[...]
    values[:rows, :] = earlier(anchor, v, prev[1])
    values[rows:, :] = v[...]
    for c in range(rows // Q_CHUNK):
        at = pl.ds(c * Q_CHUNK, Q_CHUNK)
        scores = dot(keys[...], q[at, :], ((1,), (1,)))
        highest = jnp.max(scores, axis=0, keepdims=True)
        raw = jnp.exp2((scores - highest) * SCALE_LOG2)
        part[0, :, at] = dot(values[...], raw.astype(BF16), ((0,), (0,)))
        stats[0, 0:1, at] = highest
        stats[0, 1:2, at] = jnp.sum(raw, axis=0, keepdims=True)


def far_kernel(count, anchor, q, k, v, prev, *rest):
    far_k, far_v = distant_pair(rest[:count])
    part, near, grad, *columns = rest[count : count + 7]
    out, stats, keep, send, pieces, turned = rest[count + 7 :]
    rows = q.shape[0]
    tm = lax.axis_index("tm")
    sel = (tm % 2) * 2 + (tm // 2) % 2

    @pl.when(pl.program_id(0) == 0)
    def _():
        for m, piece in enumerate(columns):
            pieces[m] = piece[...]

    keys = furthest(anchor, k, prev[0], far_k)
    values = furthest(anchor, v, prev[1], far_v)
    for c in range(rows // Q_CHUNK):
        at = pl.ds(c * Q_CHUNK, Q_CHUNK)
        scores = dot(keys, q[at, :], ((1,), (1,)))
        before = near[0, 0:1, at]
        highest = jnp.maximum(jnp.max(scores, axis=0, keepdims=True), before)
        raw = jnp.exp2((scores - highest) * SCALE_LOG2)
        fade = jnp.exp2((before - highest) * SCALE_LOG2)
        total = jnp.sum(raw, axis=0, keepdims=True) + near[0, 1:2, at] * fade
        attended = dot(values, raw.astype(BF16), ((0,), (0,))) + part[0, :, at] * fade
        attended = attended / total
        turned[:, at] = attended.astype(BF16)
        out[at, :] = attended.T.astype(BF16)
        delta = jnp.sum(attended * grad[at, :].astype(F32).T, axis=0, keepdims=True)
        stats[0, 0:1, at] = highest * SCALE_LOG2 + jnp.log2(total)
        stats[0, 1:2, at] = delta
    for at, slot in enumerate((1, 3)):
        send[at] = dot(turned[...], pieces[slot ^ sel], ((1,), (0,))).astype(BF16)
    for at, slot in enumerate((0, 2)):
        keep[at] = dot(turned[...], pieces[slot ^ sel], ((1,), (0,)))


def backward_kernel(count, lower, anchor, q, k, v, prev, *rest):
    far_k, far_v = distant_pair(rest[:count])
    grad, stats, dq, own_grad, near_dk, near_dv, stays, leaves = rest[count : count + 8]
    keys, values, dk, dv = rest[count + 8 :]
    rows = q.shape[0]
    keys[:rows, :] = furthest(anchor, k, prev[0], far_k)
    keys[rows : 2 * rows, :] = earlier(anchor, k, prev[0])
    keys[2 * rows :, :] = k[...]
    values[:rows, :] = furthest(anchor, v, prev[1], far_v)
    values[rows : 2 * rows, :] = earlier(anchor, v, prev[1])
    values[2 * rows :, :] = v[...]
    for c in range(rows // Q_CHUNK):
        at = pl.ds(c * Q_CHUNK, Q_CHUNK)
        queries, cot = q[at, :], grad[at, :]
        scores = dot(keys[...], queries, ((1,), (1,)))
        prob = jnp.exp2(scores * SCALE_LOG2 - stats[0, 0:1, at])
        prob_grad = dot(values[...], cot, ((1,), (1,)))
        score_grad = (prob * (prob_grad - stats[0, 1:2, at])).astype(BF16)
        dv_term = dot(prob.astype(BF16), cot, ((1,), (0,)))
        dk_term = dot(score_grad, queries, ((1,), (0,)))
        if c == 0:
            dv[...] = dv_term
            dk[...] = dk_term
        else:
            dv[...] += dv_term
            dk[...] += dk_term
        dq_t = dot(keys[...], score_grad, ((0,), (0,))) * SCALE
        dq[at, :] = dq_t.T.astype(BF16)
    f = lax.axis_index("tm")
    a = anchor[f]
    distant = []
    for kind, (ref, near, factor) in enumerate(((dk, near_dk, SCALE), (dv, near_dv, None))):
        parts = [ref[pl.ds(block * rows, rows), :] for block in range(3)]
        if factor is not None:
            parts = [part * factor for part in parts]
        close = parts[1] + jnp.where(f - a >= 2, 0.0, parts[0])
        distant.append(jnp.where(f - a >= 2, parts[0], 0.0).astype(BF16))
        near[...] = jnp.where(a < f, close, 0.0).astype(BF16)
        own_grad[kind] = parts[2] + jnp.where(a < f, 0.0, close)
    swapped = f != lower
    stays[...] = jnp.where(swapped, distant[1], distant[0])
    leaves[...] = jnp.where(swapped, distant[0], distant[1])


def output_kernel(attended, weight, keep, send):
    head = lax.axis_index("head")
    width = weight.shape[0]
    for m in range(4):
        start = pl.multiple_of((head ^ m) * width, 128)
        part = dot(attended[...], weight[:, pl.ds(start, width)], ((1,), (0,)))
        if m % 2:
            send[m // 2] = part.astype(BF16)
        else:
            keep[m // 2] = part


def assemble_kernel(own, other, last, out):
    head = lax.axis_index("head")
    tm = lax.axis_index("tm")
    sel = (tm % 2) * 2 + (tm // 2) % 2
    width = own.shape[0]
    for slot, value in enumerate((own[...], last[0], other[...], last[1])):
        start = pl.multiple_of((head ^ sel ^ slot) * width, 128)
        out[:, pl.ds(start, width)] = value.astype(out.dtype)


def swap(array, axis, bit):
    return lax.ppermute(array, axis, [(i, i ^ bit) for i in range(lax.axis_size(axis))])


def local(query_rows, key_rows, value_rows, output_weight, output_grad, anchor):
    rows, cols = query_rows.shape
    heads = cols // HEAD_DIM
    frames = lax.axis_size("tm")
    seg = min(8, frames // 2)
    bounds = anchor_bounds(frames, seg)
    near_pairs = [(f - 1, f) for f in range(1, frames) if bounds[f][0] < f]
    far_frames = [f for f in range(frames) if f - bounds[f][0] >= 2]
    pair_plan = len(far_frames) == 2 and all(bounds[f][0] == bounds[f][1] for f in far_frames)

    def send(array, pairs):
        return lax.ppermute(array, "tm", pairs)

    def back(pairs):
        return [(b, a) for a, b in pairs]

    own_pair = jnp.stack([key_rows, value_rows])
    prev = send(own_pair, near_pairs)
    if pair_plan:
        lower, upper = far_frames
        source = bounds[lower][0]
        far = (
            send(own_pair, [(source, lower)]),
            send(key_rows, [(source, upper)]),
            send(prev[1], [(source + 1, upper)]),
        )
    else:
        position = lax.axis_index("tm")
        own_anchor = jnp.sum(jnp.where(jnp.arange(frames) == position, anchor, 0))
        distance = position - own_anchor
        fetched = jnp.where(distance == 0, own_pair, prev)
        step = 2
        while step < seg:
            pairs = [(f - step, f) for f in range(step, frames) if f - bounds[f][0] >= step]
            fetched = jnp.where(distance >= step, send(fetched, pairs), fetched)
            step *= 2
        far = (fetched,)

    columns = (output_grad, *[swap(output_grad, "head", m) for m in (1, 2, 3)])
    attended_grad = pl.pallas_call(
        cotangent_kernel,
        out_shape=jax.ShapeDtypeStruct((rows, cols), BF16),
        in_specs=[vmem()] * 5,
        out_specs=vmem(),
        compiler_params=params(8),
        name="cotangent",
    )(*columns, output_weight)

    by_head = pl.BlockSpec((rows, HEAD_DIM), lambda h: (0, h))
    pair_by_head = pl.BlockSpec((2, rows, HEAD_DIM), lambda h: (0, 0, h))
    stat_spec = pl.BlockSpec((1, 8, rows), lambda h: (h, 0, 0))
    part_spec = pl.BlockSpec((1, HEAD_DIM, rows), lambda h: (h, 0, 0))
    narrow = jax.ShapeDtypeStruct((rows, cols), BF16)
    part_shape = jax.ShapeDtypeStruct((heads, HEAD_DIM, rows), F32)
    stat_shape = jax.ShapeDtypeStruct((heads, 8, rows), F32)

    count = len(far)
    near_args = (anchor, query_rows, key_rows, value_rows, prev)
    near_specs = [smem(), by_head, by_head, by_head, pair_by_head]
    far_specs = [*near_specs, pair_by_head, *[by_head] * (count - 1)]
    part, near = pl.pallas_call(
        near_kernel,
        grid=(heads,),
        out_shape=(part_shape, stat_shape),
        in_specs=near_specs,
        out_specs=(part_spec, stat_spec),
        scratch_shapes=[pltpu.VMEM((2 * rows, HEAD_DIM), BF16)] * 2,
        compiler_params=params(12),
        name="near",
    )(*near_args)

    half_spec = pl.BlockSpec((2, HEAD_DIM, cols), lambda h: (0, h, 0))
    attended, stats, keep, away = pl.pallas_call(
        functools.partial(far_kernel, count),
        grid=(heads,),
        out_shape=(
            narrow,
            stat_shape,
            jax.ShapeDtypeStruct((2, cols, cols), F32),
            jax.ShapeDtypeStruct((2, cols, cols), BF16),
        ),
        in_specs=[*far_specs, part_spec, stat_spec, by_head, *[vmem()] * 4],
        out_specs=(by_head, stat_spec, half_spec, half_spec),
        scratch_shapes=[pltpu.VMEM((4, rows, cols), BF16), pltpu.VMEM((HEAD_DIM, rows), BF16)],
        compiler_params=params(14),
        name="far",
    )(*near_args, *far, part, near, attended_grad, *columns)

    query_grad, own_grad, near_dk, near_dv, far_dv, far_dk = pl.pallas_call(
        functools.partial(backward_kernel, count, far_frames[0] if pair_plan else -1),
        grid=(heads,),
        out_shape=(narrow, jax.ShapeDtypeStruct((2, rows, cols), F32), narrow, narrow, narrow, narrow),
        in_specs=[*far_specs, by_head, stat_spec],
        out_specs=(by_head, pair_by_head, *[by_head] * 4),
        scratch_shapes=[pltpu.VMEM((3 * rows, HEAD_DIM), BF16)] * 2
        + [pltpu.VMEM((3 * rows, HEAD_DIM), F32)] * 2,
        compiler_params=params(16),
        name="backward",
    )(*near_args, *far, attended_grad, stats)

    if pair_plan:
        stays, leaves = far_dv, far_dk
        from_k = send(near_dk, back(near_pairs))
        crossing = send(leaves, [(lower, upper), (upper, lower)])
        merged = (stays.astype(F32) + crossing.astype(F32)).astype(BF16)
    if frames == 8:
        arrived, query_grad = lax.optimization_barrier((swap(away, "tm", 2), query_grad))
        half = keep + arrived.astype(F32)
        quarter = (half[0] + swap(half[1].astype(BF16), "tm", 1).astype(F32)).astype(BF16)
        own = (quarter.astype(F32) + swap(quarter, "tm", 4).astype(F32)).astype(BF16)
        own, merged = lax.optimization_barrier((own, merged))
        other = swap(own, "tm", 1)
        sums = (own, other, swap(jnp.stack([own, other]), "tm", 2))
    else:
        sums = (keep[0], keep[1], away.astype(F32))
    weight_grad = pl.pallas_call(
        assemble_kernel,
        out_shape=jax.ShapeDtypeStruct((cols, 4 * cols), F32),
        in_specs=[vmem()] * 3,
        out_specs=vmem(),
        compiler_params=params(8),
        name="assemble",
    )(*sums)
    if frames != 8:
        weight_grad = lax.psum(weight_grad, "tm")

    if pair_plan:
        home_k = send(merged, [(lower, source)]).astype(F32)
        home_v = send(merged, [(upper, source + 1)]).astype(F32)
        from_v = send((near_dv.astype(F32) + home_v).astype(BF16), back(near_pairs)).astype(F32)
        key_total = own_grad[0] + from_k.astype(F32) + home_k
        value_total = own_grad[1] + from_v
    else:
        both = []
        for own, near, far in ((own_grad[0], near_dk, far_dk), (own_grad[1], near_dv, far_dv)):
            held = far.astype(F32)
            step = 2
            while 2 * step < seg:
                step *= 2
            while step >= 2:
                pairs = [(f, f - step) for f in range(step, frames) if f - bounds[f][0] >= step]
                leaving = jnp.where(distance >= step, held, 0.0)
                held = (held - leaving) + send(leaving.astype(BF16), pairs).astype(F32)
                step //= 2
            to_prev = near.astype(F32) + jnp.where(distance == 1, held, 0.0)
            from_near = send(to_prev.astype(BF16), back(near_pairs)).astype(F32)
            both.append(own + from_near + jnp.where(distance == 0, held, 0.0))
        key_total, value_total = both
    key_grad, value_grad = key_total.astype(BF16), value_total.astype(BF16)

    out_keep, out_send = pl.pallas_call(
        output_kernel,
        out_shape=(
            jax.ShapeDtypeStruct((2, rows, cols), F32),
            jax.ShapeDtypeStruct((2, rows, cols), BF16),
        ),
        in_specs=[vmem()] * 2,
        out_specs=(vmem(), vmem()),
        compiler_params=params(8),
        name="output",
    )(attended, output_weight)
    pair_sum = out_keep + swap(out_send, "head", 1).astype(F32)
    layer_output = (pair_sum[0] + swap(pair_sum[1].astype(BF16), "head", 2).astype(F32)).astype(BF16)
    return layer_output, query_grad, key_grad, value_grad, weight_grad


def solution(mesh):
    in_specs = (
        P("tm", "head"),
        P("tm", "head"),
        P("tm", "head"),
        P("head", None),
        P("tm", "head"),
        P(),
    )
    out_specs = (
        P("tm", "head"),
        P("tm", "head"),
        P("tm", "head"),
        P("tm", "head"),
        P("head", None),
    )
    return jax.shard_map(local, mesh=mesh, in_specs=in_specs, out_specs=out_specs, check_vma=False)
```

time: 119 us -> 112 us (0.941)
  local copies, waits for them, and re-layouts: 6.18 us -> 0.15 us
  Pallas kernels: 22.2 us -> 23.9 us
    ppermute x10, waiting for transfers between devices: 31.6 us -> 24.9 us  [swap(): lax.ppermute(array, axis, [(i, i ^ bit) for i in range(lax.axis_size(axis...]
    ppermute x8 -> x9, waiting for transfers between devices: 30 us -> 35.9 us  [send(): return lax.ppermute(array, 'tm', pairs)]
    unnamed x36 -> x12, local copies, waits for them, and re-layouts: 5.11 us -> 0.03 us
    ppermute x10, starting transfers between devices: 9.79 us -> 6.72 us  [swap(): lax.ppermute(array, axis, [(i, i ^ bit) for i in range(lax.axis_size(axis...]
    ppermute x8 -> x9, starting transfers between devices: 13 us -> 15.2 us  [send(): return lax.ppermute(array, 'tm', pairs)]
    pallas_call x3, Pallas kernels: 18.3 us -> 20 us  [the longest x1 8.43 us: local(): pl.pallas_call(functools.partial(backward_kernel, count, far_frames[0] if...]
  transfers between devices with their start and end apart: 18 -> 19, of which waited for: 8 -> 9; matrix products, arithmetic and copies ran while one was open for 2% -> 2% of each run, Pallas kernels for 9% -> 15%
where the time goes in v3:
time: 112 us
  waiting for transfers between devices  60.8 us (54%)
  Pallas kernels  23.9 us (21%)
  starting transfers between devices  21.9 us (20%)
  other arithmetic  3.98 us (4%)
    ppermute x9, waiting for transfers between devices, send(): return lax.ppermute(array, 'tm', pairs)  35.9 us
    ppermute x10, waiting for transfers between devices, swap(): lax.ppermute(array, axis, [(i, i ^ bit) for i in range(lax.axis_size(axis...  24.9 us
    ppermute x9, starting transfers between devices, send(): return lax.ppermute(array, 'tm', pairs)  15.2 us
    pallas_call x1, Pallas kernels, local(): pl.pallas_call(functools.partial(backward_kernel, count, far_frames[0] if...  8.43 us
    ppermute x10, starting transfers between devices, swap(): lax.ppermute(array, axis, [(i, i ^ bit) for i in range(lax.axis_size(axis...  6.72 us
    pallas_call x1, Pallas kernels, local(): pl.pallas_call(functools.partial(far_kernel, count), grid=(heads,), out_s...  5.85 us
    pallas_call x1, Pallas kernels, local(): pl.pallas_call(near_kernel, grid=(heads,), out_shape=(part_shape, stat_sh...  5.73 us
  transfers between devices with their start and end apart: 19, of which 9 were waited for; matrix products, arithmetic and copies ran while one was open for 2% of the time, Pallas kernels for 15%

profile of v3, /device:TPU:12, one launch (start us, length us, event | category | flops | bytes accessed | tf_op | source)
XLA Modules:
  0.0 111.7 jit_solution(7877406128703964943)
XLA Ops:
  0.7 1.3 %pad_maximum_fusion = bf16[2,512,384]{2,1,0:T(8,128)(2,1)S(1)} fusion(bf16[1,512,384]{2,1,0:T(8,128)(2,1)} %bitcast.33, bf16[1,512,384]{2,1,0:T(8,128)(2,1)} %bitcast.32), kind=kLoop, calls=%fused_computation.6 | loop fusion | flops 393216 | bytes 1572864 | tf_op jit(solution)/shard_map/stack | solution.py:214
  2.0 3.4 %collective-permute-start = (bf16[2,512,384]{2,1,0:T(8,128)(2,1)S(1)}, bf16[2,512,384]{2,1,0:T(8,128)(2,1)S(1)}, u32[]{:S(2)}, u32[]{:S(2)}) collective-permute-start(bf16[2,512,384]{2,1,0:T(8,128)(2,1)S(1)} %pad_maximum_fusion), channel_id=1, source_target_pairs={{0,4},{8,12},{12,16},{16,20},{24,28},{1,5},{9,13},{13,17},{17,21},... | collective-permute-start | bytes 2359304 | tf_op jit(solution)/shard_map/ppermute | solution.py:209
  5.5 0.7 collective-permute-start.6
  6.2 0.7 collective-permute-start.1
  6.9 0.7 collective-permute-start.2
  7.6 0.9 collective-permute-start.5
  8.5 14.7 %collective-permute-done.prev = bf16[2,512,384]{2,1,0:T(8,128)(2,1)S(1)} collective-permute-done((bf16[2,512,384]{2,1,0:T(8,128)(2,1)S(1)}, bf16[2,512,384]{2,1,0:T(8,128)(2,1)S(1)}, u32[]{:S(2)}, u32[]{:S(2)}) %collective-permute-start) | collective-permute-done | bytes 786464 | tf_op jit(solution)/shard_map/ppermute | solution.py:209
  23.2 0.0 collective-permute-start.4
  23.2 0.0 copy-start.1
  23.2 0.0 copy-start.3
  23.3 0.0 copy-start.5
  23.3 0.0 collective-permute-done.6.fourth.rest_9_
  23.3 3.6 %collective-permute-start.3 = (bf16[512,384]{1,0:T(8,128)(2,1)S(1)}, bf16[512,384]{1,0:T(8,128)(2,1)S(1)}, u32[]{:S(2)}, u32[]{:S(2)}) collective-permute-start(bf16[512,384]{1,0:T(8,128)(2,1)S(1)} %slice_bitcast_fusion.2), channel_id=1, source_target_pairs={{12,20},{13,21},{14,22},{15,23}} | collective-permute-start | bytes 1179656 | tf_op jit(solution)/shard_map/ppermute | solution.py:209
  27.0 1.1 %cotangent.1.rest_5_.rest_3_ = bf16[512,384]{1,0:T(8,128)(2,1)S(1)} custom-call(bf16[512,384]{1,0:T(8,128)(2,1)S(1)} %copy-done.4, bf16[512,384]{1,0:T(8,128)(2,1)S(1)} %collective-permute-done.4.second.rest_7_, bf16[512,384]{1,0:T(8,128)(2,1)S(1)} %collective-permute-done.5.third.rest_8_, bf16[512,384]{1,0:T(8,128)(2,1)S(1)} %collective-permute-done.6.fourth.rest_9_, ...), custom_call_target="tpu_custom_call" | custom-call | tf_op jit(solution)/shard_map/cotangent/pallas_call | solution.py:237
  28.1 5.7 %near.1 = (f32[3,128,512]{2,1,0:T(8,128)S(1)}, f32[3,8,512]{2,1,0:T(8,128)S(1)}) custom-call(s32[8]{0:T(128)S(1)} %copy-done.5, bf16[512,384]{1,0:T(8,128)(2,1)S(1)} %copy-done.3, bf16[512,384]{1,0:T(8,128)(2,1)S(1)} %copy-done, bf16[512,384]{1,0:T(8,128)(2,1)S(1)} %copy-done.1, bf16[2,512,384]{2,1,0:T(8,128)(2,1)S(1)} %collective-permute-done.prev), custom_call_target="tpu_custom_call" | custom-call | tf_op jit(solution)/shard_map/near/pallas_call | solution.py:258
  33.9 2.0 %collective-permute-done.3.rest_2_ = bf16[512,384]{1,0:T(8,128)(2,1)S(1)} collective-permute-done((bf16[512,384]{1,0:T(8,128)(2,1)S(1)}, bf16[512,384]{1,0:T(8,128)(2,1)S(1)}, u32[]{:S(2)}, u32[]{:S(2)}) %collective-permute-start.3) | collective-permute-done | bytes 393248 | tf_op jit(solution)/shard_map/ppermute | solution.py:209
  35.9 5.8 %far.1 = (bf16[512,384]{1,0:T(8,128)(2,1)S(1)}, f32[3,8,512]{2,1,0:T(8,128)S(1)}, f32[2,384,384]{2,1,0:T(8,128)S(1)}, bf16[2,384,384]{2,1,0:T(8,128)(2,1)S(1)}) custom-call(s32[8]{0:T(128)S(1)} %copy-done.5, bf16[512,384]{1,0:T(8,128)(2,1)S(1)} %copy-done.3, bf16[512,384]{1,0:T(8,128)(2,1)S(1)} %copy-done, bf16[512,384]{1,0:T(8,128)(2,1)S(1)} %copy-done.1, ...), custom_call_target="tpu_custom_call" | custom-call | tf_op jit(solution)/shard_map/far/pallas_call | solution.py:270
  41.8 0.1 collective-permute-start.9
  41.9 8.4 %backward.1 = (bf16[512,384]{1,0:T(8,128)(2,1)}, f32[2,512,384]{2,1,0:T(8,128)S(1)}, bf16[512,384]{1,0:T(8,128)(2,1)S(1)}, bf16[512,384]{1,0:T(8,128)(2,1)S(1)},...) custom-call(s32[8]{0:T(128)S(1)} %copy-done.5, bf16[512,384]{1,0:T(8,128)(2,1)S(1)} %copy-done.3, ...), custom_call_target="tpu_custom_call" | custom-call | tf_op jit(solution)/shard_map/backward/pallas_call | solution.py:286
  50.3 6.5 %collective-permute-done.9 = bf16[2,384,384]{2,1,0:T(8,128)(2,1)S(1)} collective-permute-done((bf16[2,384,384]{2,1,0:T(8,128)(2,1)S(1)}, bf16[2,384,384]{2,1,0:T(8,128)(2,1)S(1)}, u32[]{:S(2)}, u32[]{:S(2)}) %collective-permute-start.9) | collective-permute-done | bytes 589856 | tf_op jit(solution)/shard_map/ppermute | solution.py:195
  56.8 0.1 convert_add_fusion.1
  57.0 1.0 collective-permute-start.11
  58.0 0.7 collective-permute-start.13
  58.7 1.1 %output.1 = (f32[2,512,384]{2,1,0:T(8,128)S(1)}, bf16[2,512,384]{2,1,0:T(8,128)(2,1)S(1)}) custom-call(bf16[512,384]{1,0:T(8,128)(2,1)S(1)} %get-tuple-element.25.attended, bf16[384,1536]{1,0:T(8,128)(2,1)S(1)} %copy-done.2), custom_call_target="tpu_custom_call" | custom-call | tf_op jit(solution)/shard_map/output/pallas_call | solution.py:348
  59.8 0.1 collective-permute-start.7
  59.9 4.9 %collective-permute-done.11 = bf16[384,384]{1,0:T(8,128)(2,1)S(1)} collective-permute-done((bf16[384,384]{1,0:T(8,128)(2,1)S(1)}, bf16[384,384]{1,0:T(8,128)(2,1)S(1)}, u32[]{:S(2)}, u32[]{:S(2)}) %collective-permute-start.11) | collective-permute-done | bytes 294944 | tf_op jit(solution)/shard_map/ppermute | solution.py:195
  64.8 0.1 fusion.6
  64.8 3.4 %collective-permute-start.12 = (bf16[384,384]{1,0:T(8,128)(2,1)S(1)}, bf16[384,384]{1,0:T(8,128)(2,1)S(1)}, u32[]{:S(2)}, u32[]{:S(2)}) collective-permute-start(bf16[384,384]{1,0:T(8,128)(2,1)S(1)} %fusion.6), channel_id=1, source_target_pairs={{0,16},{4,20},{8,24},{12,28},{16,0},{20,4},{24,8},{28,12},{1,17},{... | collective-permute-start | bytes 884744 | tf_op jit(solution)/shard_map/ppermute | solution.py:195
  68.2 2.2 %collective-permute-start.10 = (bf16[512,384]{1,0:T(8,128)(2,1)S(1)}, bf16[512,384]{1,0:T(8,128)(2,1)S(1)}, u32[]{:S(2)}, u32[]{:S(2)}) collective-permute-start(bf16[512,384]{1,0:T(8,128)(2,1)S(1)} %get-tuple-element.33), channel_id=1, source_target_pairs={{4,0},{12,8},{16,12},{20,16},{28,24},{5,1},{13,9},{17,13},{21,17},... | collective-permute-start | bytes 1179656 | tf_op jit(solution)/shard_map/ppermute | solution.py:209
  70.4 0.1 add_convert_fusion.1
  70.5 9.1 %collective-permute-done.12 = bf16[384,384]{1,0:T(8,128)(2,1)S(1)} collective-permute-done((bf16[384,384]{1,0:T(8,128)(2,1)S(1)}, bf16[384,384]{1,0:T(8,128)(2,1)S(1)}, u32[]{:S(2)}, u32[]{:S(2)}) %collective-permute-start.12) | collective-permute-done | bytes 294944 | tf_op jit(solution)/shard_map/ppermute | solution.py:195
  79.6 0.1 add_convert_fusion.2.own
  79.7 1.3 %collective-permute-start.15 = (bf16[512,384]{1,0:T(8,128)(2,1)S(1)}, bf16[512,384]{1,0:T(8,128)(2,1)S(1)}, u32[]{:S(2)}, u32[]{:S(2)}) collective-permute-start(bf16[512,384]{1,0:T(8,128)(2,1)S(1)} %add_convert_fusion.1), channel_id=1, source_target_pairs={{20,12},{21,13},{22,14},{23,15}} | collective-permute-start | bytes 1179656 | tf_op jit(solution)/shard_map/ppermute | solution.py:209
  81.0 0.2 convert_add_fusion
  81.2 0.1 collective-permute-start.17
  81.3 0.4 collective-permute-start.8
  81.7 0.7 collective-permute-start.14
  82.4 9.7 %collective-permute-done.15 = bf16[512,384]{1,0:T(8,128)(2,1)S(1)} collective-permute-done((bf16[512,384]{1,0:T(8,128)(2,1)S(1)}, bf16[512,384]{1,0:T(8,128)(2,1)S(1)}, u32[]{:S(2)}, u32[]{:S(2)}) %collective-permute-start.15) | collective-permute-done | bytes 393248 | tf_op jit(solution)/shard_map/ppermute | solution.py:209
  92.0 0.1 add_convert_fusion
  92.1 1.9 %collective-permute-start.16 = (bf16[512,384]{1,0:T(8,128)(2,1)S(1)}, bf16[512,384]{1,0:T(8,128)(2,1)S(1)}, u32[]{:S(2)}, u32[]{:S(2)}) collective-permute-start(bf16[512,384]{1,0:T(8,128)(2,1)S(1)} %add_convert_fusion), channel_id=1, source_target_pairs={{4,0},{12,8},{16,12},{20,16},{28,24},{5,1},{13,9},{17,13},{21,17},... | collective-permute-start | bytes 1179656 | tf_op jit(solution)/shard_map/ppermute | solution.py:209
  94.1 0.7 collective-permute-done.17.other
  94.7 0.1 pad_maximum_fusion.1
  94.8 0.1 collective-permute-start.18
  94.9 0.8 fusion.1
  95.7 9.6 %collective-permute-done.16 = bf16[512,384]{1,0:T(8,128)(2,1)S(1)} collective-permute-done((bf16[512,384]{1,0:T(8,128)(2,1)S(1)}, bf16[512,384]{1,0:T(8,128)(2,1)S(1)}, u32[]{:S(2)}, u32[]{:S(2)}) %collective-permute-start.16) | collective-permute-done | bytes 393248 | tf_op jit(solution)/shard_map/ppermute | solution.py:209
  105.3 1.1 fusion.2
  106.4 3.7 %collective-permute-done.18.last = bf16[2,384,384]{2,1,0:T(8,128)(2,1)S(1)} collective-permute-done((bf16[2,384,384]{2,1,0:T(8,128)(2,1)S(1)}, bf16[2,384,384]{2,1,0:T(8,128)(2,1)S(1)}, u32[]{:S(2)}, u32[]{:S(2)}) %collective-permute-start.18) | collective-permute-done | bytes 589856 | tf_op jit(solution)/shard_map/ppermute | solution.py:195
  110.1 1.6 %assemble.1 = f32[384,1536]{1,0:T(8,128)} custom-call(bf16[384,384]{1,0:T(8,128)(2,1)S(1)} %add_convert_fusion.2.own, bf16[384,384]{1,0:T(8,128)(2,1)S(1)} %collective-permute-done.17.other, bf16[2,384,384]{2,1,0:T(8,128)(2,1)S(1)} %collective-permute-done.18.last), custom_call_target="tpu_custom_call" | custom-call | tf_op jit(solution)/shard_map/assemble/pallas_call | solution.py:313
  (21 shorter events, 0.2 us)
Async XLA Ops:
  0.6 6.2 %copy-start = (bf16[512,384]{1,0:T(8,128)(2,1)S(1)}, bf16[512,384]{1,0:T(8,128)(2,1)}, u32[]{:S(2)}) copy-start(bf16[512,384]{1,0:T(8,128)(2,1)} %k.5) | copy-start | bytes 1179652
  0.6 4.8 %copy-start.4 = (bf16[512,384]{1,0:T(8,128)(2,1)S(1)}, bf16[512,384]{1,0:T(8,128)(2,1)}, u32[]{:S(2)}) copy-start(bf16[512,384]{1,0:T(8,128)(2,1)} %rest_6_.1) | copy-start | bytes 1179652
  0.7 26.3 %copy-start.2 = (bf16[384,1536]{1,0:T(8,128)(2,1)S(1)}, bf16[384,1536]{1,0:T(8,128)(2,1)}, u32[]{:S(2)}) copy-start(bf16[384,1536]{1,0:T(8,128)(2,1)} %weight.3) | copy-start | bytes 3538948
  2.0 21.2 %collective-permute-start = (bf16[2,512,384]{2,1,0:T(8,128)(2,1)S(1)}, bf16[2,512,384]{2,1,0:T(8,128)(2,1)S(1)}, u32[]{:S(2)}, u32[]{:S(2)}) collective-permute-start(bf16[2,512,384]{2,1,0:T(8,128)(2,1)S(1)} %pad_maximum_fusion), channel_id=1, source_target_pairs={{0,4},{8,12},{12,16},{16,20},{24,28},{1,5},{9,13},{13,17},{17,21},... | collective-permute-start | bytes 2359304 | tf_op jit(solution)/shard_map/ppermute | solution.py:209
  5.5 17.8 %collective-permute-start.6 = (bf16[512,384]{1,0:T(8,128)(2,1)S(1)}, bf16[512,384]{1,0:T(8,128)(2,1)S(1)}, u32[]{:S(2)}, u32[]{:S(2)}) collective-permute-start(bf16[512,384]{1,0:T(8,128)(2,1)S(1)} %copy-done.4), channel_id=1, source_target_pairs={{0,3},{1,2},{2,1},{3,0},{4,7},{5,6},{6,5},{7,4},{8,11},{9,10},{10,... | collective-permute-start | bytes 1179656 | tf_op jit(solution)/shard_map/ppermute | solution.py:195
  6.2 27.7 %collective-permute-start.1 = (bf16[2,512,384]{2,1,0:T(8,128)(2,1)S(1)}, bf16[2,512,384]{2,1,0:T(8,128)(2,1)S(1)}, u32[]{:S(2)}, u32[]{:S(2)}) collective-permute-start(bf16[2,512,384]{2,1,0:T(8,128)(2,1)S(1)} %pad_maximum_fusion), channel_id=1, source_target_pairs={{8,16},{9,17},{10,18},{11,19}} | collective-permute-start | bytes 2359304 | tf_op jit(solution)/shard_map/ppermute | solution.py:209
  6.9 27.0 %collective-permute-start.2 = (bf16[512,384]{1,0:T(8,128)(2,1)S(1)}, bf16[512,384]{1,0:T(8,128)(2,1)S(1)}, u32[]{:S(2)}, u32[]{:S(2)}) collective-permute-start(bf16[512,384]{1,0:T(8,128)(2,1)S(1)} %copy-done), channel_id=1, source_target_pairs={{8,20},{9,21},{10,22},{11,23}} | collective-permute-start | bytes 1179656 | tf_op jit(solution)/shard_map/ppermute | solution.py:209
  7.6 19.3 %collective-permute-start.5 = (bf16[512,384]{1,0:T(8,128)(2,1)S(1)}, bf16[512,384]{1,0:T(8,128)(2,1)S(1)}, u32[]{:S(2)}, u32[]{:S(2)}) collective-permute-start(bf16[512,384]{1,0:T(8,128)(2,1)S(1)} %copy-done.4), channel_id=1, source_target_pairs={{0,2},{1,3},{2,0},{3,1},{4,6},{5,7},{6,4},{7,5},{8,10},{9,11},{10,... | collective-permute-start | bytes 1179656 | tf_op jit(solution)/shard_map/ppermute | solution.py:195
  23.2 3.8 %collective-permute-start.4 = (bf16[512,384]{1,0:T(8,128)(2,1)S(1)}, bf16[512,384]{1,0:T(8,128)(2,1)S(1)}, u32[]{:S(2)}, u32[]{:S(2)}) collective-permute-start(bf16[512,384]{1,0:T(8,128)(2,1)S(1)} %copy-done.4), channel_id=1, source_target_pairs={{0,1},{1,0},{2,3},{3,2},{4,5},{5,4},{6,7},{7,6},{8,9},{9,8},{10,11... | collective-permute-start | bytes 1179656 | tf_op jit(solution)/shard_map/ppermute | solution.py:195
  23.2 4.9 %copy-start.1 = (bf16[512,384]{1,0:T(8,128)(2,1)S(1)}, bf16[512,384]{1,0:T(8,128)(2,1)}, u32[]{:S(2)}) copy-start(bf16[512,384]{1,0:T(8,128)(2,1)} %v.5) | copy-start | bytes 1179652
  23.2 4.9 %copy-start.3 = (bf16[512,384]{1,0:T(8,128)(2,1)S(1)}, bf16[512,384]{1,0:T(8,128)(2,1)}, u32[]{:S(2)}) copy-start(bf16[512,384]{1,0:T(8,128)(2,1)} %q.5) | copy-start | bytes 1179652
  23.3 4.9 %copy-start.5 = (s32[8]{0:T(128)S(1)}, s32[8]{0:T(128)}, u32[]{:S(2)}) copy-start(s32[8]{0:T(128)} %anchor.5) | copy-start | bytes 100
  23.3 12.6 %collective-permute-start.3 = (bf16[512,384]{1,0:T(8,128)(2,1)S(1)}, bf16[512,384]{1,0:T(8,128)(2,1)S(1)}, u32[]{:S(2)}, u32[]{:S(2)}) collective-permute-start(bf16[512,384]{1,0:T(8,128)(2,1)S(1)} %slice_bitcast_fusion.2), channel_id=1, source_target_pairs={{12,20},{13,21},{14,22},{15,23}} | collective-permute-start | bytes 1179656 | tf_op jit(solution)/shard_map/ppermute | solution.py:209
  41.8 15.0 %collective-permute-start.9 = (bf16[2,384,384]{2,1,0:T(8,128)(2,1)S(1)}, bf16[2,384,384]{2,1,0:T(8,128)(2,1)S(1)}, u32[]{:S(2)}, u32[]{:S(2)}) collective-permute-start(bf16[2,384,384]{2,1,0:T(8,128)(2,1)S(1)} %get-tuple-element.28), channel_id=1, source_target_pairs={{0,8},{4,12},{8,0},{12,4},{16,24},{20,28},{24,16},{28,20},{1,9},{5... | collective-permute-start | bytes 1769480 | tf_op jit(solution)/shard_map/ppermute | solution.py:195
  57.0 7.8 %collective-permute-start.11 = (bf16[384,384]{1,0:T(8,128)(2,1)S(1)}, bf16[384,384]{1,0:T(8,128)(2,1)S(1)}, u32[]{:S(2)}, u32[]{:S(2)}) collective-permute-start(bf16[384,384]{1,0:T(8,128)(2,1)S(1)} %fusion.8), channel_id=1, source_target_pairs={{0,4},{4,0},{8,12},{12,8},{16,20},{20,16},{24,28},{28,24},{1,5},{5... | collective-permute-start | bytes 884744 | tf_op jit(solution)/shard_map/ppermute | solution.py:195
  58.0 12.4 %collective-permute-start.13 = (bf16[512,384]{1,0:T(8,128)(2,1)S(1)}, bf16[512,384]{1,0:T(8,128)(2,1)S(1)}, u32[]{:S(2)}, u32[]{:S(2)}) collective-permute-start(bf16[512,384]{1,0:T(8,128)(2,1)S(1)} %get-tuple-element.37), channel_id=1, source_target_pairs={{16,20},{20,16},{17,21},{21,17},{18,22},{22,18},{19,23},{23,19}} | collective-permute-start | bytes 1179656 | tf_op jit(solution)/shard_map/ppermute | solution.py:209
  59.8 21.2 %collective-permute-start.7 = (bf16[2,512,384]{2,1,0:T(8,128)(2,1)S(1)}, bf16[2,512,384]{2,1,0:T(8,128)(2,1)S(1)}, u32[]{:S(2)}, u32[]{:S(2)}) collective-permute-start(bf16[2,512,384]{2,1,0:T(8,128)(2,1)S(1)} %get-tuple-element.27), channel_id=1, source_target_pairs={{0,1},{1,0},{2,3},{3,2},{4,5},{5,4},{6,7},{7,6},{8,9},{9,8},{10,11... | collective-permute-start | bytes 2359304 | tf_op jit(solution)/shard_map/ppermute | solution.py:195
  64.8 14.8 %collective-permute-start.12 = (bf16[384,384]{1,0:T(8,128)(2,1)S(1)}, bf16[384,384]{1,0:T(8,128)(2,1)S(1)}, u32[]{:S(2)}, u32[]{:S(2)}) collective-permute-start(bf16[384,384]{1,0:T(8,128)(2,1)S(1)} %fusion.6), channel_id=1, source_target_pairs={{0,16},{4,20},{8,24},{12,28},{16,0},{20,4},{24,8},{28,12},{1,17},{... | collective-permute-start | bytes 884744 | tf_op jit(solution)/shard_map/ppermute | solution.py:195
  68.2 27.5 %collective-permute-start.10 = (bf16[512,384]{1,0:T(8,128)(2,1)S(1)}, bf16[512,384]{1,0:T(8,128)(2,1)S(1)}, u32[]{:S(2)}, u32[]{:S(2)}) collective-permute-start(bf16[512,384]{1,0:T(8,128)(2,1)S(1)} %get-tuple-element.33), channel_id=1, source_target_pairs={{4,0},{12,8},{16,12},{20,16},{28,24},{5,1},{13,9},{17,13},{21,17},... | collective-permute-start | bytes 1179656 | tf_op jit(solution)/shard_map/ppermute | solution.py:209
  79.7 12.3 %collective-permute-start.15 = (bf16[512,384]{1,0:T(8,128)(2,1)S(1)}, bf16[512,384]{1,0:T(8,128)(2,1)S(1)}, u32[]{:S(2)}, u32[]{:S(2)}) collective-permute-start(bf16[512,384]{1,0:T(8,128)(2,1)S(1)} %add_convert_fusion.1), channel_id=1, source_target_pairs={{20,12},{21,13},{22,14},{23,15}} | collective-permute-start | bytes 1179656 | tf_op jit(solution)/shard_map/ppermute | solution.py:209
  81.2 13.6 %collective-permute-start.17 = (bf16[384,384]{1,0:T(8,128)(2,1)S(1)}, bf16[384,384]{1,0:T(8,128)(2,1)S(1)}, u32[]{:S(2)}, u32[]{:S(2)}) collective-permute-start(bf16[384,384]{1,0:T(8,128)(2,1)S(1)} %add_convert_fusion.2.own), channel_id=1, source_target_pairs={{0,4},{4,0},{8,12},{12,8},{16,20},{20,16},{24,28},{28,24},{1,5},{5... | collective-permute-start | bytes 884744 | tf_op jit(solution)/shard_map/ppermute | solution.py:195
  81.3 13.6 %collective-permute-start.8 = (bf16[512,384]{1,0:T(8,128)(2,1)S(1)}, bf16[512,384]{1,0:T(8,128)(2,1)S(1)}, u32[]{:S(2)}, u32[]{:S(2)}) collective-permute-start(bf16[512,384]{1,0:T(8,128)(2,1)S(1)} %fusion.7), channel_id=1, source_target_pairs={{0,2},{1,3},{2,0},{3,1},{4,6},{5,7},{6,4},{7,5},{8,10},{9,11},{10,... | collective-permute-start | bytes 1179656 | tf_op jit(solution)/shard_map/ppermute | solution.py:195
  81.7 14.0 %collective-permute-start.14 = (bf16[512,384]{1,0:T(8,128)(2,1)S(1)}, bf16[512,384]{1,0:T(8,128)(2,1)S(1)}, u32[]{:S(2)}, u32[]{:S(2)}) collective-permute-start(bf16[512,384]{1,0:T(8,128)(2,1)S(1)} %add_convert_fusion.1), channel_id=1, source_target_pairs={{16,8},{17,9},{18,10},{19,11}} | collective-permute-start | bytes 1179656 | tf_op jit(solution)/shard_map/ppermute | solution.py:209
  92.1 13.2 %collective-permute-start.16 = (bf16[512,384]{1,0:T(8,128)(2,1)S(1)}, bf16[512,384]{1,0:T(8,128)(2,1)S(1)}, u32[]{:S(2)}, u32[]{:S(2)}) collective-permute-start(bf16[512,384]{1,0:T(8,128)(2,1)S(1)} %add_convert_fusion), channel_id=1, source_target_pairs={{4,0},{12,8},{16,12},{20,16},{28,24},{5,1},{13,9},{17,13},{21,17},... | collective-permute-start | bytes 1179656 | tf_op jit(solution)/shard_map/ppermute | solution.py:209
  94.8 15.3 %collective-permute-start.18 = (bf16[2,384,384]{2,1,0:T(8,128)(2,1)S(1)}, bf16[2,384,384]{2,1,0:T(8,128)(2,1)S(1)}, u32[]{:S(2)}, u32[]{:S(2)}) collective-permute-start(bf16[2,384,384]{2,1,0:T(8,128)(2,1)S(1)} %pad_maximum_fusion.1), channel_id=1, source_target_pairs={{0,8},{4,12},{8,0},{12,4},{16,24},{20,28},{24,16},{28,20},{1,9},{5... | collective-permute-start | bytes 1769480 | tf_op jit(solution)/shard_map/ppermute | solution.py:195

commit v4 on v3

--- a/solution.py
+++ b/solution.py
@@ -119,10 +119,16 @@
         delta = jnp.sum(attended * grad[at, :].astype(F32).T, axis=0, keepdims=True)
         stats[0, 0:1, at] = highest * SCALE_LOG2 + jnp.log2(total)
         stats[0, 1:2, at] = delta
-    for at, slot in enumerate((1, 3)):
-        send[at] = dot(turned[...], pieces[slot ^ sel], ((1,), (0,))).astype(BF16)
-    for at, slot in enumerate((0, 2)):
-        keep[at] = dot(turned[...], pieces[slot ^ sel], ((1,), (0,)))
+    def term(slot):
+        return dot(turned[...], pieces[slot ^ sel], ((1,), (0,)))
+
+    row = pl.program_id(0) * HEAD_DIM + lax.broadcasted_iota(jnp.int32, keep.shape[1:], 0)
+    upper = row < keep.shape[2] // 2
+    second, third = term(1), term(2)
+    send[0] = jnp.where(upper, third, second).astype(BF16)
+    send[1] = term(3).astype(BF16)
+    keep[0] = term(0)
+    keep[1] = jnp.where(upper, second, third)
 
 
 def backward_kernel(count, lower, anchor, q, k, v, prev, *rest):
@@ -181,14 +187,20 @@
             keep[m // 2] = part
 
 
-def assemble_kernel(own, other, last, out):
+def assemble_kernel(*refs):
+    *parts, out = refs
     head = lax.axis_index("head")
     tm = lax.axis_index("tm")
     sel = (tm % 2) * 2 + (tm // 2) % 2
-    width = own.shape[0]
-    for slot, value in enumerate((own[...], last[0], other[...], last[1])):
-        start = pl.multiple_of((head ^ sel ^ slot) * width, 128)
-        out[:, pl.ds(start, width)] = value.astype(out.dtype)
+    row = 0
+    for group, (second, others) in enumerate(((1, (2, 3)), (2, (1, 3)))):
+        first_ref, second_ref, last_ref = parts[3 * group : 3 * group + 3]
+        height, width = first_ref.shape
+        values = {0: first_ref[...], second: second_ref[...], others[0]: last_ref[0], others[1]: last_ref[1]}
+        for slot, value in values.items():
+            start = pl.multiple_of((head ^ sel ^ slot) * width, 128)
+            out[row : row + height, pl.ds(start, width)] = value.astype(out.dtype)
+        row += height
 
 
 def swap(array, axis, bit):
@@ -298,22 +310,32 @@
     if pair_plan:
         stays, leaves = far_dv, far_dk
         from_k = send(near_dk, back(near_pairs))
+    keep_a, keep_b = keep[:, : cols // 2], keep[:, cols // 2 :]
+    away_a, away_b = away[:, : cols // 2], away[:, cols // 2 :]
+    if frames == 8:
+        arrived_a, arrived_b = swap(away_a, "tm", 1), swap(away_b, "tm", 2)
+        arrived_a, arrived_b, query_grad = lax.optimization_barrier((arrived_a, arrived_b, query_grad))
+        half_a, half_b = keep_a + arrived_a.astype(F32), keep_b + arrived_b.astype(F32)
+        quarter_a = half_a[0] + swap(half_a[1].astype(BF16), "tm", 2).astype(F32)
+        quarter_b = half_b[0] + swap(half_b[1].astype(BF16), "tm", 1).astype(F32)
+        quarter = jnp.concatenate([quarter_a, quarter_b], 0).astype(BF16)
+        quarter, leaves = lax.optimization_barrier((quarter, leaves))
         crossing = send(leaves, [(lower, upper), (upper, lower)])
         merged = (stays.astype(F32) + crossing.astype(F32)).astype(BF16)
-    if frames == 8:
-        arrived, query_grad = lax.optimization_barrier((swap(away, "tm", 2), query_grad))
-        half = keep + arrived.astype(F32)
-        quarter = (half[0] + swap(half[1].astype(BF16), "tm", 1).astype(F32)).astype(BF16)
         own = (quarter.astype(F32) + swap(quarter, "tm", 4).astype(F32)).astype(BF16)
         own, merged = lax.optimization_barrier((own, merged))
-        other = swap(own, "tm", 1)
-        sums = (own, other, swap(jnp.stack([own, other]), "tm", 2))
+        own_a, own_b = own[: cols // 2], own[cols // 2 :]
+        other_a, other_b = swap(own_a, "tm", 2), swap(own_b, "tm", 1)
+        sums = (
+            *(own_a, other_a, swap(jnp.stack([own_a, other_a]), "tm", 1)),
+            *(own_b, other_b, swap(jnp.stack([own_b, other_b]), "tm", 2)),
+        )
     else:
-        sums = (keep[0], keep[1], away.astype(F32))
+        sums = (keep_a[0], keep_a[1], away_a.astype(F32), keep_b[0], keep_b[1], away_b.astype(F32))
     weight_grad = pl.pallas_call(
         assemble_kernel,
         out_shape=jax.ShapeDtypeStruct((cols, 4 * cols), F32),
-        in_specs=[vmem()] * 3,
+        in_specs=[vmem()] * 6,
         out_specs=vmem(),
         compiler_params=params(8),
         name="assemble",
@@ -323,8 +345,10 @@
 
     if pair_plan:
         home_k = send(merged, [(lower, source)]).astype(F32)
-        home_v = send(merged, [(upper, source + 1)]).astype(F32)
-        from_v = send((near_dv.astype(F32) + home_v).astype(BF16), back(near_pairs)).astype(F32)
+        home_v = send(merged, [(upper, source + 1)])
+        if frames == 8:
+            home_v = lax.optimization_barrier((home_v, other_a, other_b))[0]
+        from_v = send((near_dv.astype(F32) + home_v.astype(F32)).astype(BF16), back(near_pairs)).astype(F32)
         key_total = own_grad[0] + from_k.astype(F32) + home_k
         value_total = own_grad[1] + from_v
     else:

time: 112 us -> 108 us (0.964)
  waiting for transfers between devices: 60.8 us -> 49 us
  starting transfers between devices: 21.9 us -> 29 us
    ppermute x9, waiting for transfers between devices: 35.9 us -> 24.1 us  [send(): return lax.ppermute(array, 'tm', pairs)]
    ppermute x10 -> x14, starting transfers between devices: 6.72 us -> 13.8 us  [swap(): lax.ppermute(array, axis, [(i, i ^ bit) for i in range(lax.axis_size(axis...]
    ppermute x10 -> x14, waiting for transfers between devices: 24.9 us -> 24.9 us  [swap(): lax.ppermute(array, axis, [(i, i ^ bit) for i in range(lax.axis_size(axis...]
  transfers between devices with their start and end apart: 19 -> 23, of which waited for: 9 -> 11; matrix products, arithmetic and copies ran while one was open for 2% -> 2% of each run, Pallas kernels for 15% -> 17%
where the time goes in v4:
time: 108 us; the launch traced here: 107 us
  waiting for transfers between devices  49 us (45%)
  starting transfers between devices  29 us (27%)
  Pallas kernels  23.8 us (22%)
  other arithmetic  3.98 us (4%)
    ppermute x14, waiting for transfers between devices, swap(): lax.ppermute(array, axis, [(i, i ^ bit) for i in range(lax.axis_size(axis...  24.9 us
    ppermute x9, waiting for transfers between devices, send(): return lax.ppermute(array, 'tm', pairs)  24.1 us
    ppermute x9, starting transfers between devices, send(): return lax.ppermute(array, 'tm', pairs)  15.2 us
    ppermute x14, starting transfers between devices, swap(): lax.ppermute(array, axis, [(i, i ^ bit) for i in range(lax.axis_size(axis...  13.8 us
    pallas_call x1, Pallas kernels, local(): pl.pallas_call(functools.partial(backward_kernel, count, far_frames[0] if...  8.44 us
    pallas_call x1, Pallas kernels, local(): pl.pallas_call(functools.partial(far_kernel, count), grid=(heads,), out_s...  5.8 us
    pallas_call x1, Pallas kernels, local(): pl.pallas_call(near_kernel, grid=(heads,), out_shape=(part_shape, stat_sh...  5.73 us
  transfers between devices with their start and end apart: 23, of which 11 were waited for; matrix products, arithmetic and copies ran while one was open for 2% of the time, Pallas kernels for 17%

profile of v4, /device:TPU:12, one launch (start us, length us, event | category | flops | bytes accessed | tf_op | source)
XLA Modules:
  0.0 107.1 jit_solution(2173823574197520437)
XLA Ops:
  0.7 1.3 %pad_maximum_fusion = bf16[2,512,384]{2,1,0:T(8,128)(2,1)S(1)} fusion(bf16[1,512,384]{2,1,0:T(8,128)(2,1)} %bitcast.45, bf16[1,512,384]{2,1,0:T(8,128)(2,1)} %bitcast.44), kind=kLoop, calls=%fused_computation.5 | loop fusion | flops 393216 | bytes 1572864 | tf_op jit(solution)/shard_map/stack | solution.py:226
  2.0 3.4 %collective-permute-start = (bf16[2,512,384]{2,1,0:T(8,128)(2,1)S(1)}, bf16[2,512,384]{2,1,0:T(8,128)(2,1)S(1)}, u32[]{:S(2)}, u32[]{:S(2)}) collective-permute-start(bf16[2,512,384]{2,1,0:T(8,128)(2,1)S(1)} %pad_maximum_fusion), channel_id=1, source_target_pairs={{0,4},{8,12},{12,16},{16,20},{24,28},{1,5},{9,13},{13,17},{17,21},... | collective-permute-start | bytes 2359304 | tf_op jit(solution)/shard_map/ppermute | solution.py:221
  5.5 0.7 collective-permute-start.6
  6.2 0.7 collective-permute-start.1
  6.9 0.7 collective-permute-start.2
  7.6 0.9 collective-permute-start.5
  8.5 14.7 %collective-permute-done.prev = bf16[2,512,384]{2,1,0:T(8,128)(2,1)S(1)} collective-permute-done((bf16[2,512,384]{2,1,0:T(8,128)(2,1)S(1)}, bf16[2,512,384]{2,1,0:T(8,128)(2,1)S(1)}, u32[]{:S(2)}, u32[]{:S(2)}) %collective-permute-start) | collective-permute-done | bytes 786464 | tf_op jit(solution)/shard_map/ppermute | solution.py:221
  23.3 3.6 %collective-permute-start.3 = (bf16[512,384]{1,0:T(8,128)(2,1)S(1)}, bf16[512,384]{1,0:T(8,128)(2,1)S(1)}, u32[]{:S(2)}, u32[]{:S(2)}) collective-permute-start(bf16[512,384]{1,0:T(8,128)(2,1)S(1)} %slice_bitcast_fusion.1), channel_id=1, source_target_pairs={{12,20},{13,21},{14,22},{15,23}} | collective-permute-start | bytes 1179656 | tf_op jit(solution)/shard_map/ppermute | solution.py:221
  27.0 1.1 %cotangent.1.rest_5_.rest_3_ = bf16[512,384]{1,0:T(8,128)(2,1)S(1)} custom-call(bf16[512,384]{1,0:T(8,128)(2,1)S(1)} %copy-done.4, bf16[512,384]{1,0:T(8,128)(2,1)S(1)} %collective-permute-done.4.second.rest_7_, bf16[512,384]{1,0:T(8,128)(2,1)S(1)} %collective-permute-done.5.third.rest_8_, bf16[512,384]{1,0:T(8,128)(2,1)S(1)} %collective-permute-done.6.fourth.rest_9_, ...), custom_call_target="tpu_custom_call" | custom-call | tf_op jit(solution)/shard_map/cotangent/pallas_call | solution.py:249
  28.1 5.7 %near.1 = (f32[3,128,512]{2,1,0:T(8,128)S(1)}, f32[3,8,512]{2,1,0:T(8,128)S(1)}) custom-call(s32[8]{0:T(128)S(1)} %copy-done.5, bf16[512,384]{1,0:T(8,128)(2,1)S(1)} %copy-done.3, bf16[512,384]{1,0:T(8,128)(2,1)S(1)} %copy-done, bf16[512,384]{1,0:T(8,128)(2,1)S(1)} %copy-done.1, bf16[2,512,384]{2,1,0:T(8,128)(2,1)S(1)} %collective-permute-done.prev), custom_call_target="tpu_custom_call" | custom-call | tf_op jit(solution)/shard_map/near/pallas_call | solution.py:270
  33.9 2.0 %collective-permute-done.3.rest_2_ = bf16[512,384]{1,0:T(8,128)(2,1)S(1)} collective-permute-done((bf16[512,384]{1,0:T(8,128)(2,1)S(1)}, bf16[512,384]{1,0:T(8,128)(2,1)S(1)}, u32[]{:S(2)}, u32[]{:S(2)}) %collective-permute-start.3) | collective-permute-done | bytes 393248 | tf_op jit(solution)/shard_map/ppermute | solution.py:221
  35.9 5.8 %far.1 = (bf16[512,384]{1,0:T(8,128)(2,1)S(1)}, f32[3,8,512]{2,1,0:T(8,128)S(1)}, f32[2,384,384]{2,1,0:T(8,128)S(1)}, bf16[2,384,384]{2,1,0:T(8,128)(2,1)S(1)}) custom-call(s32[8]{0:T(128)S(1)} %copy-done.5, bf16[512,384]{1,0:T(8,128)(2,1)S(1)} %copy-done.3, bf16[512,384]{1,0:T(8,128)(2,1)S(1)} %copy-done, bf16[512,384]{1,0:T(8,128)(2,1)S(1)} %copy-done.1, ...), custom_call_target="tpu_custom_call" | custom-call | tf_op jit(solution)/shard_map/far/pallas_call | solution.py:282
  41.7 0.1 fusion.12
  41.8 0.1 collective-permute-start.10
  41.9 0.6 collective-permute-start.9
  42.5 1.1 %output.1 = (f32[2,512,384]{2,1,0:T(8,128)S(1)}, bf16[2,512,384]{2,1,0:T(8,128)(2,1)S(1)}) custom-call(bf16[512,384]{1,0:T(8,128)(2,1)S(1)} %get-tuple-element.29.attended, bf16[384,1536]{1,0:T(8,128)(2,1)S(1)} %copy-done.2), custom_call_target="tpu_custom_call" | custom-call | tf_op jit(solution)/shard_map/output/pallas_call | solution.py:372
  43.7 0.1 collective-permute-start.7
  43.7 8.4 %backward.1 = (bf16[512,384]{1,0:T(8,128)(2,1)}, f32[2,512,384]{2,1,0:T(8,128)S(1)}, bf16[512,384]{1,0:T(8,128)(2,1)S(1)}, bf16[512,384]{1,0:T(8,128)(2,1)S(1)},...) custom-call(s32[8]{0:T(128)S(1)} %copy-done.5, bf16[512,384]{1,0:T(8,128)(2,1)S(1)} %copy-done.3, ...), custom_call_target="tpu_custom_call" | custom-call | tf_op jit(solution)/shard_map/backward/pallas_call | solution.py:298
  52.2 0.1 convert_add_fusion.2
  52.3 1.5 %collective-permute-start.13 = (bf16[192,384]{1,0:T(8,128)(2,1)S(1)}, bf16[192,384]{1,0:T(8,128)(2,1)S(1)}, u32[]{:S(2)}, u32[]{:S(2)}) collective-permute-start(bf16[192,384]{1,0:T(8,128)(2,1)S(1)} %fusion.11), channel_id=1, source_target_pairs={{0,4},{4,0},{8,12},{12,8},{16,20},{20,16},{24,28},{28,24},{1,5},{5... | collective-permute-start | bytes 442376 | tf_op jit(solution)/shard_map/ppermute | solution.py:207
  53.8 2.0 %collective-permute-start.12 = (bf16[192,384]{1,0:T(8,128)(2,1)S(1)}, bf16[192,384]{1,0:T(8,128)(2,1)S(1)}, u32[]{:S(2)}, u32[]{:S(2)}) collective-permute-start(bf16[192,384]{1,0:T(8,128)(2,1)S(1)} %fusion.10), channel_id=1, source_target_pairs={{0,8},{4,12},{8,0},{12,4},{16,24},{20,28},{24,16},{28,20},{1,9},{5... | collective-permute-start | bytes 442376 | tf_op jit(solution)/shard_map/ppermute | solution.py:207
  55.9 2.7 %collective-permute-done.13 = bf16[192,384]{1,0:T(8,128)(2,1)S(1)} collective-permute-done((bf16[192,384]{1,0:T(8,128)(2,1)S(1)}, bf16[192,384]{1,0:T(8,128)(2,1)S(1)}, u32[]{:S(2)}, u32[]{:S(2)}) %collective-permute-start.13) | collective-permute-done | bytes 147488 | tf_op jit(solution)/shard_map/ppermute | solution.py:207
  58.6 1.4 %collective-permute-done.12 = bf16[192,384]{1,0:T(8,128)(2,1)S(1)} collective-permute-done((bf16[192,384]{1,0:T(8,128)(2,1)S(1)}, bf16[192,384]{1,0:T(8,128)(2,1)S(1)}, u32[]{:S(2)}, u32[]{:S(2)}) %collective-permute-start.12) | collective-permute-done | bytes 147488 | tf_op jit(solution)/shard_map/ppermute | solution.py:207
  60.1 3.7 %collective-permute-start.14 = (bf16[384,384]{1,0:T(8,128)(2,1)S(1)}, bf16[384,384]{1,0:T(8,128)(2,1)S(1)}, u32[]{:S(2)}, u32[]{:S(2)}) collective-permute-start(bf16[384,384]{1,0:T(8,128)(2,1)S(1)} %pad_maximum_fusion.1), channel_id=1, source_target_pairs={{0,16},{4,20},{8,24},{12,28},{16,0},{20,4},{24,8},{28,12},{1,17},{... | collective-permute-start | bytes 884744 | tf_op jit(solution)/shard_map/ppermute | solution.py:207
  63.9 2.2 %collective-permute-start.11 = (bf16[512,384]{1,0:T(8,128)(2,1)S(1)}, bf16[512,384]{1,0:T(8,128)(2,1)S(1)}, u32[]{:S(2)}, u32[]{:S(2)}) collective-permute-start(bf16[512,384]{1,0:T(8,128)(2,1)S(1)} %get-tuple-element.37), channel_id=1, source_target_pairs={{4,0},{12,8},{16,12},{20,16},{28,24},{5,1},{13,9},{17,13},{21,17},... | collective-permute-start | bytes 1179656 | tf_op jit(solution)/shard_map/ppermute | solution.py:221
  66.1 0.7 collective-permute-start.15
  66.8 9.2 %collective-permute-done.14 = bf16[384,384]{1,0:T(8,128)(2,1)S(1)} collective-permute-done((bf16[384,384]{1,0:T(8,128)(2,1)S(1)}, bf16[384,384]{1,0:T(8,128)(2,1)S(1)}, u32[]{:S(2)}, u32[]{:S(2)}) %collective-permute-start.14) | collective-permute-done | bytes 294944 | tf_op jit(solution)/shard_map/ppermute | solution.py:207
  75.9 0.1 add_convert_fusion.2
  76.0 0.1 convert_add_fusion
  76.2 0.1 add_convert_fusion.1
  76.3 1.3 %collective-permute-start.17 = (bf16[512,384]{1,0:T(8,128)(2,1)S(1)}, bf16[512,384]{1,0:T(8,128)(2,1)S(1)}, u32[]{:S(2)}, u32[]{:S(2)}) collective-permute-start(bf16[512,384]{1,0:T(8,128)(2,1)S(1)} %add_convert_fusion.1), channel_id=1, source_target_pairs={{20,12},{21,13},{22,14},{23,15}} | collective-permute-start | bytes 1179656 | tf_op jit(solution)/shard_map/ppermute | solution.py:221
  77.6 0.1 slice_bitcast_fusion.4
  77.6 0.1 collective-permute-start.19
  77.7 2.4 %collective-permute-start.18 = (bf16[192,384]{1,0:T(8,128)(2,1)S(1)}, bf16[192,384]{1,0:T(8,128)(2,1)S(1)}, u32[]{:S(2)}, u32[]{:S(2)}) collective-permute-start(bf16[192,384]{1,0:T(8,128)(2,1)S(1)} %get-tuple-element.58.refs_0_), channel_id=1, source_target_pairs={{0,8},{4,12},{8,0},{12,4},{16,24},{20,28},{24,16},{28,20},{1,9},{5... | collective-permute-start | bytes 442376 | tf_op jit(solution)/shard_map/ppermute | solution.py:207
  80.2 1.5 %collective-permute-start.8 = (bf16[512,384]{1,0:T(8,128)(2,1)S(1)}, bf16[512,384]{1,0:T(8,128)(2,1)S(1)}, u32[]{:S(2)}, u32[]{:S(2)}) collective-permute-start(bf16[512,384]{1,0:T(8,128)(2,1)S(1)} %fusion.5), channel_id=1, source_target_pairs={{0,2},{1,3},{2,0},{3,1},{4,6},{5,7},{6,4},{7,5},{8,10},{9,11},{10,... | collective-permute-start | bytes 1179656 | tf_op jit(solution)/shard_map/ppermute | solution.py:207
  81.7 1.9 %collective-permute-done.18.refs_1_ = bf16[192,384]{1,0:T(8,128)(2,1)S(1)} collective-permute-done((bf16[192,384]{1,0:T(8,128)(2,1)S(1)}, bf16[192,384]{1,0:T(8,128)(2,1)S(1)}, u32[]{:S(2)}, u32[]{:S(2)}) %collective-permute-start.18) | collective-permute-done | bytes 147488 | tf_op jit(solution)/shard_map/ppermute | solution.py:207
  83.6 0.7 collective-permute-start.16
  84.3 3.3 %collective-permute-done.19.refs_4_ = bf16[192,384]{1,0:T(8,128)(2,1)S(1)} collective-permute-done((bf16[192,384]{1,0:T(8,128)(2,1)S(1)}, bf16[192,384]{1,0:T(8,128)(2,1)S(1)}, u32[]{:S(2)}, u32[]{:S(2)}) %collective-permute-start.19) | collective-permute-done | bytes 147488 | tf_op jit(solution)/shard_map/ppermute | solution.py:207
  87.6 3.1 %collective-permute-done.17 = bf16[512,384]{1,0:T(8,128)(2,1)S(1)} collective-permute-done((bf16[512,384]{1,0:T(8,128)(2,1)S(1)}, bf16[512,384]{1,0:T(8,128)(2,1)S(1)}, u32[]{:S(2)}, u32[]{:S(2)}) %collective-permute-start.17) | collective-permute-done | bytes 393248 | tf_op jit(solution)/shard_map/ppermute | solution.py:221
  90.7 0.1 add_convert_fusion
  90.8 1.9 %collective-permute-start.20 = (bf16[512,384]{1,0:T(8,128)(2,1)S(1)}, bf16[512,384]{1,0:T(8,128)(2,1)S(1)}, u32[]{:S(2)}, u32[]{:S(2)}) collective-permute-start(bf16[512,384]{1,0:T(8,128)(2,1)S(1)} %add_convert_fusion), channel_id=1, source_target_pairs={{4,0},{12,8},{16,12},{20,16},{28,24},{5,1},{13,9},{17,13},{21,17},... | collective-permute-start | bytes 1179656 | tf_op jit(solution)/shard_map/ppermute | solution.py:221
  92.8 0.1 collective-permute-start.22
  92.9 0.8 fusion.1
  93.7 5.6 %collective-permute-done.21.refs_2_ = bf16[2,192,384]{2,1,0:T(8,128)(2,1)S(1)} collective-permute-done((bf16[2,192,384]{2,1,0:T(8,128)(2,1)S(1)}, bf16[2,192,384]{2,1,0:T(8,128)(2,1)S(1)}, u32[]{:S(2)}, u32[]{:S(2)}) %collective-permute-start.21) | collective-permute-done | bytes 294944 | tf_op jit(solution)/shard_map/ppermute | solution.py:207
  99.3 0.8 collective-permute-done.22.refs_5_
  100.1 1.6 %assemble.1 = f32[384,1536]{1,0:T(8,128)} custom-call(bf16[192,384]{1,0:T(8,128)(2,1)S(1)} %get-tuple-element.58.refs_0_, bf16[192,384]{1,0:T(8,128)(2,1)S(1)} %collective-permute-done.18.refs_1_, bf16[2,192,384]{2,1,0:T(8,128)(2,1)S(1)} %collective-permute-done.21.refs_2_, bf16[192,384]{1,0:T(8,128)(2,1)S(1)} %get-tuple-element.57.refs_3_, ...), custom_call_target="tpu_custom_call" | custom-call | tf_op jit(solution)/shard_map/assemble/pallas_call | solution.py:335
  101.7 4.2 %collective-permute-done.20 = bf16[512,384]{1,0:T(8,128)(2,1)S(1)} collective-permute-done((bf16[512,384]{1,0:T(8,128)(2,1)S(1)}, bf16[512,384]{1,0:T(8,128)(2,1)S(1)}, u32[]{:S(2)}, u32[]{:S(2)}) %collective-permute-start.20) | collective-permute-done | bytes 393248 | tf_op jit(solution)/shard_map/ppermute | solution.py:221
  105.9 1.1 %fusion.2 = (bf16[512,384]{1,0:T(8,128)(2,1)}, bf16[512,384]{1,0:T(8,128)(2,1)}) fusion(bf16[512,384]{1,0:T(8,128)(2,1)S(1)} %collective-permute-done.20, f32[2,512,384]{2,1,0:T(8,128)S(1)} %get-tuple-element.36, bf16[512,384]{1,0:T(8,128)(2,1)S(1)} %collective-permute-done.16, bf16[512,384]{1,0:T(8,128)(2,1)S(1)} %collective-permute-done.11), kind=kLoop, calls=%fused_computation.7 | loop fusion | flops 1572864 | bytes 3538944 | tf_op jit(solution)/shard_map/convert_element_type | solution.py:370
  (35 shorter events, 0.4 us)
Async XLA Ops:
  0.6 6.2 %copy-start = (bf16[512,384]{1,0:T(8,128)(2,1)S(1)}, bf16[512,384]{1,0:T(8,128)(2,1)}, u32[]{:S(2)}) copy-start(bf16[512,384]{1,0:T(8,128)(2,1)} %k.5) | copy-start | bytes 1179652
  0.6 4.8 %copy-start.4 = (bf16[512,384]{1,0:T(8,128)(2,1)S(1)}, bf16[512,384]{1,0:T(8,128)(2,1)}, u32[]{:S(2)}) copy-start(bf16[512,384]{1,0:T(8,128)(2,1)} %rest_6_.1) | copy-start | bytes 1179652
  0.7 26.3 %copy-start.2 = (bf16[384,1536]{1,0:T(8,128)(2,1)S(1)}, bf16[384,1536]{1,0:T(8,128)(2,1)}, u32[]{:S(2)}) copy-start(bf16[384,1536]{1,0:T(8,128)(2,1)} %weight.3) | copy-start | bytes 3538948
  2.0 21.2 %collective-permute-start = (bf16[2,512,384]{2,1,0:T(8,128)(2,1)S(1)}, bf16[2,512,384]{2,1,0:T(8,128)(2,1)S(1)}, u32[]{:S(2)}, u32[]{:S(2)}) collective-permute-start(bf16[2,512,384]{2,1,0:T(8,128)(2,1)S(1)} %pad_maximum_fusion), channel_id=1, source_target_pairs={{0,4},{8,12},{12,16},{16,20},{24,28},{1,5},{9,13},{13,17},{17,21},... | collective-permute-start | bytes 2359304 | tf_op jit(solution)/shard_map/ppermute | solution.py:221
  5.5 17.8 %collective-permute-start.6 = (bf16[512,384]{1,0:T(8,128)(2,1)S(1)}, bf16[512,384]{1,0:T(8,128)(2,1)S(1)}, u32[]{:S(2)}, u32[]{:S(2)}) collective-permute-start(bf16[512,384]{1,0:T(8,128)(2,1)S(1)} %copy-done.4), channel_id=1, source_target_pairs={{0,3},{1,2},{2,1},{3,0},{4,7},{5,6},{6,5},{7,4},{8,11},{9,10},{10,... | collective-permute-start | bytes 1179656 | tf_op jit(solution)/shard_map/ppermute | solution.py:207
  6.2 27.7 %collective-permute-start.1 = (bf16[2,512,384]{2,1,0:T(8,128)(2,1)S(1)}, bf16[2,512,384]{2,1,0:T(8,128)(2,1)S(1)}, u32[]{:S(2)}, u32[]{:S(2)}) collective-permute-start(bf16[2,512,384]{2,1,0:T(8,128)(2,1)S(1)} %pad_maximum_fusion), channel_id=1, source_target_pairs={{8,16},{9,17},{10,18},{11,19}} | collective-permute-start | bytes 2359304 | tf_op jit(solution)/shard_map/ppermute | solution.py:221
  6.9 27.0 %collective-permute-start.2 = (bf16[512,384]{1,0:T(8,128)(2,1)S(1)}, bf16[512,384]{1,0:T(8,128)(2,1)S(1)}, u32[]{:S(2)}, u32[]{:S(2)}) collective-permute-start(bf16[512,384]{1,0:T(8,128)(2,1)S(1)} %copy-done), channel_id=1, source_target_pairs={{8,20},{9,21},{10,22},{11,23}} | collective-permute-start | bytes 1179656 | tf_op jit(solution)/shard_map/ppermute | solution.py:221
  7.6 19.3 %collective-permute-start.5 = (bf16[512,384]{1,0:T(8,128)(2,1)S(1)}, bf16[512,384]{1,0:T(8,128)(2,1)S(1)}, u32[]{:S(2)}, u32[]{:S(2)}) collective-permute-start(bf16[512,384]{1,0:T(8,128)(2,1)S(1)} %copy-done.4), channel_id=1, source_target_pairs={{0,2},{1,3},{2,0},{3,1},{4,6},{5,7},{6,4},{7,5},{8,10},{9,11},{10,... | collective-permute-start | bytes 1179656 | tf_op jit(solution)/shard_map/ppermute | solution.py:207
  23.2 3.8 %collective-permute-start.4 = (bf16[512,384]{1,0:T(8,128)(2,1)S(1)}, bf16[512,384]{1,0:T(8,128)(2,1)S(1)}, u32[]{:S(2)}, u32[]{:S(2)}) collective-permute-start(bf16[512,384]{1,0:T(8,128)(2,1)S(1)} %copy-done.4), channel_id=1, source_target_pairs={{0,1},{1,0},{2,3},{3,2},{4,5},{5,4},{6,7},{7,6},{8,9},{9,8},{10,11... | collective-permute-start | bytes 1179656 | tf_op jit(solution)/shard_map/ppermute | solution.py:207
  23.2 4.9 %copy-start.1 = (bf16[512,384]{1,0:T(8,128)(2,1)S(1)}, bf16[512,384]{1,0:T(8,128)(2,1)}, u32[]{:S(2)}) copy-start(bf16[512,384]{1,0:T(8,128)(2,1)} %v.5) | copy-start | bytes 1179652
  23.2 4.9 %copy-start.3 = (bf16[512,384]{1,0:T(8,128)(2,1)S(1)}, bf16[512,384]{1,0:T(8,128)(2,1)}, u32[]{:S(2)}) copy-start(bf16[512,384]{1,0:T(8,128)(2,1)} %q.5) | copy-start | bytes 1179652
  23.3 4.9 %copy-start.5 = (s32[8]{0:T(128)S(1)}, s32[8]{0:T(128)}, u32[]{:S(2)}) copy-start(s32[8]{0:T(128)} %anchor.5) | copy-start | bytes 100
  23.3 12.6 %collective-permute-start.3 = (bf16[512,384]{1,0:T(8,128)(2,1)S(1)}, bf16[512,384]{1,0:T(8,128)(2,1)S(1)}, u32[]{:S(2)}, u32[]{:S(2)}) collective-permute-start(bf16[512,384]{1,0:T(8,128)(2,1)S(1)} %slice_bitcast_fusion.1), channel_id=1, source_target_pairs={{12,20},{13,21},{14,22},{15,23}} | collective-permute-start | bytes 1179656 | tf_op jit(solution)/shard_map/ppermute | solution.py:221
  41.8 10.4 %collective-permute-start.10 = (bf16[2,192,384]{2,1,0:T(8,128)(2,1)S(1)}, bf16[2,192,384]{2,1,0:T(8,128)(2,1)S(1)}, u32[]{:S(2)}, u32[]{:S(2)}) collective-permute-start(bf16[2,192,384]{2,1,0:T(8,128)(2,1)S(1)} %get-tuple-element.53), channel_id=1, source_target_pairs={{0,8},{4,12},{8,0},{12,4},{16,24},{20,28},{24,16},{28,20},{1,9},{5... | collective-permute-start | bytes 884744 | tf_op jit(solution)/shard_map/ppermute | solution.py:207
  41.9 10.3 %collective-permute-start.9 = (bf16[2,192,384]{2,1,0:T(8,128)(2,1)S(1)}, bf16[2,192,384]{2,1,0:T(8,128)(2,1)S(1)}, u32[]{:S(2)}, u32[]{:S(2)}) collective-permute-start(bf16[2,192,384]{2,1,0:T(8,128)(2,1)S(1)} %get-tuple-element.54), channel_id=1, source_target_pairs={{0,4},{4,0},{8,12},{12,8},{16,20},{20,16},{24,28},{28,24},{1,5},{5... | collective-permute-start | bytes 884744 | tf_op jit(solution)/shard_map/ppermute | solution.py:207
  43.7 32.4 %collective-permute-start.7 = (bf16[2,512,384]{2,1,0:T(8,128)(2,1)S(1)}, bf16[2,512,384]{2,1,0:T(8,128)(2,1)S(1)}, u32[]{:S(2)}, u32[]{:S(2)}) collective-permute-start(bf16[2,512,384]{2,1,0:T(8,128)(2,1)S(1)} %get-tuple-element.31), channel_id=1, source_target_pairs={{0,1},{1,0},{2,3},{3,2},{4,5},{5,4},{6,7},{7,6},{8,9},{9,8},{10,11... | collective-permute-start | bytes 2359304 | tf_op jit(solution)/shard_map/ppermute | solution.py:207
  52.3 6.3 %collective-permute-start.13 = (bf16[192,384]{1,0:T(8,128)(2,1)S(1)}, bf16[192,384]{1,0:T(8,128)(2,1)S(1)}, u32[]{:S(2)}, u32[]{:S(2)}) collective-permute-start(bf16[192,384]{1,0:T(8,128)(2,1)S(1)} %fusion.11), channel_id=1, source_target_pairs={{0,4},{4,0},{8,12},{12,8},{16,20},{20,16},{24,28},{28,24},{1,5},{5... | collective-permute-start | bytes 442376 | tf_op jit(solution)/shard_map/ppermute | solution.py:207
  53.8 6.2 %collective-permute-start.12 = (bf16[192,384]{1,0:T(8,128)(2,1)S(1)}, bf16[192,384]{1,0:T(8,128)(2,1)S(1)}, u32[]{:S(2)}, u32[]{:S(2)}) collective-permute-start(bf16[192,384]{1,0:T(8,128)(2,1)S(1)} %fusion.10), channel_id=1, source_target_pairs={{0,8},{4,12},{8,0},{12,4},{16,24},{20,28},{24,16},{28,20},{1,9},{5... | collective-permute-start | bytes 442376 | tf_op jit(solution)/shard_map/ppermute | solution.py:207
  60.1 15.8 %collective-permute-start.14 = (bf16[384,384]{1,0:T(8,128)(2,1)S(1)}, bf16[384,384]{1,0:T(8,128)(2,1)S(1)}, u32[]{:S(2)}, u32[]{:S(2)}) collective-permute-start(bf16[384,384]{1,0:T(8,128)(2,1)S(1)} %pad_maximum_fusion.1), channel_id=1, source_target_pairs={{0,16},{4,20},{8,24},{12,28},{16,0},{20,4},{24,8},{28,12},{1,17},{... | collective-permute-start | bytes 884744 | tf_op jit(solution)/shard_map/ppermute | solution.py:207
  63.9 37.8 %collective-permute-start.11 = (bf16[512,384]{1,0:T(8,128)(2,1)S(1)}, bf16[512,384]{1,0:T(8,128)(2,1)S(1)}, u32[]{:S(2)}, u32[]{:S(2)}) collective-permute-start(bf16[512,384]{1,0:T(8,128)(2,1)S(1)} %get-tuple-element.37), channel_id=1, source_target_pairs={{4,0},{12,8},{16,12},{20,16},{28,24},{5,1},{13,9},{17,13},{21,17},... | collective-permute-start | bytes 1179656 | tf_op jit(solution)/shard_map/ppermute | solution.py:221
  66.1 10.1 %collective-permute-start.15 = (bf16[512,384]{1,0:T(8,128)(2,1)S(1)}, bf16[512,384]{1,0:T(8,128)(2,1)S(1)}, u32[]{:S(2)}, u32[]{:S(2)}) collective-permute-start(bf16[512,384]{1,0:T(8,128)(2,1)S(1)} %get-tuple-element.44), channel_id=1, source_target_pairs={{16,20},{20,16},{17,21},{21,17},{18,22},{22,18},{19,23},{23,19}} | collective-permute-start | bytes 1179656 | tf_op jit(solution)/shard_map/ppermute | solution.py:221
  76.3 14.4 %collective-permute-start.17 = (bf16[512,384]{1,0:T(8,128)(2,1)S(1)}, bf16[512,384]{1,0:T(8,128)(2,1)S(1)}, u32[]{:S(2)}, u32[]{:S(2)}) collective-permute-start(bf16[512,384]{1,0:T(8,128)(2,1)S(1)} %add_convert_fusion.1), channel_id=1, source_target_pairs={{20,12},{21,13},{22,14},{23,15}} | collective-permute-start | bytes 1179656 | tf_op jit(solution)/shard_map/ppermute | solution.py:221
  77.6 9.9 %collective-permute-start.19 = (bf16[192,384]{1,0:T(8,128)(2,1)S(1)}, bf16[192,384]{1,0:T(8,128)(2,1)S(1)}, u32[]{:S(2)}, u32[]{:S(2)}) collective-permute-start(bf16[192,384]{1,0:T(8,128)(2,1)S(1)} %get-tuple-element.57.refs_3_), channel_id=1, source_target_pairs={{0,4},{4,0},{8,12},{12,8},{16,20},{20,16},{24,28},{28,24},{1,5},{5... | collective-permute-start | bytes 442376 | tf_op jit(solution)/shard_map/ppermute | solution.py:207
  77.7 5.8 %collective-permute-start.18 = (bf16[192,384]{1,0:T(8,128)(2,1)S(1)}, bf16[192,384]{1,0:T(8,128)(2,1)S(1)}, u32[]{:S(2)}, u32[]{:S(2)}) collective-permute-start(bf16[192,384]{1,0:T(8,128)(2,1)S(1)} %get-tuple-element.58.refs_0_), channel_id=1, source_target_pairs={{0,8},{4,12},{8,0},{12,4},{16,24},{20,28},{24,16},{28,20},{1,9},{5... | collective-permute-start | bytes 442376 | tf_op jit(solution)/shard_map/ppermute | solution.py:207
  80.2 12.6 %collective-permute-start.8 = (bf16[512,384]{1,0:T(8,128)(2,1)S(1)}, bf16[512,384]{1,0:T(8,128)(2,1)S(1)}, u32[]{:S(2)}, u32[]{:S(2)}) collective-permute-start(bf16[512,384]{1,0:T(8,128)(2,1)S(1)} %fusion.5), channel_id=1, source_target_pairs={{0,2},{1,3},{2,0},{3,1},{4,6},{5,7},{6,4},{7,5},{8,10},{9,11},{10,... | collective-permute-start | bytes 1179656 | tf_op jit(solution)/shard_map/ppermute | solution.py:207
  83.6 18.1 %collective-permute-start.16 = (bf16[512,384]{1,0:T(8,128)(2,1)S(1)}, bf16[512,384]{1,0:T(8,128)(2,1)S(1)}, u32[]{:S(2)}, u32[]{:S(2)}) collective-permute-start(bf16[512,384]{1,0:T(8,128)(2,1)S(1)} %add_convert_fusion.1), channel_id=1, source_target_pairs={{16,8},{17,9},{18,10},{19,11}} | collective-permute-start | bytes 1179656 | tf_op jit(solution)/shard_map/ppermute | solution.py:221
  87.6 11.7 %collective-permute-start.21 = (bf16[2,192,384]{2,1,0:T(8,128)(2,1)S(1)}, bf16[2,192,384]{2,1,0:T(8,128)(2,1)S(1)}, u32[]{:S(2)}, u32[]{:S(2)}) collective-permute-start(bf16[2,192,384]{2,1,0:T(8,128)(2,1)S(1)} %pad_maximum_fusion.2), channel_id=1, source_target_pairs={{0,4},{4,0},{8,12},{12,8},{16,20},{20,16},{24,28},{28,24},{1,5},{5... | collective-permute-start | bytes 884744 | tf_op jit(solution)/shard_map/ppermute | solution.py:207
  90.8 15.1 %collective-permute-start.20 = (bf16[512,384]{1,0:T(8,128)(2,1)S(1)}, bf16[512,384]{1,0:T(8,128)(2,1)S(1)}, u32[]{:S(2)}, u32[]{:S(2)}) collective-permute-start(bf16[512,384]{1,0:T(8,128)(2,1)S(1)} %add_convert_fusion), channel_id=1, source_target_pairs={{4,0},{12,8},{16,12},{20,16},{28,24},{5,1},{13,9},{17,13},{21,17},... | collective-permute-start | bytes 1179656 | tf_op jit(solution)/shard_map/ppermute | solution.py:221
  92.8 7.3 %collective-permute-start.22 = (bf16[2,192,384]{2,1,0:T(8,128)(2,1)S(1)}, bf16[2,192,384]{2,1,0:T(8,128)(2,1)S(1)}, u32[]{:S(2)}, u32[]{:S(2)}) collective-permute-start(bf16[2,192,384]{2,1,0:T(8,128)(2,1)S(1)} %pad_maximum_fusion.3), channel_id=1, source_target_pairs={{0,8},{4,12},{8,0},{12,4},{16,24},{20,28},{24,16},{28,20},{1,9},{5... | collective-permute-start | bytes 884744 | tf_op jit(solution)/shard_map/ppermute | solution.py:207

commit v5 on v4

--- a/solution.py
+++ b/solution.py
@@ -245,7 +245,8 @@
             step *= 2
         far = (fetched,)
 
-    columns = (output_grad, *[swap(output_grad, "head", m) for m in (1, 2, 3)])
+    across = swap(output_grad, "head", 2)
+    columns = (output_grad, swap(output_grad, "head", 1), across, swap(across, "head", 1))
     attended_grad = pl.pallas_call(
         cotangent_kernel,
         out_shape=jax.ShapeDtypeStruct((rows, cols), BF16),

time: 108 us -> 107 us (level)
    ppermute x9, waiting for transfers between devices: 24.1 us -> 15 us  [send(): return lax.ppermute(array, 'tm', pairs)]
    ppermute x14, waiting for transfers between devices: 24.9 us -> 33.3 us  [swap(): lax.ppermute(array, axis, [(i, i ^ bit) for i in range(lax.axis_size(axis...]
  transfers between devices with their start and end apart: 23 -> 23, of which waited for: 11 -> 12; matrix products, arithmetic and copies ran while one was open for 2% -> 2% of each run, Pallas kernels for 17% -> 17%
where the time goes in v5:
time: 107 us; the launch traced here: 106 us
  waiting for transfers between devices  48.3 us (45%)
  starting transfers between devices  29 us (27%)
  Pallas kernels  23.8 us (22%)
  other arithmetic  3.95 us (4%)
    ppermute x14, waiting for transfers between devices, swap(): lax.ppermute(array, axis, [(i, i ^ bit) for i in range(lax.axis_size(axis...  33.3 us
    ppermute x9, starting transfers between devices, send(): return lax.ppermute(array, 'tm', pairs)  15.2 us
    ppermute x9, waiting for transfers between devices, send(): return lax.ppermute(array, 'tm', pairs)  15 us
    ppermute x14, starting transfers between devices, swap(): lax.ppermute(array, axis, [(i, i ^ bit) for i in range(lax.axis_size(axis...  13.8 us
    pallas_call x1, Pallas kernels, local(): pl.pallas_call(functools.partial(backward_kernel, count, far_frames[0] if...  8.44 us
    pallas_call x1, Pallas kernels, local(): pl.pallas_call(functools.partial(far_kernel, count), grid=(heads,), out_s...  5.8 us
    pallas_call x1, Pallas kernels, local(): pl.pallas_call(near_kernel, grid=(heads,), out_shape=(part_shape, stat_sh...  5.73 us
  transfers between devices with their start and end apart: 23, of which 12 were waited for; matrix products, arithmetic and copies ran while one was open for 2% of the time, Pallas kernels for 17%

profile of v5, /device:TPU:12, one launch (start us, length us, event | category | flops | bytes accessed | tf_op | source)
XLA Modules:
  0.0 106.3 jit_solution(1645255424459334755)
XLA Ops:
  0.7 1.3 %pad_maximum_fusion = bf16[2,512,384]{2,1,0:T(8,128)(2,1)S(1)} fusion(bf16[1,512,384]{2,1,0:T(8,128)(2,1)} %bitcast.45, bf16[1,512,384]{2,1,0:T(8,128)(2,1)} %bitcast.44), kind=kLoop, calls=%fused_computation.5 | loop fusion | flops 393216 | bytes 1572864 | tf_op jit(solution)/shard_map/stack | solution.py:226
  2.0 3.6 %collective-permute-start = (bf16[2,512,384]{2,1,0:T(8,128)(2,1)S(1)}, bf16[2,512,384]{2,1,0:T(8,128)(2,1)S(1)}, u32[]{:S(2)}, u32[]{:S(2)}) collective-permute-start(bf16[2,512,384]{2,1,0:T(8,128)(2,1)S(1)} %pad_maximum_fusion), channel_id=1, source_target_pairs={{0,4},{8,12},{12,16},{16,20},{24,28},{1,5},{9,13},{13,17},{17,21},... | collective-permute-start | bytes 2359304 | tf_op jit(solution)/shard_map/ppermute | solution.py:221
  5.6 1.6 %collective-permute-start.5 = (bf16[512,384]{1,0:T(8,128)(2,1)S(1)}, bf16[512,384]{1,0:T(8,128)(2,1)S(1)}, u32[]{:S(2)}, u32[]{:S(2)}) collective-permute-start(bf16[512,384]{1,0:T(8,128)(2,1)S(1)} %copy-done.4), channel_id=1, source_target_pairs={{0,2},{1,3},{2,0},{3,1},{4,6},{5,7},{6,4},{7,5},{8,10},{9,11},{10,... | collective-permute-start | bytes 1179656 | tf_op jit(solution)/shard_map/ppermute | solution.py:207
  7.1 0.7 collective-permute-start.1
  7.9 0.1 collective-permute-start.4
  7.9 0.7 collective-permute-start.2
  8.6 7.6 %collective-permute-done.5.third.rest_8_ = bf16[512,384]{1,0:T(8,128)(2,1)S(1)} collective-permute-done((bf16[512,384]{1,0:T(8,128)(2,1)S(1)}, bf16[512,384]{1,0:T(8,128)(2,1)S(1)}, u32[]{:S(2)}, u32[]{:S(2)}) %collective-permute-start.5) | collective-permute-done | bytes 393248 | tf_op jit(solution)/shard_map/ppermute | solution.py:207
  16.2 7.1 %collective-permute-done.prev = bf16[2,512,384]{2,1,0:T(8,128)(2,1)S(1)} collective-permute-done((bf16[2,512,384]{2,1,0:T(8,128)(2,1)S(1)}, bf16[2,512,384]{2,1,0:T(8,128)(2,1)S(1)}, u32[]{:S(2)}, u32[]{:S(2)}) %collective-permute-start) | collective-permute-done | bytes 786464 | tf_op jit(solution)/shard_map/ppermute | solution.py:221
  23.4 3.5 %collective-permute-start.3 = (bf16[512,384]{1,0:T(8,128)(2,1)S(1)}, bf16[512,384]{1,0:T(8,128)(2,1)S(1)}, u32[]{:S(2)}, u32[]{:S(2)}) collective-permute-start(bf16[512,384]{1,0:T(8,128)(2,1)S(1)} %slice_bitcast_fusion.1), channel_id=1, source_target_pairs={{12,20},{13,21},{14,22},{15,23}} | collective-permute-start | bytes 1179656 | tf_op jit(solution)/shard_map/ppermute | solution.py:221
  26.9 5.7 %near.1 = (f32[3,128,512]{2,1,0:T(8,128)S(1)}, f32[3,8,512]{2,1,0:T(8,128)S(1)}) custom-call(s32[8]{0:T(128)S(1)} %copy-done.5, bf16[512,384]{1,0:T(8,128)(2,1)S(1)} %copy-done.3, bf16[512,384]{1,0:T(8,128)(2,1)S(1)} %copy-done, bf16[512,384]{1,0:T(8,128)(2,1)S(1)} %copy-done.1, bf16[2,512,384]{2,1,0:T(8,128)(2,1)S(1)} %collective-permute-done.prev), custom_call_target="tpu_custom_call" | custom-call | tf_op jit(solution)/shard_map/near/pallas_call | solution.py:271
  32.7 1.1 %cotangent.1.rest_5_.rest_3_ = bf16[512,384]{1,0:T(8,128)(2,1)S(1)} custom-call(bf16[512,384]{1,0:T(8,128)(2,1)S(1)} %copy-done.4, bf16[512,384]{1,0:T(8,128)(2,1)S(1)} %collective-permute-done.4.second.rest_7_, bf16[512,384]{1,0:T(8,128)(2,1)S(1)} %collective-permute-done.5.third.rest_8_, bf16[512,384]{1,0:T(8,128)(2,1)S(1)} %collective-permute-done.6.fourth.rest_9_, ...), custom_call_target="tpu_custom_call" | custom-call | tf_op jit(solution)/shard_map/cotangent/pallas_call | solution.py:250
  33.8 0.5 collective-permute-done.3.rest_2_
  34.3 5.8 %far.1 = (bf16[512,384]{1,0:T(8,128)(2,1)S(1)}, f32[3,8,512]{2,1,0:T(8,128)S(1)}, f32[2,384,384]{2,1,0:T(8,128)S(1)}, bf16[2,384,384]{2,1,0:T(8,128)(2,1)S(1)}) custom-call(s32[8]{0:T(128)S(1)} %copy-done.5, bf16[512,384]{1,0:T(8,128)(2,1)S(1)} %copy-done.3, bf16[512,384]{1,0:T(8,128)(2,1)S(1)} %copy-done, bf16[512,384]{1,0:T(8,128)(2,1)S(1)} %copy-done.1, ...), custom_call_target="tpu_custom_call" | custom-call | tf_op jit(solution)/shard_map/far/pallas_call | solution.py:283
  40.1 0.1 fusion.12
  40.2 0.1 collective-permute-start.10
  40.3 1.5 %collective-permute-start.9 = (bf16[2,192,384]{2,1,0:T(8,128)(2,1)S(1)}, bf16[2,192,384]{2,1,0:T(8,128)(2,1)S(1)}, u32[]{:S(2)}, u32[]{:S(2)}) collective-permute-start(bf16[2,192,384]{2,1,0:T(8,128)(2,1)S(1)} %get-tuple-element.54), channel_id=1, source_target_pairs={{0,4},{4,0},{8,12},{12,8},{16,20},{20,16},{24,28},{28,24},{1,5},{5... | collective-permute-start | bytes 884744 | tf_op jit(solution)/shard_map/ppermute | solution.py:207
  41.8 1.1 %output.1 = (f32[2,512,384]{2,1,0:T(8,128)S(1)}, bf16[2,512,384]{2,1,0:T(8,128)(2,1)S(1)}) custom-call(bf16[512,384]{1,0:T(8,128)(2,1)S(1)} %get-tuple-element.29.attended, bf16[384,1536]{1,0:T(8,128)(2,1)S(1)} %copy-done.2), custom_call_target="tpu_custom_call" | custom-call | tf_op jit(solution)/shard_map/output/pallas_call | solution.py:373
  42.9 0.1 collective-permute-start.7
  43.0 8.4 %backward.1 = (bf16[512,384]{1,0:T(8,128)(2,1)}, f32[2,512,384]{2,1,0:T(8,128)S(1)}, bf16[512,384]{1,0:T(8,128)(2,1)S(1)}, bf16[512,384]{1,0:T(8,128)(2,1)S(1)},...) custom-call(s32[8]{0:T(128)S(1)} %copy-done.5, bf16[512,384]{1,0:T(8,128)(2,1)S(1)} %copy-done.3, ...), custom_call_target="tpu_custom_call" | custom-call | tf_op jit(solution)/shard_map/backward/pallas_call | solution.py:299
  51.5 0.1 convert_add_fusion.2
  51.6 0.6 collective-permute-start.13
  52.3 2.0 %collective-permute-start.12 = (bf16[192,384]{1,0:T(8,128)(2,1)S(1)}, bf16[192,384]{1,0:T(8,128)(2,1)S(1)}, u32[]{:S(2)}, u32[]{:S(2)}) collective-permute-start(bf16[192,384]{1,0:T(8,128)(2,1)S(1)} %fusion.10), channel_id=1, source_target_pairs={{0,8},{4,12},{8,0},{12,4},{16,24},{20,28},{24,16},{28,20},{1,9},{5... | collective-permute-start | bytes 442376 | tf_op jit(solution)/shard_map/ppermute | solution.py:207
  54.3 3.6 %collective-permute-done.13 = bf16[192,384]{1,0:T(8,128)(2,1)S(1)} collective-permute-done((bf16[192,384]{1,0:T(8,128)(2,1)S(1)}, bf16[192,384]{1,0:T(8,128)(2,1)S(1)}, u32[]{:S(2)}, u32[]{:S(2)}) %collective-permute-start.13) | collective-permute-done | bytes 147488 | tf_op jit(solution)/shard_map/ppermute | solution.py:207
  57.9 0.6 collective-permute-done.12
  58.5 4.6 %collective-permute-start.14 = (bf16[384,384]{1,0:T(8,128)(2,1)S(1)}, bf16[384,384]{1,0:T(8,128)(2,1)S(1)}, u32[]{:S(2)}, u32[]{:S(2)}) collective-permute-start(bf16[384,384]{1,0:T(8,128)(2,1)S(1)} %pad_maximum_fusion.1), channel_id=1, source_target_pairs={{0,16},{4,20},{8,24},{12,28},{16,0},{20,4},{24,8},{28,12},{1,17},{... | collective-permute-start | bytes 884744 | tf_op jit(solution)/shard_map/ppermute | solution.py:207
  63.2 2.2 %collective-permute-start.11 = (bf16[512,384]{1,0:T(8,128)(2,1)S(1)}, bf16[512,384]{1,0:T(8,128)(2,1)S(1)}, u32[]{:S(2)}, u32[]{:S(2)}) collective-permute-start(bf16[512,384]{1,0:T(8,128)(2,1)S(1)} %get-tuple-element.37), channel_id=1, source_target_pairs={{4,0},{12,8},{16,12},{20,16},{28,24},{5,1},{13,9},{17,13},{21,17},... | collective-permute-start | bytes 1179656 | tf_op jit(solution)/shard_map/ppermute | solution.py:221
  65.4 0.7 collective-permute-start.15
  66.0 9.2 %collective-permute-done.14 = bf16[384,384]{1,0:T(8,128)(2,1)S(1)} collective-permute-done((bf16[384,384]{1,0:T(8,128)(2,1)S(1)}, bf16[384,384]{1,0:T(8,128)(2,1)S(1)}, u32[]{:S(2)}, u32[]{:S(2)}) %collective-permute-start.14) | collective-permute-done | bytes 294944 | tf_op jit(solution)/shard_map/ppermute | solution.py:207
  75.2 0.1 add_convert_fusion.2
  75.3 0.1 convert_add_fusion
  75.5 0.1 add_convert_fusion.1
  75.6 1.3 %collective-permute-start.17 = (bf16[512,384]{1,0:T(8,128)(2,1)S(1)}, bf16[512,384]{1,0:T(8,128)(2,1)S(1)}, u32[]{:S(2)}, u32[]{:S(2)}) collective-permute-start(bf16[512,384]{1,0:T(8,128)(2,1)S(1)} %add_convert_fusion.1), channel_id=1, source_target_pairs={{20,12},{21,13},{22,14},{23,15}} | collective-permute-start | bytes 1179656 | tf_op jit(solution)/shard_map/ppermute | solution.py:221
  76.9 0.1 collective-permute-start.19
  77.0 2.4 %collective-permute-start.18 = (bf16[192,384]{1,0:T(8,128)(2,1)S(1)}, bf16[192,384]{1,0:T(8,128)(2,1)S(1)}, u32[]{:S(2)}, u32[]{:S(2)}) collective-permute-start(bf16[192,384]{1,0:T(8,128)(2,1)S(1)} %get-tuple-element.58.refs_0_), channel_id=1, source_target_pairs={{0,8},{4,12},{8,0},{12,4},{16,24},{20,28},{24,16},{28,20},{1,9},{5... | collective-permute-start | bytes 442376 | tf_op jit(solution)/shard_map/ppermute | solution.py:207
  79.5 0.7 collective-permute-start.8
  80.1 2.7 %collective-permute-done.18.refs_1_ = bf16[192,384]{1,0:T(8,128)(2,1)S(1)} collective-permute-done((bf16[192,384]{1,0:T(8,128)(2,1)S(1)}, bf16[192,384]{1,0:T(8,128)(2,1)S(1)}, u32[]{:S(2)}, u32[]{:S(2)}) %collective-permute-start.18) | collective-permute-done | bytes 147488 | tf_op jit(solution)/shard_map/ppermute | solution.py:207
  82.8 0.7 collective-permute-start.16
  83.6 3.3 %collective-permute-done.19.refs_4_ = bf16[192,384]{1,0:T(8,128)(2,1)S(1)} collective-permute-done((bf16[192,384]{1,0:T(8,128)(2,1)S(1)}, bf16[192,384]{1,0:T(8,128)(2,1)S(1)}, u32[]{:S(2)}, u32[]{:S(2)}) %collective-permute-start.19) | collective-permute-done | bytes 147488 | tf_op jit(solution)/shard_map/ppermute | solution.py:207
  86.9 3.1 %collective-permute-done.17 = bf16[512,384]{1,0:T(8,128)(2,1)S(1)} collective-permute-done((bf16[512,384]{1,0:T(8,128)(2,1)S(1)}, bf16[512,384]{1,0:T(8,128)(2,1)S(1)}, u32[]{:S(2)}, u32[]{:S(2)}) %collective-permute-start.17) | collective-permute-done | bytes 393248 | tf_op jit(solution)/shard_map/ppermute | solution.py:221
  90.0 0.1 add_convert_fusion
  90.1 1.9 %collective-permute-start.20 = (bf16[512,384]{1,0:T(8,128)(2,1)S(1)}, bf16[512,384]{1,0:T(8,128)(2,1)S(1)}, u32[]{:S(2)}, u32[]{:S(2)}) collective-permute-start(bf16[512,384]{1,0:T(8,128)(2,1)S(1)} %add_convert_fusion), channel_id=1, source_target_pairs={{4,0},{12,8},{16,12},{20,16},{28,24},{5,1},{13,9},{17,13},{21,17},... | collective-permute-start | bytes 1179656 | tf_op jit(solution)/shard_map/ppermute | solution.py:221
  92.1 0.1 collective-permute-start.22
  92.2 0.8 fusion.1
  93.0 5.6 %collective-permute-done.21.refs_2_ = bf16[2,192,384]{2,1,0:T(8,128)(2,1)S(1)} collective-permute-done((bf16[2,192,384]{2,1,0:T(8,128)(2,1)S(1)}, bf16[2,192,384]{2,1,0:T(8,128)(2,1)S(1)}, u32[]{:S(2)}, u32[]{:S(2)}) %collective-permute-start.21) | collective-permute-done | bytes 294944 | tf_op jit(solution)/shard_map/ppermute | solution.py:207
  98.6 0.8 collective-permute-done.22.refs_5_
  99.4 1.6 %assemble.1 = f32[384,1536]{1,0:T(8,128)} custom-call(bf16[192,384]{1,0:T(8,128)(2,1)S(1)} %get-tuple-element.58.refs_0_, bf16[192,384]{1,0:T(8,128)(2,1)S(1)} %collective-permute-done.18.refs_1_, bf16[2,192,384]{2,1,0:T(8,128)(2,1)S(1)} %collective-permute-done.21.refs_2_, bf16[192,384]{1,0:T(8,128)(2,1)S(1)} %get-tuple-element.57.refs_3_, ...), custom_call_target="tpu_custom_call" | custom-call | tf_op jit(solution)/shard_map/assemble/pallas_call | solution.py:336
  101.0 4.2 %collective-permute-done.20 = bf16[512,384]{1,0:T(8,128)(2,1)S(1)} collective-permute-done((bf16[512,384]{1,0:T(8,128)(2,1)S(1)}, bf16[512,384]{1,0:T(8,128)(2,1)S(1)}, u32[]{:S(2)}, u32[]{:S(2)}) %collective-permute-start.20) | collective-permute-done | bytes 393248 | tf_op jit(solution)/shard_map/ppermute | solution.py:221
  105.2 1.1 %fusion.2 = (bf16[512,384]{1,0:T(8,128)(2,1)}, bf16[512,384]{1,0:T(8,128)(2,1)}) fusion(bf16[512,384]{1,0:T(8,128)(2,1)S(1)} %collective-permute-done.20, f32[2,512,384]{2,1,0:T(8,128)S(1)} %get-tuple-element.36, bf16[512,384]{1,0:T(8,128)(2,1)S(1)} %collective-permute-done.16, bf16[512,384]{1,0:T(8,128)(2,1)S(1)} %collective-permute-done.11), kind=kLoop, calls=%fused_computation.7 | loop fusion | flops 1572864 | bytes 3538944 | tf_op jit(solution)/shard_map/convert_element_type | solution.py:371
  (35 shorter events, 0.4 us)
Async XLA Ops:
  0.6 26.2 %copy-start.1 = (bf16[512,384]{1,0:T(8,128)(2,1)S(1)}, bf16[512,384]{1,0:T(8,128)(2,1)}, u32[]{:S(2)}) copy-start(bf16[512,384]{1,0:T(8,128)(2,1)} %v.5) | copy-start | bytes 1179652
  0.6 7.3 %copy-start = (bf16[512,384]{1,0:T(8,128)(2,1)S(1)}, bf16[512,384]{1,0:T(8,128)(2,1)}, u32[]{:S(2)}) copy-start(bf16[512,384]{1,0:T(8,128)(2,1)} %k.5) | copy-start | bytes 1179652
  0.7 4.9 %copy-start.4 = (bf16[512,384]{1,0:T(8,128)(2,1)S(1)}, bf16[512,384]{1,0:T(8,128)(2,1)}, u32[]{:S(2)}) copy-start(bf16[512,384]{1,0:T(8,128)(2,1)} %rest_6_.1) | copy-start | bytes 1179652
  0.7 26.2 %copy-start.5 = (s32[8]{0:T(128)S(1)}, s32[8]{0:T(128)}, u32[]{:S(2)}) copy-start(s32[8]{0:T(128)} %anchor.5) | copy-start | bytes 100
  0.7 26.2 %copy-start.3 = (bf16[512,384]{1,0:T(8,128)(2,1)S(1)}, bf16[512,384]{1,0:T(8,128)(2,1)}, u32[]{:S(2)}) copy-start(bf16[512,384]{1,0:T(8,128)(2,1)} %q.5) | copy-start | bytes 1179652
  2.0 30.7 %copy-start.2 = (bf16[384,1536]{1,0:T(8,128)(2,1)S(1)}, bf16[384,1536]{1,0:T(8,128)(2,1)}, u32[]{:S(2)}) copy-start(bf16[384,1536]{1,0:T(8,128)(2,1)} %weight.3) | copy-start | bytes 3538948
  2.0 21.3 %collective-permute-start = (bf16[2,512,384]{2,1,0:T(8,128)(2,1)S(1)}, bf16[2,512,384]{2,1,0:T(8,128)(2,1)S(1)}, u32[]{:S(2)}, u32[]{:S(2)}) collective-permute-start(bf16[2,512,384]{2,1,0:T(8,128)(2,1)S(1)} %pad_maximum_fusion), channel_id=1, source_target_pairs={{0,4},{8,12},{12,16},{16,20},{24,28},{1,5},{9,13},{13,17},{17,21},... | collective-permute-start | bytes 2359304 | tf_op jit(solution)/shard_map/ppermute | solution.py:221
  5.6 10.6 %collective-permute-start.5 = (bf16[512,384]{1,0:T(8,128)(2,1)S(1)}, bf16[512,384]{1,0:T(8,128)(2,1)S(1)}, u32[]{:S(2)}, u32[]{:S(2)}) collective-permute-start(bf16[512,384]{1,0:T(8,128)(2,1)S(1)} %copy-done.4), channel_id=1, source_target_pairs={{0,2},{1,3},{2,0},{3,1},{4,6},{5,7},{6,4},{7,5},{8,10},{9,11},{10,... | collective-permute-start | bytes 1179656 | tf_op jit(solution)/shard_map/ppermute | solution.py:207
  7.1 26.7 %collective-permute-start.1 = (bf16[2,512,384]{2,1,0:T(8,128)(2,1)S(1)}, bf16[2,512,384]{2,1,0:T(8,128)(2,1)S(1)}, u32[]{:S(2)}, u32[]{:S(2)}) collective-permute-start(bf16[2,512,384]{2,1,0:T(8,128)(2,1)S(1)} %pad_maximum_fusion), channel_id=1, source_target_pairs={{8,16},{9,17},{10,18},{11,19}} | collective-permute-start | bytes 2359304 | tf_op jit(solution)/shard_map/ppermute | solution.py:221
  7.9 24.8 %collective-permute-start.4 = (bf16[512,384]{1,0:T(8,128)(2,1)S(1)}, bf16[512,384]{1,0:T(8,128)(2,1)S(1)}, u32[]{:S(2)}, u32[]{:S(2)}) collective-permute-start(bf16[512,384]{1,0:T(8,128)(2,1)S(1)} %copy-done.4), channel_id=1, source_target_pairs={{0,1},{1,0},{2,3},{3,2},{4,5},{5,4},{6,7},{7,6},{8,9},{9,8},{10,11... | collective-permute-start | bytes 1179656 | tf_op jit(solution)/shard_map/ppermute | solution.py:207
  7.9 25.9 %collective-permute-start.2 = (bf16[512,384]{1,0:T(8,128)(2,1)S(1)}, bf16[512,384]{1,0:T(8,128)(2,1)S(1)}, u32[]{:S(2)}, u32[]{:S(2)}) collective-permute-start(bf16[512,384]{1,0:T(8,128)(2,1)S(1)} %copy-done), channel_id=1, source_target_pairs={{8,20},{9,21},{10,22},{11,23}} | collective-permute-start | bytes 1179656 | tf_op jit(solution)/shard_map/ppermute | solution.py:221
  16.2 16.4 %collective-permute-start.6 = (bf16[512,384]{1,0:T(8,128)(2,1)S(1)}, bf16[512,384]{1,0:T(8,128)(2,1)S(1)}, u32[]{:S(2)}, u32[]{:S(2)}) collective-permute-start(bf16[512,384]{1,0:T(8,128)(2,1)S(1)} %collective-permute-done.5.third.rest_8_), channel_id=1, source_target_pairs={{0,1},{1,0},{2,3},{3,2},{4,5},{5,4},{6,7},{7,6},{8,9},{9,8},{10,11... | collective-permute-start | bytes 1179656 | tf_op jit(solution)/shard_map/ppermute | solution.py:207
  23.4 11.0 %collective-permute-start.3 = (bf16[512,384]{1,0:T(8,128)(2,1)S(1)}, bf16[512,384]{1,0:T(8,128)(2,1)S(1)}, u32[]{:S(2)}, u32[]{:S(2)}) collective-permute-start(bf16[512,384]{1,0:T(8,128)(2,1)S(1)} %slice_bitcast_fusion.1), channel_id=1, source_target_pairs={{12,20},{13,21},{14,22},{15,23}} | collective-permute-start | bytes 1179656 | tf_op jit(solution)/shard_map/ppermute | solution.py:221
  40.2 11.3 %collective-permute-start.10 = (bf16[2,192,384]{2,1,0:T(8,128)(2,1)S(1)}, bf16[2,192,384]{2,1,0:T(8,128)(2,1)S(1)}, u32[]{:S(2)}, u32[]{:S(2)}) collective-permute-start(bf16[2,192,384]{2,1,0:T(8,128)(2,1)S(1)} %get-tuple-element.53), channel_id=1, source_target_pairs={{0,8},{4,12},{8,0},{12,4},{16,24},{20,28},{24,16},{28,20},{1,9},{5... | collective-permute-start | bytes 884744 | tf_op jit(solution)/shard_map/ppermute | solution.py:207
  40.3 11.2 %collective-permute-start.9 = (bf16[2,192,384]{2,1,0:T(8,128)(2,1)S(1)}, bf16[2,192,384]{2,1,0:T(8,128)(2,1)S(1)}, u32[]{:S(2)}, u32[]{:S(2)}) collective-permute-start(bf16[2,192,384]{2,1,0:T(8,128)(2,1)S(1)} %get-tuple-element.54), channel_id=1, source_target_pairs={{0,4},{4,0},{8,12},{12,8},{16,20},{20,16},{24,28},{28,24},{1,5},{5... | collective-permute-start | bytes 884744 | tf_op jit(solution)/shard_map/ppermute | solution.py:207
  42.9 32.4 %collective-permute-start.7 = (bf16[2,512,384]{2,1,0:T(8,128)(2,1)S(1)}, bf16[2,512,384]{2,1,0:T(8,128)(2,1)S(1)}, u32[]{:S(2)}, u32[]{:S(2)}) collective-permute-start(bf16[2,512,384]{2,1,0:T(8,128)(2,1)S(1)} %get-tuple-element.31), channel_id=1, source_target_pairs={{0,1},{1,0},{2,3},{3,2},{4,5},{5,4},{6,7},{7,6},{8,9},{9,8},{10,11... | collective-permute-start | bytes 2359304 | tf_op jit(solution)/shard_map/ppermute | solution.py:207
  51.6 6.3 %collective-permute-start.13 = (bf16[192,384]{1,0:T(8,128)(2,1)S(1)}, bf16[192,384]{1,0:T(8,128)(2,1)S(1)}, u32[]{:S(2)}, u32[]{:S(2)}) collective-permute-start(bf16[192,384]{1,0:T(8,128)(2,1)S(1)} %fusion.11), channel_id=1, source_target_pairs={{0,4},{4,0},{8,12},{12,8},{16,20},{20,16},{24,28},{28,24},{1,5},{5... | collective-permute-start | bytes 442376 | tf_op jit(solution)/shard_map/ppermute | solution.py:207
  52.3 6.2 %collective-permute-start.12 = (bf16[192,384]{1,0:T(8,128)(2,1)S(1)}, bf16[192,384]{1,0:T(8,128)(2,1)S(1)}, u32[]{:S(2)}, u32[]{:S(2)}) collective-permute-start(bf16[192,384]{1,0:T(8,128)(2,1)S(1)} %fusion.10), channel_id=1, source_target_pairs={{0,8},{4,12},{8,0},{12,4},{16,24},{20,28},{24,16},{28,20},{1,9},{5... | collective-permute-start | bytes 442376 | tf_op jit(solution)/shard_map/ppermute | solution.py:207
  58.5 16.7 %collective-permute-start.14 = (bf16[384,384]{1,0:T(8,128)(2,1)S(1)}, bf16[384,384]{1,0:T(8,128)(2,1)S(1)}, u32[]{:S(2)}, u32[]{:S(2)}) collective-permute-start(bf16[384,384]{1,0:T(8,128)(2,1)S(1)} %pad_maximum_fusion.1), channel_id=1, source_target_pairs={{0,16},{4,20},{8,24},{12,28},{16,0},{20,4},{24,8},{28,12},{1,17},{... | collective-permute-start | bytes 884744 | tf_op jit(solution)/shard_map/ppermute | solution.py:207
  63.2 37.8 %collective-permute-start.11 = (bf16[512,384]{1,0:T(8,128)(2,1)S(1)}, bf16[512,384]{1,0:T(8,128)(2,1)S(1)}, u32[]{:S(2)}, u32[]{:S(2)}) collective-permute-start(bf16[512,384]{1,0:T(8,128)(2,1)S(1)} %get-tuple-element.37), channel_id=1, source_target_pairs={{4,0},{12,8},{16,12},{20,16},{28,24},{5,1},{13,9},{17,13},{21,17},... | collective-permute-start | bytes 1179656 | tf_op jit(solution)/shard_map/ppermute | solution.py:221
  65.4 10.1 %collective-permute-start.15 = (bf16[512,384]{1,0:T(8,128)(2,1)S(1)}, bf16[512,384]{1,0:T(8,128)(2,1)S(1)}, u32[]{:S(2)}, u32[]{:S(2)}) collective-permute-start(bf16[512,384]{1,0:T(8,128)(2,1)S(1)} %get-tuple-element.44), channel_id=1, source_target_pairs={{16,20},{20,16},{17,21},{21,17},{18,22},{22,18},{19,23},{23,19}} | collective-permute-start | bytes 1179656 | tf_op jit(solution)/shard_map/ppermute | solution.py:221
  75.6 14.4 %collective-permute-start.17 = (bf16[512,384]{1,0:T(8,128)(2,1)S(1)}, bf16[512,384]{1,0:T(8,128)(2,1)S(1)}, u32[]{:S(2)}, u32[]{:S(2)}) collective-permute-start(bf16[512,384]{1,0:T(8,128)(2,1)S(1)} %add_convert_fusion.1), channel_id=1, source_target_pairs={{20,12},{21,13},{22,14},{23,15}} | collective-permute-start | bytes 1179656 | tf_op jit(solution)/shard_map/ppermute | solution.py:221
  76.9 9.9 %collective-permute-start.19 = (bf16[192,384]{1,0:T(8,128)(2,1)S(1)}, bf16[192,384]{1,0:T(8,128)(2,1)S(1)}, u32[]{:S(2)}, u32[]{:S(2)}) collective-permute-start(bf16[192,384]{1,0:T(8,128)(2,1)S(1)} %get-tuple-element.57.refs_3_), channel_id=1, source_target_pairs={{0,4},{4,0},{8,12},{12,8},{16,20},{20,16},{24,28},{28,24},{1,5},{5... | collective-permute-start | bytes 442376 | tf_op jit(solution)/shard_map/ppermute | solution.py:207
  77.0 5.8 %collective-permute-start.18 = (bf16[192,384]{1,0:T(8,128)(2,1)S(1)}, bf16[192,384]{1,0:T(8,128)(2,1)S(1)}, u32[]{:S(2)}, u32[]{:S(2)}) collective-permute-start(bf16[192,384]{1,0:T(8,128)(2,1)S(1)} %get-tuple-element.58.refs_0_), channel_id=1, source_target_pairs={{0,8},{4,12},{8,0},{12,4},{16,24},{20,28},{24,16},{28,20},{1,9},{5... | collective-permute-start | bytes 442376 | tf_op jit(solution)/shard_map/ppermute | solution.py:207
  79.5 12.6 %collective-permute-start.8 = (bf16[512,384]{1,0:T(8,128)(2,1)S(1)}, bf16[512,384]{1,0:T(8,128)(2,1)S(1)}, u32[]{:S(2)}, u32[]{:S(2)}) collective-permute-start(bf16[512,384]{1,0:T(8,128)(2,1)S(1)} %fusion.5), channel_id=1, source_target_pairs={{0,2},{1,3},{2,0},{3,1},{4,6},{5,7},{6,4},{7,5},{8,10},{9,11},{10,... | collective-permute-start | bytes 1179656 | tf_op jit(solution)/shard_map/ppermute | solution.py:207
  82.8 18.1 %collective-permute-start.16 = (bf16[512,384]{1,0:T(8,128)(2,1)S(1)}, bf16[512,384]{1,0:T(8,128)(2,1)S(1)}, u32[]{:S(2)}, u32[]{:S(2)}) collective-permute-start(bf16[512,384]{1,0:T(8,128)(2,1)S(1)} %add_convert_fusion.1), channel_id=1, source_target_pairs={{16,8},{17,9},{18,10},{19,11}} | collective-permute-start | bytes 1179656 | tf_op jit(solution)/shard_map/ppermute | solution.py:221
  86.9 11.7 %collective-permute-start.21 = (bf16[2,192,384]{2,1,0:T(8,128)(2,1)S(1)}, bf16[2,192,384]{2,1,0:T(8,128)(2,1)S(1)}, u32[]{:S(2)}, u32[]{:S(2)}) collective-permute-start(bf16[2,192,384]{2,1,0:T(8,128)(2,1)S(1)} %pad_maximum_fusion.2), channel_id=1, source_target_pairs={{0,4},{4,0},{8,12},{12,8},{16,20},{20,16},{24,28},{28,24},{1,5},{5... | collective-permute-start | bytes 884744 | tf_op jit(solution)/shard_map/ppermute | solution.py:207
  90.1 15.1 %collective-permute-start.20 = (bf16[512,384]{1,0:T(8,128)(2,1)S(1)}, bf16[512,384]{1,0:T(8,128)(2,1)S(1)}, u32[]{:S(2)}, u32[]{:S(2)}) collective-permute-start(bf16[512,384]{1,0:T(8,128)(2,1)S(1)} %add_convert_fusion), channel_id=1, source_target_pairs={{4,0},{12,8},{16,12},{20,16},{28,24},{5,1},{13,9},{17,13},{21,17},... | collective-permute-start | bytes 1179656 | tf_op jit(solution)/shard_map/ppermute | solution.py:221
  92.1 7.3 %collective-permute-start.22 = (bf16[2,192,384]{2,1,0:T(8,128)(2,1)S(1)}, bf16[2,192,384]{2,1,0:T(8,128)(2,1)S(1)}, u32[]{:S(2)}, u32[]{:S(2)}) collective-permute-start(bf16[2,192,384]{2,1,0:T(8,128)(2,1)S(1)} %pad_maximum_fusion.3), channel_id=1, source_target_pairs={{0,8},{4,12},{8,0},{12,4},{16,24},{20,28},{24,16},{28,20},{1,9},{5... | collective-permute-start | bytes 884744 | tf_op jit(solution)/shard_map/ppermute | solution.py:207

commit v6 on v5

--- a/solution.py
+++ b/solution.py
@@ -13,7 +13,7 @@
 F32 = jnp.float32
 SCALE = HEAD_DIM ** -0.5
 SCALE_LOG2 = SCALE * math.log2(math.e)
-Q_CHUNK = 256
+Q_CHUNK = 512
 
 
 def dot(a, b, dims):
@@ -349,9 +349,10 @@
         home_v = send(merged, [(upper, source + 1)])
         if frames == 8:
             home_v = lax.optimization_barrier((home_v, other_a, other_b))[0]
-        from_v = send((near_dv.astype(F32) + home_v.astype(F32)).astype(BF16), back(near_pairs)).astype(F32)
+        from_v = send((near_dv.astype(F32) + home_v.astype(F32)).astype(BF16), back(near_pairs))
         key_total = own_grad[0] + from_k.astype(F32) + home_k
-        value_total = own_grad[1] + from_v
+        key_total, from_v = lax.optimization_barrier((key_total.astype(BF16), from_v))
+        value_total = own_grad[1] + from_v.astype(F32)
     else:
         both = []
         for own, near, far in ((own_grad[0], near_dk, far_dk), (own_grad[1], near_dv, far_dv)):

time: 107 us -> 105 us (0.981)
  Pallas kernels: 23.8 us -> 22 us
    ppermute x14, waiting for transfers between devices: 33.3 us -> 29.3 us  [swap(): lax.ppermute(array, axis, [(i, i ^ bit) for i in range(lax.axis_size(axis...]
    ppermute x9, waiting for transfers between devices: 15 us -> 18.1 us  [send(): return lax.ppermute(array, 'tm', pairs)]
    pallas_call x1, Pallas kernels: 5.73 us -> 4.51 us  [local(): pl.pallas_call(near_kernel, grid=(heads,), out_shape=(part_shape, stat_sh...]
  transfers between devices with their start and end apart: 23 -> 23, of which waited for: 12 -> 12; matrix products, arithmetic and copies ran while one was open for 2% -> 2% of each run, Pallas kernels for 17% -> 16%
where the time goes in v6:
time: 105 us
  waiting for transfers between devices  47.4 us (45%)
  starting transfers between devices  29.5 us (28%)
  Pallas kernels  22 us (21%)
  other arithmetic  4.59 us (4%)
    ppermute x14, waiting for transfers between devices, swap(): lax.ppermute(array, axis, [(i, i ^ bit) for i in range(lax.axis_size(axis...  29.3 us
    ppermute x9, waiting for transfers between devices, send(): return lax.ppermute(array, 'tm', pairs)  18.1 us
    ppermute x9, starting transfers between devices, send(): return lax.ppermute(array, 'tm', pairs)  15.2 us
    ppermute x14, starting transfers between devices, swap(): lax.ppermute(array, axis, [(i, i ^ bit) for i in range(lax.axis_size(axis...  14.3 us
    pallas_call x1, Pallas kernels, local(): pl.pallas_call(functools.partial(backward_kernel, count, far_frames[0] if...  8.5 us
    pallas_call x1, Pallas kernels, local(): pl.pallas_call(functools.partial(far_kernel, count), grid=(heads,), out_s...  5.15 us
    pallas_call x1, Pallas kernels, local(): pl.pallas_call(near_kernel, grid=(heads,), out_shape=(part_shape, stat_sh...  4.51 us
  transfers between devices with their start and end apart: 23, of which 12 were waited for; matrix products, arithmetic and copies ran while one was open for 2% of the time, Pallas kernels for 16%

profile of v6, /device:TPU:12, one launch (start us, length us, event | category | flops | bytes accessed | tf_op | source)
XLA Modules:
  0.0 104.8 jit_solution(14630904680306556091)
XLA Ops:
  0.7 1.3 %pad_maximum_fusion = bf16[2,512,384]{2,1,0:T(8,128)(2,1)S(1)} fusion(bf16[1,512,384]{2,1,0:T(8,128)(2,1)} %bitcast.45, bf16[1,512,384]{2,1,0:T(8,128)(2,1)} %bitcast.44), kind=kLoop, calls=%fused_computation.5 | loop fusion | flops 393216 | bytes 1572864 | tf_op jit(solution)/shard_map/stack | solution.py:226
  2.0 3.6 %collective-permute-start = (bf16[2,512,384]{2,1,0:T(8,128)(2,1)S(1)}, bf16[2,512,384]{2,1,0:T(8,128)(2,1)S(1)}, u32[]{:S(2)}, u32[]{:S(2)}) collective-permute-start(bf16[2,512,384]{2,1,0:T(8,128)(2,1)S(1)} %pad_maximum_fusion), channel_id=1, source_target_pairs={{0,4},{8,12},{12,16},{16,20},{24,28},{1,5},{9,13},{13,17},{17,21},... | collective-permute-start | bytes 2359304 | tf_op jit(solution)/shard_map/ppermute | solution.py:221
  5.6 1.6 %collective-permute-start.5 = (bf16[512,384]{1,0:T(8,128)(2,1)S(1)}, bf16[512,384]{1,0:T(8,128)(2,1)S(1)}, u32[]{:S(2)}, u32[]{:S(2)}) collective-permute-start(bf16[512,384]{1,0:T(8,128)(2,1)S(1)} %copy-done.4), channel_id=1, source_target_pairs={{0,2},{1,3},{2,0},{3,1},{4,6},{5,7},{6,4},{7,5},{8,10},{9,11},{10,... | collective-permute-start | bytes 1179656 | tf_op jit(solution)/shard_map/ppermute | solution.py:207
  7.1 0.7 collective-permute-start.1
  7.9 0.1 collective-permute-start.4
  7.9 0.7 collective-permute-start.2
  8.6 7.6 %collective-permute-done.5.third.rest_8_ = bf16[512,384]{1,0:T(8,128)(2,1)S(1)} collective-permute-done((bf16[512,384]{1,0:T(8,128)(2,1)S(1)}, bf16[512,384]{1,0:T(8,128)(2,1)S(1)}, u32[]{:S(2)}, u32[]{:S(2)}) %collective-permute-start.5) | collective-permute-done | bytes 393248 | tf_op jit(solution)/shard_map/ppermute | solution.py:207
  16.2 7.1 %collective-permute-done.prev = bf16[2,512,384]{2,1,0:T(8,128)(2,1)S(1)} collective-permute-done((bf16[2,512,384]{2,1,0:T(8,128)(2,1)S(1)}, bf16[2,512,384]{2,1,0:T(8,128)(2,1)S(1)}, u32[]{:S(2)}, u32[]{:S(2)}) %collective-permute-start) | collective-permute-done | bytes 786464 | tf_op jit(solution)/shard_map/ppermute | solution.py:221
  23.4 3.5 %collective-permute-start.3 = (bf16[512,384]{1,0:T(8,128)(2,1)S(1)}, bf16[512,384]{1,0:T(8,128)(2,1)S(1)}, u32[]{:S(2)}, u32[]{:S(2)}) collective-permute-start(bf16[512,384]{1,0:T(8,128)(2,1)S(1)} %slice_bitcast_fusion.1), channel_id=1, source_target_pairs={{12,20},{13,21},{14,22},{15,23}} | collective-permute-start | bytes 1179656 | tf_op jit(solution)/shard_map/ppermute | solution.py:221
  26.9 4.5 %near.1 = (f32[3,128,512]{2,1,0:T(8,128)S(1)}, f32[3,8,512]{2,1,0:T(8,128)S(1)}) custom-call(s32[8]{0:T(128)S(1)} %copy-done.5, bf16[512,384]{1,0:T(8,128)(2,1)S(1)} %copy-done.3, bf16[512,384]{1,0:T(8,128)(2,1)S(1)} %copy-done, bf16[512,384]{1,0:T(8,128)(2,1)S(1)} %copy-done.1, bf16[2,512,384]{2,1,0:T(8,128)(2,1)S(1)} %collective-permute-done.prev), custom_call_target="tpu_custom_call" | custom-call | tf_op jit(solution)/shard_map/near/pallas_call | solution.py:271
  31.5 1.1 %cotangent.1.rest_5_.rest_3_ = bf16[512,384]{1,0:T(8,128)(2,1)S(1)} custom-call(bf16[512,384]{1,0:T(8,128)(2,1)S(1)} %copy-done.4, bf16[512,384]{1,0:T(8,128)(2,1)S(1)} %collective-permute-done.4.second.rest_7_, bf16[512,384]{1,0:T(8,128)(2,1)S(1)} %collective-permute-done.5.third.rest_8_, bf16[512,384]{1,0:T(8,128)(2,1)S(1)} %collective-permute-done.6.fourth.rest_9_, ...), custom_call_target="tpu_custom_call" | custom-call | tf_op jit(solution)/shard_map/cotangent/pallas_call | solution.py:250
  32.6 1.7 %collective-permute-done.3.rest_2_ = bf16[512,384]{1,0:T(8,128)(2,1)S(1)} collective-permute-done((bf16[512,384]{1,0:T(8,128)(2,1)S(1)}, bf16[512,384]{1,0:T(8,128)(2,1)S(1)}, u32[]{:S(2)}, u32[]{:S(2)}) %collective-permute-start.3) | collective-permute-done | bytes 393248 | tf_op jit(solution)/shard_map/ppermute | solution.py:221
  34.3 5.1 %far.1 = (bf16[512,384]{1,0:T(8,128)(2,1)S(1)}, f32[3,8,512]{2,1,0:T(8,128)S(1)}, f32[2,384,384]{2,1,0:T(8,128)S(1)}, bf16[2,384,384]{2,1,0:T(8,128)(2,1)S(1)}) custom-call(s32[8]{0:T(128)S(1)} %copy-done.5, bf16[512,384]{1,0:T(8,128)(2,1)S(1)} %copy-done.3, bf16[512,384]{1,0:T(8,128)(2,1)S(1)} %copy-done, bf16[512,384]{1,0:T(8,128)(2,1)S(1)} %copy-done.1, ...), custom_call_target="tpu_custom_call" | custom-call | tf_op jit(solution)/shard_map/far/pallas_call | solution.py:283
  39.5 0.1 fusion.12
  39.6 0.1 collective-permute-start.10
  39.6 1.5 %collective-permute-start.9 = (bf16[2,192,384]{2,1,0:T(8,128)(2,1)S(1)}, bf16[2,192,384]{2,1,0:T(8,128)(2,1)S(1)}, u32[]{:S(2)}, u32[]{:S(2)}) collective-permute-start(bf16[2,192,384]{2,1,0:T(8,128)(2,1)S(1)} %get-tuple-element.56), channel_id=1, source_target_pairs={{0,4},{4,0},{8,12},{12,8},{16,20},{20,16},{24,28},{28,24},{1,5},{5... | collective-permute-start | bytes 884744 | tf_op jit(solution)/shard_map/ppermute | solution.py:207
  41.2 1.1 %output.1 = (f32[2,512,384]{2,1,0:T(8,128)S(1)}, bf16[2,512,384]{2,1,0:T(8,128)(2,1)S(1)}) custom-call(bf16[512,384]{1,0:T(8,128)(2,1)S(1)} %get-tuple-element.31.attended, bf16[384,1536]{1,0:T(8,128)(2,1)S(1)} %copy-done.2), custom_call_target="tpu_custom_call" | custom-call | tf_op jit(solution)/shard_map/output/pallas_call | solution.py:374
  42.3 0.1 collective-permute-start.7
  42.4 8.5 %backward.1 = (bf16[512,384]{1,0:T(8,128)(2,1)}, f32[2,512,384]{2,1,0:T(8,128)S(1)}, bf16[512,384]{1,0:T(8,128)(2,1)S(1)}, bf16[512,384]{1,0:T(8,128)(2,1)S(1)},...) custom-call(s32[8]{0:T(128)S(1)} %copy-done.5, bf16[512,384]{1,0:T(8,128)(2,1)S(1)} %copy-done.3, ...), custom_call_target="tpu_custom_call" | custom-call | tf_op jit(solution)/shard_map/backward/pallas_call | solution.py:299
  50.9 0.1 convert_add_fusion.2
  51.0 0.6 collective-permute-start.13
  51.7 2.0 %collective-permute-start.12 = (bf16[192,384]{1,0:T(8,128)(2,1)S(1)}, bf16[192,384]{1,0:T(8,128)(2,1)S(1)}, u32[]{:S(2)}, u32[]{:S(2)}) collective-permute-start(bf16[192,384]{1,0:T(8,128)(2,1)S(1)} %fusion.10), channel_id=1, source_target_pairs={{0,8},{4,12},{8,0},{12,4},{16,24},{20,28},{24,16},{28,20},{1,9},{5... | collective-permute-start | bytes 442376 | tf_op jit(solution)/shard_map/ppermute | solution.py:207
  53.7 3.6 %collective-permute-done.13 = bf16[192,384]{1,0:T(8,128)(2,1)S(1)} collective-permute-done((bf16[192,384]{1,0:T(8,128)(2,1)S(1)}, bf16[192,384]{1,0:T(8,128)(2,1)S(1)}, u32[]{:S(2)}, u32[]{:S(2)}) %collective-permute-start.13) | collective-permute-done | bytes 147488 | tf_op jit(solution)/shard_map/ppermute | solution.py:207
  57.3 0.6 collective-permute-done.12
  58.0 4.6 %collective-permute-start.14 = (bf16[384,384]{1,0:T(8,128)(2,1)S(1)}, bf16[384,384]{1,0:T(8,128)(2,1)S(1)}, u32[]{:S(2)}, u32[]{:S(2)}) collective-permute-start(bf16[384,384]{1,0:T(8,128)(2,1)S(1)} %pad_maximum_fusion.1), channel_id=1, source_target_pairs={{0,16},{4,20},{8,24},{12,28},{16,0},{20,4},{24,8},{28,12},{1,17},{... | collective-permute-start | bytes 884744 | tf_op jit(solution)/shard_map/ppermute | solution.py:207
  62.5 2.2 %collective-permute-start.11 = (bf16[512,384]{1,0:T(8,128)(2,1)S(1)}, bf16[512,384]{1,0:T(8,128)(2,1)S(1)}, u32[]{:S(2)}, u32[]{:S(2)}) collective-permute-start(bf16[512,384]{1,0:T(8,128)(2,1)S(1)} %get-tuple-element.39), channel_id=1, source_target_pairs={{4,0},{12,8},{16,12},{20,16},{28,24},{5,1},{13,9},{17,13},{21,17},... | collective-permute-start | bytes 1179656 | tf_op jit(solution)/shard_map/ppermute | solution.py:221
  64.7 0.7 collective-permute-start.15
  65.4 9.2 %collective-permute-done.14 = bf16[384,384]{1,0:T(8,128)(2,1)S(1)} collective-permute-done((bf16[384,384]{1,0:T(8,128)(2,1)S(1)}, bf16[384,384]{1,0:T(8,128)(2,1)S(1)}, u32[]{:S(2)}, u32[]{:S(2)}) %collective-permute-start.14) | collective-permute-done | bytes 294944 | tf_op jit(solution)/shard_map/ppermute | solution.py:207
  74.6 0.1 add_convert_fusion.2
  74.7 0.1 convert_add_fusion
  74.8 0.1 add_convert_fusion.1
  75.0 0.6 collective-permute-start.19
  75.6 2.5 %collective-permute-start.18 = (bf16[192,384]{1,0:T(8,128)(2,1)S(1)}, bf16[192,384]{1,0:T(8,128)(2,1)S(1)}, u32[]{:S(2)}, u32[]{:S(2)}) collective-permute-start(bf16[192,384]{1,0:T(8,128)(2,1)S(1)} %get-tuple-element.60.refs_0_), channel_id=1, source_target_pairs={{0,8},{4,12},{8,0},{12,4},{16,24},{20,28},{24,16},{28,20},{1,9},{5... | collective-permute-start | bytes 442376 | tf_op jit(solution)/shard_map/ppermute | solution.py:207
  78.1 1.3 %collective-permute-start.17 = (bf16[512,384]{1,0:T(8,128)(2,1)S(1)}, bf16[512,384]{1,0:T(8,128)(2,1)S(1)}, u32[]{:S(2)}, u32[]{:S(2)}) collective-permute-start(bf16[512,384]{1,0:T(8,128)(2,1)S(1)} %add_convert_fusion.1), channel_id=1, source_target_pairs={{20,12},{21,13},{22,14},{23,15}} | collective-permute-start | bytes 1179656 | tf_op jit(solution)/shard_map/ppermute | solution.py:221
  79.5 0.7 collective-permute-start.8
  80.1 1.1 %collective-permute-done.18.refs_1_ = bf16[192,384]{1,0:T(8,128)(2,1)S(1)} collective-permute-done((bf16[192,384]{1,0:T(8,128)(2,1)S(1)}, bf16[192,384]{1,0:T(8,128)(2,1)S(1)}, u32[]{:S(2)}, u32[]{:S(2)}) %collective-permute-start.18) | collective-permute-done | bytes 147488 | tf_op jit(solution)/shard_map/ppermute | solution.py:207
  81.2 0.7 collective-permute-start.16
  82.0 4.3 %collective-permute-done.19.refs_4_ = bf16[192,384]{1,0:T(8,128)(2,1)S(1)} collective-permute-done((bf16[192,384]{1,0:T(8,128)(2,1)S(1)}, bf16[192,384]{1,0:T(8,128)(2,1)S(1)}, u32[]{:S(2)}, u32[]{:S(2)}) %collective-permute-start.19) | collective-permute-done | bytes 147488 | tf_op jit(solution)/shard_map/ppermute | solution.py:207
  86.3 5.4 %collective-permute-done.17 = bf16[512,384]{1,0:T(8,128)(2,1)S(1)} collective-permute-done((bf16[512,384]{1,0:T(8,128)(2,1)S(1)}, bf16[512,384]{1,0:T(8,128)(2,1)S(1)}, u32[]{:S(2)}, u32[]{:S(2)}) %collective-permute-start.17) | collective-permute-done | bytes 393248 | tf_op jit(solution)/shard_map/ppermute | solution.py:221
  91.7 0.1 add_convert_fusion
  91.9 1.9 %collective-permute-start.20 = (bf16[512,384]{1,0:T(8,128)(2,1)S(1)}, bf16[512,384]{1,0:T(8,128)(2,1)S(1)}, u32[]{:S(2)}, u32[]{:S(2)}) collective-permute-start(bf16[512,384]{1,0:T(8,128)(2,1)S(1)} %add_convert_fusion), channel_id=1, source_target_pairs={{4,0},{12,8},{16,12},{20,16},{28,24},{5,1},{13,9},{17,13},{21,17},... | collective-permute-start | bytes 1179656 | tf_op jit(solution)/shard_map/ppermute | solution.py:221
  93.8 0.8 fusion.1
  94.7 0.9 fusion.4
  95.6 0.3 collective-permute-done.21.refs_2_
  95.8 2.6 %collective-permute-done.22.refs_5_ = bf16[2,192,384]{2,1,0:T(8,128)(2,1)S(1)} collective-permute-done((bf16[2,192,384]{2,1,0:T(8,128)(2,1)S(1)}, bf16[2,192,384]{2,1,0:T(8,128)(2,1)S(1)}, u32[]{:S(2)}, u32[]{:S(2)}) %collective-permute-start.22) | collective-permute-done | bytes 294944 | tf_op jit(solution)/shard_map/ppermute | solution.py:207
  98.5 1.6 %assemble.1 = f32[384,1536]{1,0:T(8,128)} custom-call(bf16[192,384]{1,0:T(8,128)(2,1)S(1)} %get-tuple-element.60.refs_0_, bf16[192,384]{1,0:T(8,128)(2,1)S(1)} %collective-permute-done.18.refs_1_, bf16[2,192,384]{2,1,0:T(8,128)(2,1)S(1)} %collective-permute-done.21.refs_2_, bf16[192,384]{1,0:T(8,128)(2,1)S(1)} %get-tuple-element.59.refs_3_, ...), custom_call_target="tpu_custom_call" | custom-call | tf_op jit(solution)/shard_map/assemble/pallas_call | solution.py:336
  100.1 3.9 %collective-permute-done.20 = bf16[512,384]{1,0:T(8,128)(2,1)S(1)} collective-permute-done((bf16[512,384]{1,0:T(8,128)(2,1)S(1)}, bf16[512,384]{1,0:T(8,128)(2,1)S(1)}, u32[]{:S(2)}, u32[]{:S(2)}) %collective-permute-start.20) | collective-permute-done | bytes 393248 | tf_op jit(solution)/shard_map/ppermute | solution.py:221
  104.0 0.8 fusion.2
  (36 shorter events, 0.4 us)
Async XLA Ops:
  0.6 26.2 %copy-start.1 = (bf16[512,384]{1,0:T(8,128)(2,1)S(1)}, bf16[512,384]{1,0:T(8,128)(2,1)}, u32[]{:S(2)}) copy-start(bf16[512,384]{1,0:T(8,128)(2,1)} %v.5) | copy-start | bytes 1179652
  0.6 7.3 %copy-start = (bf16[512,384]{1,0:T(8,128)(2,1)S(1)}, bf16[512,384]{1,0:T(8,128)(2,1)}, u32[]{:S(2)}) copy-start(bf16[512,384]{1,0:T(8,128)(2,1)} %k.5) | copy-start | bytes 1179652
  0.7 4.9 %copy-start.4 = (bf16[512,384]{1,0:T(8,128)(2,1)S(1)}, bf16[512,384]{1,0:T(8,128)(2,1)}, u32[]{:S(2)}) copy-start(bf16[512,384]{1,0:T(8,128)(2,1)} %rest_6_.1) | copy-start | bytes 1179652
  0.7 26.2 %copy-start.5 = (s32[8]{0:T(128)S(1)}, s32[8]{0:T(128)}, u32[]{:S(2)}) copy-start(s32[8]{0:T(128)} %anchor.5) | copy-start | bytes 100
  0.7 26.2 %copy-start.3 = (bf16[512,384]{1,0:T(8,128)(2,1)S(1)}, bf16[512,384]{1,0:T(8,128)(2,1)}, u32[]{:S(2)}) copy-start(bf16[512,384]{1,0:T(8,128)(2,1)} %q.5) | copy-start | bytes 1179652
  2.0 29.4 %copy-start.2 = (bf16[384,1536]{1,0:T(8,128)(2,1)S(1)}, bf16[384,1536]{1,0:T(8,128)(2,1)}, u32[]{:S(2)}) copy-start(bf16[384,1536]{1,0:T(8,128)(2,1)} %weight.3) | copy-start | bytes 3538948
  2.0 21.3 %collective-permute-start = (bf16[2,512,384]{2,1,0:T(8,128)(2,1)S(1)}, bf16[2,512,384]{2,1,0:T(8,128)(2,1)S(1)}, u32[]{:S(2)}, u32[]{:S(2)}) collective-permute-start(bf16[2,512,384]{2,1,0:T(8,128)(2,1)S(1)} %pad_maximum_fusion), channel_id=1, source_target_pairs={{0,4},{8,12},{12,16},{16,20},{24,28},{1,5},{9,13},{13,17},{17,21},... | collective-permute-start | bytes 2359304 | tf_op jit(solution)/shard_map/ppermute | solution.py:221
  5.6 10.6 %collective-permute-start.5 = (bf16[512,384]{1,0:T(8,128)(2,1)S(1)}, bf16[512,384]{1,0:T(8,128)(2,1)S(1)}, u32[]{:S(2)}, u32[]{:S(2)}) collective-permute-start(bf16[512,384]{1,0:T(8,128)(2,1)S(1)} %copy-done.4), channel_id=1, source_target_pairs={{0,2},{1,3},{2,0},{3,1},{4,6},{5,7},{6,4},{7,5},{8,10},{9,11},{10,... | collective-permute-start | bytes 1179656 | tf_op jit(solution)/shard_map/ppermute | solution.py:207
  7.1 25.5 %collective-permute-start.1 = (bf16[2,512,384]{2,1,0:T(8,128)(2,1)S(1)}, bf16[2,512,384]{2,1,0:T(8,128)(2,1)S(1)}, u32[]{:S(2)}, u32[]{:S(2)}) collective-permute-start(bf16[2,512,384]{2,1,0:T(8,128)(2,1)S(1)} %pad_maximum_fusion), channel_id=1, source_target_pairs={{8,16},{9,17},{10,18},{11,19}} | collective-permute-start | bytes 2359304 | tf_op jit(solution)/shard_map/ppermute | solution.py:221
  7.9 23.6 %collective-permute-start.4 = (bf16[512,384]{1,0:T(8,128)(2,1)S(1)}, bf16[512,384]{1,0:T(8,128)(2,1)S(1)}, u32[]{:S(2)}, u32[]{:S(2)}) collective-permute-start(bf16[512,384]{1,0:T(8,128)(2,1)S(1)} %copy-done.4), channel_id=1, source_target_pairs={{0,1},{1,0},{2,3},{3,2},{4,5},{5,4},{6,7},{7,6},{8,9},{9,8},{10,11... | collective-permute-start | bytes 1179656 | tf_op jit(solution)/shard_map/ppermute | solution.py:207
  7.9 24.7 %collective-permute-start.2 = (bf16[512,384]{1,0:T(8,128)(2,1)S(1)}, bf16[512,384]{1,0:T(8,128)(2,1)S(1)}, u32[]{:S(2)}, u32[]{:S(2)}) collective-permute-start(bf16[512,384]{1,0:T(8,128)(2,1)S(1)} %copy-done), channel_id=1, source_target_pairs={{8,20},{9,21},{10,22},{11,23}} | collective-permute-start | bytes 1179656 | tf_op jit(solution)/shard_map/ppermute | solution.py:221
  16.2 15.2 %collective-permute-start.6 = (bf16[512,384]{1,0:T(8,128)(2,1)S(1)}, bf16[512,384]{1,0:T(8,128)(2,1)S(1)}, u32[]{:S(2)}, u32[]{:S(2)}) collective-permute-start(bf16[512,384]{1,0:T(8,128)(2,1)S(1)} %collective-permute-done.5.third.rest_8_), channel_id=1, source_target_pairs={{0,1},{1,0},{2,3},{3,2},{4,5},{5,4},{6,7},{7,6},{8,9},{9,8},{10,11... | collective-permute-start | bytes 1179656 | tf_op jit(solution)/shard_map/ppermute | solution.py:207
  23.4 11.0 %collective-permute-start.3 = (bf16[512,384]{1,0:T(8,128)(2,1)S(1)}, bf16[512,384]{1,0:T(8,128)(2,1)S(1)}, u32[]{:S(2)}, u32[]{:S(2)}) collective-permute-start(bf16[512,384]{1,0:T(8,128)(2,1)S(1)} %slice_bitcast_fusion.1), channel_id=1, source_target_pairs={{12,20},{13,21},{14,22},{15,23}} | collective-permute-start | bytes 1179656 | tf_op jit(solution)/shard_map/ppermute | solution.py:221
  39.6 11.3 %collective-permute-start.10 = (bf16[2,192,384]{2,1,0:T(8,128)(2,1)S(1)}, bf16[2,192,384]{2,1,0:T(8,128)(2,1)S(1)}, u32[]{:S(2)}, u32[]{:S(2)}) collective-permute-start(bf16[2,192,384]{2,1,0:T(8,128)(2,1)S(1)} %get-tuple-element.55), channel_id=1, source_target_pairs={{0,8},{4,12},{8,0},{12,4},{16,24},{20,28},{24,16},{28,20},{1,9},{5... | collective-permute-start | bytes 884744 | tf_op jit(solution)/shard_map/ppermute | solution.py:207
  39.6 11.2 %collective-permute-start.9 = (bf16[2,192,384]{2,1,0:T(8,128)(2,1)S(1)}, bf16[2,192,384]{2,1,0:T(8,128)(2,1)S(1)}, u32[]{:S(2)}, u32[]{:S(2)}) collective-permute-start(bf16[2,192,384]{2,1,0:T(8,128)(2,1)S(1)} %get-tuple-element.56), channel_id=1, source_target_pairs={{0,4},{4,0},{8,12},{12,8},{16,20},{20,16},{24,28},{28,24},{1,5},{5... | collective-permute-start | bytes 884744 | tf_op jit(solution)/shard_map/ppermute | solution.py:207
  42.3 32.4 %collective-permute-start.7 = (bf16[2,512,384]{2,1,0:T(8,128)(2,1)S(1)}, bf16[2,512,384]{2,1,0:T(8,128)(2,1)S(1)}, u32[]{:S(2)}, u32[]{:S(2)}) collective-permute-start(bf16[2,512,384]{2,1,0:T(8,128)(2,1)S(1)} %get-tuple-element.33), channel_id=1, source_target_pairs={{0,1},{1,0},{2,3},{3,2},{4,5},{5,4},{6,7},{7,6},{8,9},{9,8},{10,11... | collective-permute-start | bytes 2359304 | tf_op jit(solution)/shard_map/ppermute | solution.py:207
  51.0 6.3 %collective-permute-start.13 = (bf16[192,384]{1,0:T(8,128)(2,1)S(1)}, bf16[192,384]{1,0:T(8,128)(2,1)S(1)}, u32[]{:S(2)}, u32[]{:S(2)}) collective-permute-start(bf16[192,384]{1,0:T(8,128)(2,1)S(1)} %fusion.11), channel_id=1, source_target_pairs={{0,4},{4,0},{8,12},{12,8},{16,20},{20,16},{24,28},{28,24},{1,5},{5... | collective-permute-start | bytes 442376 | tf_op jit(solution)/shard_map/ppermute | solution.py:207
  51.7 6.2 %collective-permute-start.12 = (bf16[192,384]{1,0:T(8,128)(2,1)S(1)}, bf16[192,384]{1,0:T(8,128)(2,1)S(1)}, u32[]{:S(2)}, u32[]{:S(2)}) collective-permute-start(bf16[192,384]{1,0:T(8,128)(2,1)S(1)} %fusion.10), channel_id=1, source_target_pairs={{0,8},{4,12},{8,0},{12,4},{16,24},{20,28},{24,16},{28,20},{1,9},{5... | collective-permute-start | bytes 442376 | tf_op jit(solution)/shard_map/ppermute | solution.py:207
  58.0 16.7 %collective-permute-start.14 = (bf16[384,384]{1,0:T(8,128)(2,1)S(1)}, bf16[384,384]{1,0:T(8,128)(2,1)S(1)}, u32[]{:S(2)}, u32[]{:S(2)}) collective-permute-start(bf16[384,384]{1,0:T(8,128)(2,1)S(1)} %pad_maximum_fusion.1), channel_id=1, source_target_pairs={{0,16},{4,20},{8,24},{12,28},{16,0},{20,4},{24,8},{28,12},{1,17},{... | collective-permute-start | bytes 884744 | tf_op jit(solution)/shard_map/ppermute | solution.py:207
  62.5 32.1 %collective-permute-start.11 = (bf16[512,384]{1,0:T(8,128)(2,1)S(1)}, bf16[512,384]{1,0:T(8,128)(2,1)S(1)}, u32[]{:S(2)}, u32[]{:S(2)}) collective-permute-start(bf16[512,384]{1,0:T(8,128)(2,1)S(1)} %get-tuple-element.39), channel_id=1, source_target_pairs={{4,0},{12,8},{16,12},{20,16},{28,24},{5,1},{13,9},{17,13},{21,17},... | collective-permute-start | bytes 1179656 | tf_op jit(solution)/shard_map/ppermute | solution.py:221
  64.7 10.1 %collective-permute-start.15 = (bf16[512,384]{1,0:T(8,128)(2,1)S(1)}, bf16[512,384]{1,0:T(8,128)(2,1)S(1)}, u32[]{:S(2)}, u32[]{:S(2)}) collective-permute-start(bf16[512,384]{1,0:T(8,128)(2,1)S(1)} %get-tuple-element.46), channel_id=1, source_target_pairs={{16,20},{20,16},{17,21},{21,17},{18,22},{22,18},{19,23},{23,19}} | collective-permute-start | bytes 1179656 | tf_op jit(solution)/shard_map/ppermute | solution.py:221
  75.0 11.3 %collective-permute-start.19 = (bf16[192,384]{1,0:T(8,128)(2,1)S(1)}, bf16[192,384]{1,0:T(8,128)(2,1)S(1)}, u32[]{:S(2)}, u32[]{:S(2)}) collective-permute-start(bf16[192,384]{1,0:T(8,128)(2,1)S(1)} %get-tuple-element.59.refs_3_), channel_id=1, source_target_pairs={{0,4},{4,0},{8,12},{12,8},{16,20},{20,16},{24,28},{28,24},{1,5},{5... | collective-permute-start | bytes 442376 | tf_op jit(solution)/shard_map/ppermute | solution.py:207
  75.6 5.6 %collective-permute-start.18 = (bf16[192,384]{1,0:T(8,128)(2,1)S(1)}, bf16[192,384]{1,0:T(8,128)(2,1)S(1)}, u32[]{:S(2)}, u32[]{:S(2)}) collective-permute-start(bf16[192,384]{1,0:T(8,128)(2,1)S(1)} %get-tuple-element.60.refs_0_), channel_id=1, source_target_pairs={{0,8},{4,12},{8,0},{12,4},{16,24},{20,28},{24,16},{28,20},{1,9},{5... | collective-permute-start | bytes 442376 | tf_op jit(solution)/shard_map/ppermute | solution.py:207
  78.1 13.6 %collective-permute-start.17 = (bf16[512,384]{1,0:T(8,128)(2,1)S(1)}, bf16[512,384]{1,0:T(8,128)(2,1)S(1)}, u32[]{:S(2)}, u32[]{:S(2)}) collective-permute-start(bf16[512,384]{1,0:T(8,128)(2,1)S(1)} %add_convert_fusion.1), channel_id=1, source_target_pairs={{20,12},{21,13},{22,14},{23,15}} | collective-permute-start | bytes 1179656 | tf_op jit(solution)/shard_map/ppermute | solution.py:221
  79.5 12.4 %collective-permute-start.8 = (bf16[512,384]{1,0:T(8,128)(2,1)S(1)}, bf16[512,384]{1,0:T(8,128)(2,1)S(1)}, u32[]{:S(2)}, u32[]{:S(2)}) collective-permute-start(bf16[512,384]{1,0:T(8,128)(2,1)S(1)} %fusion.5), channel_id=1, source_target_pairs={{0,2},{1,3},{2,0},{3,1},{4,6},{5,7},{6,4},{7,5},{8,10},{9,11},{10,... | collective-permute-start | bytes 1179656 | tf_op jit(solution)/shard_map/ppermute | solution.py:207
  81.2 13.4 %collective-permute-start.16 = (bf16[512,384]{1,0:T(8,128)(2,1)S(1)}, bf16[512,384]{1,0:T(8,128)(2,1)S(1)}, u32[]{:S(2)}, u32[]{:S(2)}) collective-permute-start(bf16[512,384]{1,0:T(8,128)(2,1)S(1)} %add_convert_fusion.1), channel_id=1, source_target_pairs={{16,8},{17,9},{18,10},{19,11}} | collective-permute-start | bytes 1179656 | tf_op jit(solution)/shard_map/ppermute | solution.py:221
  86.3 9.6 %collective-permute-start.21 = (bf16[2,192,384]{2,1,0:T(8,128)(2,1)S(1)}, bf16[2,192,384]{2,1,0:T(8,128)(2,1)S(1)}, u32[]{:S(2)}, u32[]{:S(2)}) collective-permute-start(bf16[2,192,384]{2,1,0:T(8,128)(2,1)S(1)} %pad_maximum_fusion.2), channel_id=1, source_target_pairs={{0,4},{4,0},{8,12},{12,8},{16,20},{20,16},{24,28},{28,24},{1,5},{5... | collective-permute-start | bytes 884744 | tf_op jit(solution)/shard_map/ppermute | solution.py:207
  91.7 6.7 %collective-permute-start.22 = (bf16[2,192,384]{2,1,0:T(8,128)(2,1)S(1)}, bf16[2,192,384]{2,1,0:T(8,128)(2,1)S(1)}, u32[]{:S(2)}, u32[]{:S(2)}) collective-permute-start(bf16[2,192,384]{2,1,0:T(8,128)(2,1)S(1)} %pad_maximum_fusion.3), channel_id=1, source_target_pairs={{0,8},{4,12},{8,0},{12,4},{16,24},{20,28},{24,16},{28,20},{1,9},{5... | collective-permute-start | bytes 884744 | tf_op jit(solution)/shard_map/ppermute | solution.py:207
  91.9 12.1 %collective-permute-start.20 = (bf16[512,384]{1,0:T(8,128)(2,1)S(1)}, bf16[512,384]{1,0:T(8,128)(2,1)S(1)}, u32[]{:S(2)}, u32[]{:S(2)}) collective-permute-start(bf16[512,384]{1,0:T(8,128)(2,1)S(1)} %add_convert_fusion), channel_id=1, source_target_pairs={{4,0},{12,8},{16,12},{20,16},{28,24},{5,1},{13,9},{17,13},{21,17},... | collective-permute-start | bytes 1179656 | tf_op jit(solution)/shard_map/ppermute | solution.py:221

commit v7 on v6

--- a/solution.py
+++ b/solution.py
@@ -371,6 +371,8 @@
         key_total, value_total = both
     key_grad, value_grad = key_total.astype(BF16), value_total.astype(BF16)
 
+    if pair_plan and frames == 8:
+        attended = lax.optimization_barrier((attended, leaves))[0]
     out_keep, out_send = pl.pallas_call(
         output_kernel,
         out_shape=(

time: 105 us -> 104 us (level)
  waiting for transfers between devices: 47.4 us -> 45.2 us
  starting transfers between devices: 29.5 us -> 31 us
    ppermute x9, starting transfers between devices: 15.2 us -> 18.3 us  [send(): return lax.ppermute(array, 'tm', pairs)]
    ppermute x14, waiting for transfers between devices: 29.3 us -> 27.5 us  [swap(): lax.ppermute(array, axis, [(i, i ^ bit) for i in range(lax.axis_size(axis...]
    ppermute x14, starting transfers between devices: 14.3 us -> 12.7 us  [swap(): lax.ppermute(array, axis, [(i, i ^ bit) for i in range(lax.axis_size(axis...]
  transfers between devices with their start and end apart: 23 -> 23, of which waited for: 12 -> 11; matrix products, arithmetic and copies ran while one was open for 2% -> 2% of each run, Pallas kernels for 16% -> 16%
where the time goes in v7:
time: 104 us
  waiting for transfers between devices  45.2 us (43%)
  starting transfers between devices  31 us (30%)
  Pallas kernels  22 us (21%)
  other arithmetic  4.52 us (4%)
    ppermute x14, waiting for transfers between devices, swap(): lax.ppermute(array, axis, [(i, i ^ bit) for i in range(lax.axis_size(axis...  27.5 us
    ppermute x9, starting transfers between devices, send(): return lax.ppermute(array, 'tm', pairs)  18.3 us
    ppermute x9, waiting for transfers between devices, send(): return lax.ppermute(array, 'tm', pairs)  17.6 us
    ppermute x14, starting transfers between devices, swap(): lax.ppermute(array, axis, [(i, i ^ bit) for i in range(lax.axis_size(axis...  12.7 us
    pallas_call x1, Pallas kernels, local(): pl.pallas_call(functools.partial(backward_kernel, count, far_frames[0] if...  8.46 us
    pallas_call x1, Pallas kernels, local(): pl.pallas_call(functools.partial(far_kernel, count), grid=(heads,), out_s...  5.15 us
    pallas_call x1, Pallas kernels, local(): pl.pallas_call(near_kernel, grid=(heads,), out_shape=(part_shape, stat_sh...  4.51 us
  transfers between devices with their start and end apart: 23, of which 11 were waited for; matrix products, arithmetic and copies ran while one was open for 2% of the time, Pallas kernels for 16%

profile of v7, /device:TPU:12, one launch (start us, length us, event | category | flops | bytes accessed | tf_op | source)
XLA Modules:
  0.0 104.0 jit_solution(8767364817206034560)
XLA Ops:
  0.7 1.3 %pad_maximum_fusion = bf16[2,512,384]{2,1,0:T(8,128)(2,1)S(1)} fusion(bf16[1,512,384]{2,1,0:T(8,128)(2,1)} %bitcast.45, bf16[1,512,384]{2,1,0:T(8,128)(2,1)} %bitcast.44), kind=kLoop, calls=%fused_computation.5 | loop fusion | flops 393216 | bytes 1572864 | tf_op jit(solution)/shard_map/stack | solution.py:226
  2.0 3.6 %collective-permute-start = (bf16[2,512,384]{2,1,0:T(8,128)(2,1)S(1)}, bf16[2,512,384]{2,1,0:T(8,128)(2,1)S(1)}, u32[]{:S(2)}, u32[]{:S(2)}) collective-permute-start(bf16[2,512,384]{2,1,0:T(8,128)(2,1)S(1)} %pad_maximum_fusion), channel_id=1, source_target_pairs={{0,4},{8,12},{12,16},{16,20},{24,28},{1,5},{9,13},{13,17},{17,21},... | collective-permute-start | bytes 2359304 | tf_op jit(solution)/shard_map/ppermute | solution.py:221
  5.6 1.6 %collective-permute-start.5 = (bf16[512,384]{1,0:T(8,128)(2,1)S(1)}, bf16[512,384]{1,0:T(8,128)(2,1)S(1)}, u32[]{:S(2)}, u32[]{:S(2)}) collective-permute-start(bf16[512,384]{1,0:T(8,128)(2,1)S(1)} %copy-done.4), channel_id=1, source_target_pairs={{0,2},{1,3},{2,0},{3,1},{4,6},{5,7},{6,4},{7,5},{8,10},{9,11},{10,... | collective-permute-start | bytes 1179656 | tf_op jit(solution)/shard_map/ppermute | solution.py:207
  7.1 0.7 collective-permute-start.1
  7.9 0.1 collective-permute-start.4
  7.9 0.7 collective-permute-start.2
  8.6 7.6 %collective-permute-done.5.third.rest_8_ = bf16[512,384]{1,0:T(8,128)(2,1)S(1)} collective-permute-done((bf16[512,384]{1,0:T(8,128)(2,1)S(1)}, bf16[512,384]{1,0:T(8,128)(2,1)S(1)}, u32[]{:S(2)}, u32[]{:S(2)}) %collective-permute-start.5) | collective-permute-done | bytes 393248 | tf_op jit(solution)/shard_map/ppermute | solution.py:207
  16.2 7.1 %collective-permute-done.prev = bf16[2,512,384]{2,1,0:T(8,128)(2,1)S(1)} collective-permute-done((bf16[2,512,384]{2,1,0:T(8,128)(2,1)S(1)}, bf16[2,512,384]{2,1,0:T(8,128)(2,1)S(1)}, u32[]{:S(2)}, u32[]{:S(2)}) %collective-permute-start) | collective-permute-done | bytes 786464 | tf_op jit(solution)/shard_map/ppermute | solution.py:221
  23.4 3.5 %collective-permute-start.3 = (bf16[512,384]{1,0:T(8,128)(2,1)S(1)}, bf16[512,384]{1,0:T(8,128)(2,1)S(1)}, u32[]{:S(2)}, u32[]{:S(2)}) collective-permute-start(bf16[512,384]{1,0:T(8,128)(2,1)S(1)} %slice_bitcast_fusion.1), channel_id=1, source_target_pairs={{12,20},{13,21},{14,22},{15,23}} | collective-permute-start | bytes 1179656 | tf_op jit(solution)/shard_map/ppermute | solution.py:221
  26.9 4.5 %near.1 = (f32[3,128,512]{2,1,0:T(8,128)S(1)}, f32[3,8,512]{2,1,0:T(8,128)S(1)}) custom-call(s32[8]{0:T(128)S(1)} %copy-done.5, bf16[512,384]{1,0:T(8,128)(2,1)S(1)} %copy-done.3, bf16[512,384]{1,0:T(8,128)(2,1)S(1)} %copy-done, bf16[512,384]{1,0:T(8,128)(2,1)S(1)} %copy-done.1, bf16[2,512,384]{2,1,0:T(8,128)(2,1)S(1)} %collective-permute-done.prev), custom_call_target="tpu_custom_call" | custom-call | tf_op jit(solution)/shard_map/near/pallas_call | solution.py:271
  31.5 1.1 %cotangent.1.rest_5_.rest_3_ = bf16[512,384]{1,0:T(8,128)(2,1)S(1)} custom-call(bf16[512,384]{1,0:T(8,128)(2,1)S(1)} %copy-done.4, bf16[512,384]{1,0:T(8,128)(2,1)S(1)} %collective-permute-done.4.second.rest_7_, bf16[512,384]{1,0:T(8,128)(2,1)S(1)} %collective-permute-done.5.third.rest_8_, bf16[512,384]{1,0:T(8,128)(2,1)S(1)} %collective-permute-done.6.fourth.rest_9_, ...), custom_call_target="tpu_custom_call" | custom-call | tf_op jit(solution)/shard_map/cotangent/pallas_call | solution.py:250
  32.6 1.7 %collective-permute-done.3.rest_2_ = bf16[512,384]{1,0:T(8,128)(2,1)S(1)} collective-permute-done((bf16[512,384]{1,0:T(8,128)(2,1)S(1)}, bf16[512,384]{1,0:T(8,128)(2,1)S(1)}, u32[]{:S(2)}, u32[]{:S(2)}) %collective-permute-start.3) | collective-permute-done | bytes 393248 | tf_op jit(solution)/shard_map/ppermute | solution.py:221
  34.3 5.1 %far.1 = (bf16[512,384]{1,0:T(8,128)(2,1)S(1)}, f32[3,8,512]{2,1,0:T(8,128)S(1)}, f32[2,384,384]{2,1,0:T(8,128)S(1)}, bf16[2,384,384]{2,1,0:T(8,128)(2,1)S(1)}) custom-call(s32[8]{0:T(128)S(1)} %copy-done.5, bf16[512,384]{1,0:T(8,128)(2,1)S(1)} %copy-done.3, bf16[512,384]{1,0:T(8,128)(2,1)S(1)} %copy-done, bf16[512,384]{1,0:T(8,128)(2,1)S(1)} %copy-done.1, ...), custom_call_target="tpu_custom_call" | custom-call | tf_op jit(solution)/shard_map/far/pallas_call | solution.py:283
  39.5 0.1 fusion.12
  39.6 0.1 collective-permute-start.8
  39.6 1.5 %collective-permute-start.7 = (bf16[2,192,384]{2,1,0:T(8,128)(2,1)S(1)}, bf16[2,192,384]{2,1,0:T(8,128)(2,1)S(1)}, u32[]{:S(2)}, u32[]{:S(2)}) collective-permute-start(bf16[2,192,384]{2,1,0:T(8,128)(2,1)S(1)} %get-tuple-element.58), channel_id=1, source_target_pairs={{0,4},{4,0},{8,12},{12,8},{16,20},{20,16},{24,28},{28,24},{1,5},{5... | collective-permute-start | bytes 884744 | tf_op jit(solution)/shard_map/ppermute | solution.py:207
  41.2 8.5 %backward.1 = (bf16[512,384]{1,0:T(8,128)(2,1)}, f32[2,512,384]{2,1,0:T(8,128)S(1)}, bf16[512,384]{1,0:T(8,128)(2,1)S(1)}, bf16[512,384]{1,0:T(8,128)(2,1)S(1)},...) custom-call(s32[8]{0:T(128)S(1)} %copy-done.5, bf16[512,384]{1,0:T(8,128)(2,1)S(1)} %copy-done.3, ...), custom_call_target="tpu_custom_call" | custom-call | tf_op jit(solution)/shard_map/backward/pallas_call | solution.py:299
  49.6 0.1 convert_add_fusion.2
  49.8 0.6 collective-permute-start.10
  50.4 2.0 %collective-permute-start.9 = (bf16[192,384]{1,0:T(8,128)(2,1)S(1)}, bf16[192,384]{1,0:T(8,128)(2,1)S(1)}, u32[]{:S(2)}, u32[]{:S(2)}) collective-permute-start(bf16[192,384]{1,0:T(8,128)(2,1)S(1)} %fusion.10), channel_id=1, source_target_pairs={{0,8},{4,12},{8,0},{12,4},{16,24},{20,28},{24,16},{28,20},{1,9},{5... | collective-permute-start | bytes 442376 | tf_op jit(solution)/shard_map/ppermute | solution.py:207
  52.4 2.5 %collective-permute-done.10 = bf16[192,384]{1,0:T(8,128)(2,1)S(1)} collective-permute-done((bf16[192,384]{1,0:T(8,128)(2,1)S(1)}, bf16[192,384]{1,0:T(8,128)(2,1)S(1)}, u32[]{:S(2)}, u32[]{:S(2)}) %collective-permute-start.10) | collective-permute-done | bytes 147488 | tf_op jit(solution)/shard_map/ppermute | solution.py:207
  55.0 0.6 collective-permute-done.9
  55.7 4.8 %collective-permute-start.14 = (bf16[384,384]{1,0:T(8,128)(2,1)S(1)}, bf16[384,384]{1,0:T(8,128)(2,1)S(1)}, u32[]{:S(2)}, u32[]{:S(2)}) collective-permute-start(bf16[384,384]{1,0:T(8,128)(2,1)S(1)} %pad_maximum_fusion.1), channel_id=1, source_target_pairs={{0,16},{4,20},{8,24},{12,28},{16,0},{20,4},{24,8},{28,12},{1,17},{... | collective-permute-start | bytes 884744 | tf_op jit(solution)/shard_map/ppermute | solution.py:207
  60.5 0.7 collective-permute-start.15
  61.2 1.1 %output.1 = (f32[2,512,384]{2,1,0:T(8,128)S(1)}, bf16[2,512,384]{2,1,0:T(8,128)(2,1)S(1)}) custom-call(bf16[512,384]{1,0:T(8,128)(2,1)S(1)} %get-tuple-element.41.attended, bf16[384,1536]{1,0:T(8,128)(2,1)S(1)} %copy-done.2), custom_call_target="tpu_custom_call" | custom-call | tf_op jit(solution)/shard_map/output/pallas_call | solution.py:376
  62.3 0.1 collective-permute-start.11
  62.4 7.3 %collective-permute-done.14 = bf16[384,384]{1,0:T(8,128)(2,1)S(1)} collective-permute-done((bf16[384,384]{1,0:T(8,128)(2,1)S(1)}, bf16[384,384]{1,0:T(8,128)(2,1)S(1)}, u32[]{:S(2)}, u32[]{:S(2)}) %collective-permute-start.14) | collective-permute-done | bytes 294944 | tf_op jit(solution)/shard_map/ppermute | solution.py:207
  69.7 0.1 add_convert_fusion.2
  69.8 0.1 add_convert_fusion.1
  69.9 1.3 %collective-permute-start.17 = (bf16[512,384]{1,0:T(8,128)(2,1)S(1)}, bf16[512,384]{1,0:T(8,128)(2,1)S(1)}, u32[]{:S(2)}, u32[]{:S(2)}) collective-permute-start(bf16[512,384]{1,0:T(8,128)(2,1)S(1)} %add_convert_fusion.1), channel_id=1, source_target_pairs={{20,12},{21,13},{22,14},{23,15}} | collective-permute-start | bytes 1179656 | tf_op jit(solution)/shard_map/ppermute | solution.py:221
  71.3 0.8 collective-permute-start.18
  72.0 0.6 collective-permute-start.19
  72.7 3.3 %collective-permute-start.13 = (bf16[512,384]{1,0:T(8,128)(2,1)S(1)}, bf16[512,384]{1,0:T(8,128)(2,1)S(1)}, u32[]{:S(2)}, u32[]{:S(2)}) collective-permute-start(bf16[512,384]{1,0:T(8,128)(2,1)S(1)} %get-tuple-element.46), channel_id=1, source_target_pairs={{4,0},{12,8},{16,12},{20,16},{28,24},{5,1},{13,9},{17,13},{21,17},... | collective-permute-start | bytes 1179656 | tf_op jit(solution)/shard_map/ppermute | solution.py:221
  76.0 0.5 collective-permute-done.18.refs_1_
  76.5 0.7 collective-permute-start.16
  77.2 5.9 %collective-permute-done.19.refs_4_ = bf16[192,384]{1,0:T(8,128)(2,1)S(1)} collective-permute-done((bf16[192,384]{1,0:T(8,128)(2,1)S(1)}, bf16[192,384]{1,0:T(8,128)(2,1)S(1)}, u32[]{:S(2)}, u32[]{:S(2)}) %collective-permute-start.19) | collective-permute-done | bytes 147488 | tf_op jit(solution)/shard_map/ppermute | solution.py:207
  83.2 0.1 collective-permute-start.22
  83.3 0.1 add_convert_fusion
  83.4 3.9 %collective-permute-start.20 = (bf16[512,384]{1,0:T(8,128)(2,1)S(1)}, bf16[512,384]{1,0:T(8,128)(2,1)S(1)}, u32[]{:S(2)}, u32[]{:S(2)}) collective-permute-start(bf16[512,384]{1,0:T(8,128)(2,1)S(1)} %add_convert_fusion), channel_id=1, source_target_pairs={{4,0},{12,8},{16,12},{20,16},{28,24},{5,1},{13,9},{17,13},{21,17},... | collective-permute-start | bytes 1179656 | tf_op jit(solution)/shard_map/ppermute | solution.py:221
  87.3 0.1 convert_add_fusion
  87.5 0.5 collective-permute-done.13
  88.1 0.5 collective-permute-start.12
  88.6 0.9 fusion.4
  89.5 3.0 %collective-permute-done.21.refs_2_ = bf16[2,192,384]{2,1,0:T(8,128)(2,1)S(1)} collective-permute-done((bf16[2,192,384]{2,1,0:T(8,128)(2,1)S(1)}, bf16[2,192,384]{2,1,0:T(8,128)(2,1)S(1)}, u32[]{:S(2)}, u32[]{:S(2)}) %collective-permute-start.21) | collective-permute-done | bytes 294944 | tf_op jit(solution)/shard_map/ppermute | solution.py:207
  92.5 1.6 %assemble.1 = f32[384,1536]{1,0:T(8,128)} custom-call(bf16[192,384]{1,0:T(8,128)(2,1)S(1)} %get-tuple-element.62.refs_0_, bf16[192,384]{1,0:T(8,128)(2,1)S(1)} %collective-permute-done.18.refs_1_, bf16[2,192,384]{2,1,0:T(8,128)(2,1)S(1)} %collective-permute-done.21.refs_2_, bf16[192,384]{1,0:T(8,128)(2,1)S(1)} %get-tuple-element.61.refs_3_, ...), custom_call_target="tpu_custom_call" | custom-call | tf_op jit(solution)/shard_map/assemble/pallas_call | solution.py:336
  94.1 8.3 %collective-permute-done.20 = bf16[512,384]{1,0:T(8,128)(2,1)S(1)} collective-permute-done((bf16[512,384]{1,0:T(8,128)(2,1)S(1)}, bf16[512,384]{1,0:T(8,128)(2,1)S(1)}, u32[]{:S(2)}, u32[]{:S(2)}) %collective-permute-start.20) | collective-permute-done | bytes 393248 | tf_op jit(solution)/shard_map/ppermute | solution.py:221
  102.4 0.8 fusion.2
  103.2 0.8 fusion.1
  (36 shorter events, 0.4 us)
Async XLA Ops:
  0.6 26.2 %copy-start.1 = (bf16[512,384]{1,0:T(8,128)(2,1)S(1)}, bf16[512,384]{1,0:T(8,128)(2,1)}, u32[]{:S(2)}) copy-start(bf16[512,384]{1,0:T(8,128)(2,1)} %v.5) | copy-start | bytes 1179652
  0.6 7.3 %copy-start = (bf16[512,384]{1,0:T(8,128)(2,1)S(1)}, bf16[512,384]{1,0:T(8,128)(2,1)}, u32[]{:S(2)}) copy-start(bf16[512,384]{1,0:T(8,128)(2,1)} %k.5) | copy-start | bytes 1179652
  0.7 4.9 %copy-start.4 = (bf16[512,384]{1,0:T(8,128)(2,1)S(1)}, bf16[512,384]{1,0:T(8,128)(2,1)}, u32[]{:S(2)}) copy-start(bf16[512,384]{1,0:T(8,128)(2,1)} %rest_6_.1) | copy-start | bytes 1179652
  0.7 26.2 %copy-start.5 = (s32[8]{0:T(128)S(1)}, s32[8]{0:T(128)}, u32[]{:S(2)}) copy-start(s32[8]{0:T(128)} %anchor.5) | copy-start | bytes 100
  0.7 26.2 %copy-start.3 = (bf16[512,384]{1,0:T(8,128)(2,1)S(1)}, bf16[512,384]{1,0:T(8,128)(2,1)}, u32[]{:S(2)}) copy-start(bf16[512,384]{1,0:T(8,128)(2,1)} %q.5) | copy-start | bytes 1179652
  2.0 29.4 %copy-start.2 = (bf16[384,1536]{1,0:T(8,128)(2,1)S(1)}, bf16[384,1536]{1,0:T(8,128)(2,1)}, u32[]{:S(2)}) copy-start(bf16[384,1536]{1,0:T(8,128)(2,1)} %weight.3) | copy-start | bytes 3538948
  2.0 21.3 %collective-permute-start = (bf16[2,512,384]{2,1,0:T(8,128)(2,1)S(1)}, bf16[2,512,384]{2,1,0:T(8,128)(2,1)S(1)}, u32[]{:S(2)}, u32[]{:S(2)}) collective-permute-start(bf16[2,512,384]{2,1,0:T(8,128)(2,1)S(1)} %pad_maximum_fusion), channel_id=1, source_target_pairs={{0,4},{8,12},{12,16},{16,20},{24,28},{1,5},{9,13},{13,17},{17,21},... | collective-permute-start | bytes 2359304 | tf_op jit(solution)/shard_map/ppermute | solution.py:221
  5.6 10.6 %collective-permute-start.5 = (bf16[512,384]{1,0:T(8,128)(2,1)S(1)}, bf16[512,384]{1,0:T(8,128)(2,1)S(1)}, u32[]{:S(2)}, u32[]{:S(2)}) collective-permute-start(bf16[512,384]{1,0:T(8,128)(2,1)S(1)} %copy-done.4), channel_id=1, source_target_pairs={{0,2},{1,3},{2,0},{3,1},{4,6},{5,7},{6,4},{7,5},{8,10},{9,11},{10,... | collective-permute-start | bytes 1179656 | tf_op jit(solution)/shard_map/ppermute | solution.py:207
  7.1 25.5 %collective-permute-start.1 = (bf16[2,512,384]{2,1,0:T(8,128)(2,1)S(1)}, bf16[2,512,384]{2,1,0:T(8,128)(2,1)S(1)}, u32[]{:S(2)}, u32[]{:S(2)}) collective-permute-start(bf16[2,512,384]{2,1,0:T(8,128)(2,1)S(1)} %pad_maximum_fusion), channel_id=1, source_target_pairs={{8,16},{9,17},{10,18},{11,19}} | collective-permute-start | bytes 2359304 | tf_op jit(solution)/shard_map/ppermute | solution.py:221
  7.9 23.6 %collective-permute-start.4 = (bf16[512,384]{1,0:T(8,128)(2,1)S(1)}, bf16[512,384]{1,0:T(8,128)(2,1)S(1)}, u32[]{:S(2)}, u32[]{:S(2)}) collective-permute-start(bf16[512,384]{1,0:T(8,128)(2,1)S(1)} %copy-done.4), channel_id=1, source_target_pairs={{0,1},{1,0},{2,3},{3,2},{4,5},{5,4},{6,7},{7,6},{8,9},{9,8},{10,11... | collective-permute-start | bytes 1179656 | tf_op jit(solution)/shard_map/ppermute | solution.py:207
  7.9 24.7 %collective-permute-start.2 = (bf16[512,384]{1,0:T(8,128)(2,1)S(1)}, bf16[512,384]{1,0:T(8,128)(2,1)S(1)}, u32[]{:S(2)}, u32[]{:S(2)}) collective-permute-start(bf16[512,384]{1,0:T(8,128)(2,1)S(1)} %copy-done), channel_id=1, source_target_pairs={{8,20},{9,21},{10,22},{11,23}} | collective-permute-start | bytes 1179656 | tf_op jit(solution)/shard_map/ppermute | solution.py:221
  16.2 15.2 %collective-permute-start.6 = (bf16[512,384]{1,0:T(8,128)(2,1)S(1)}, bf16[512,384]{1,0:T(8,128)(2,1)S(1)}, u32[]{:S(2)}, u32[]{:S(2)}) collective-permute-start(bf16[512,384]{1,0:T(8,128)(2,1)S(1)} %collective-permute-done.5.third.rest_8_), channel_id=1, source_target_pairs={{0,1},{1,0},{2,3},{3,2},{4,5},{5,4},{6,7},{7,6},{8,9},{9,8},{10,11... | collective-permute-start | bytes 1179656 | tf_op jit(solution)/shard_map/ppermute | solution.py:207
  23.4 11.0 %collective-permute-start.3 = (bf16[512,384]{1,0:T(8,128)(2,1)S(1)}, bf16[512,384]{1,0:T(8,128)(2,1)S(1)}, u32[]{:S(2)}, u32[]{:S(2)}) collective-permute-start(bf16[512,384]{1,0:T(8,128)(2,1)S(1)} %slice_bitcast_fusion.1), channel_id=1, source_target_pairs={{12,20},{13,21},{14,22},{15,23}} | collective-permute-start | bytes 1179656 | tf_op jit(solution)/shard_map/ppermute | solution.py:221
  39.6 10.1 %collective-permute-start.8 = (bf16[2,192,384]{2,1,0:T(8,128)(2,1)S(1)}, bf16[2,192,384]{2,1,0:T(8,128)(2,1)S(1)}, u32[]{:S(2)}, u32[]{:S(2)}) collective-permute-start(bf16[2,192,384]{2,1,0:T(8,128)(2,1)S(1)} %get-tuple-element.57), channel_id=1, source_target_pairs={{0,8},{4,12},{8,0},{12,4},{16,24},{20,28},{24,16},{28,20},{1,9},{5... | collective-permute-start | bytes 884744 | tf_op jit(solution)/shard_map/ppermute | solution.py:207
  39.6 10.0 %collective-permute-start.7 = (bf16[2,192,384]{2,1,0:T(8,128)(2,1)S(1)}, bf16[2,192,384]{2,1,0:T(8,128)(2,1)S(1)}, u32[]{:S(2)}, u32[]{:S(2)}) collective-permute-start(bf16[2,192,384]{2,1,0:T(8,128)(2,1)S(1)} %get-tuple-element.58), channel_id=1, source_target_pairs={{0,4},{4,0},{8,12},{12,8},{16,20},{20,16},{24,28},{28,24},{1,5},{5... | collective-permute-start | bytes 884744 | tf_op jit(solution)/shard_map/ppermute | solution.py:207
  49.8 5.2 %collective-permute-start.10 = (bf16[192,384]{1,0:T(8,128)(2,1)S(1)}, bf16[192,384]{1,0:T(8,128)(2,1)S(1)}, u32[]{:S(2)}, u32[]{:S(2)}) collective-permute-start(bf16[192,384]{1,0:T(8,128)(2,1)S(1)} %fusion.11), channel_id=1, source_target_pairs={{0,4},{4,0},{8,12},{12,8},{16,20},{20,16},{24,28},{28,24},{1,5},{5... | collective-permute-start | bytes 442376 | tf_op jit(solution)/shard_map/ppermute | solution.py:207
  50.4 5.2 %collective-permute-start.9 = (bf16[192,384]{1,0:T(8,128)(2,1)S(1)}, bf16[192,384]{1,0:T(8,128)(2,1)S(1)}, u32[]{:S(2)}, u32[]{:S(2)}) collective-permute-start(bf16[192,384]{1,0:T(8,128)(2,1)S(1)} %fusion.10), channel_id=1, source_target_pairs={{0,8},{4,12},{8,0},{12,4},{16,24},{20,28},{24,16},{28,20},{1,9},{5... | collective-permute-start | bytes 442376 | tf_op jit(solution)/shard_map/ppermute | solution.py:207
  55.7 14.0 %collective-permute-start.14 = (bf16[384,384]{1,0:T(8,128)(2,1)S(1)}, bf16[384,384]{1,0:T(8,128)(2,1)S(1)}, u32[]{:S(2)}, u32[]{:S(2)}) collective-permute-start(bf16[384,384]{1,0:T(8,128)(2,1)S(1)} %pad_maximum_fusion.1), channel_id=1, source_target_pairs={{0,16},{4,20},{8,24},{12,28},{16,0},{20,4},{24,8},{28,12},{1,17},{... | collective-permute-start | bytes 884744 | tf_op jit(solution)/shard_map/ppermute | solution.py:207
  60.5 9.3 %collective-permute-start.15 = (bf16[512,384]{1,0:T(8,128)(2,1)S(1)}, bf16[512,384]{1,0:T(8,128)(2,1)S(1)}, u32[]{:S(2)}, u32[]{:S(2)}) collective-permute-start(bf16[512,384]{1,0:T(8,128)(2,1)S(1)} %get-tuple-element.40), channel_id=1, source_target_pairs={{16,20},{20,16},{17,21},{21,17},{18,22},{22,18},{19,23},{23,19}} | collective-permute-start | bytes 1179656 | tf_op jit(solution)/shard_map/ppermute | solution.py:221
  62.3 21.1 %collective-permute-start.11 = (bf16[2,512,384]{2,1,0:T(8,128)(2,1)S(1)}, bf16[2,512,384]{2,1,0:T(8,128)(2,1)S(1)}, u32[]{:S(2)}, u32[]{:S(2)}) collective-permute-start(bf16[2,512,384]{2,1,0:T(8,128)(2,1)S(1)} %get-tuple-element.43), channel_id=1, source_target_pairs={{0,1},{1,0},{2,3},{3,2},{4,5},{5,4},{6,7},{7,6},{8,9},{9,8},{10,11... | collective-permute-start | bytes 2359304 | tf_op jit(solution)/shard_map/ppermute | solution.py:207
  69.9 13.3 %collective-permute-start.17 = (bf16[512,384]{1,0:T(8,128)(2,1)S(1)}, bf16[512,384]{1,0:T(8,128)(2,1)S(1)}, u32[]{:S(2)}, u32[]{:S(2)}) collective-permute-start(bf16[512,384]{1,0:T(8,128)(2,1)S(1)} %add_convert_fusion.1), channel_id=1, source_target_pairs={{20,12},{21,13},{22,14},{23,15}} | collective-permute-start | bytes 1179656 | tf_op jit(solution)/shard_map/ppermute | solution.py:221
  71.3 5.2 %collective-permute-start.18 = (bf16[192,384]{1,0:T(8,128)(2,1)S(1)}, bf16[192,384]{1,0:T(8,128)(2,1)S(1)}, u32[]{:S(2)}, u32[]{:S(2)}) collective-permute-start(bf16[192,384]{1,0:T(8,128)(2,1)S(1)} %get-tuple-element.62.refs_0_), channel_id=1, source_target_pairs={{0,8},{4,12},{8,0},{12,4},{16,24},{20,28},{24,16},{28,20},{1,9},{5... | collective-permute-start | bytes 442376 | tf_op jit(solution)/shard_map/ppermute | solution.py:207
  72.0 11.1 %collective-permute-start.19 = (bf16[192,384]{1,0:T(8,128)(2,1)S(1)}, bf16[192,384]{1,0:T(8,128)(2,1)S(1)}, u32[]{:S(2)}, u32[]{:S(2)}) collective-permute-start(bf16[192,384]{1,0:T(8,128)(2,1)S(1)} %get-tuple-element.61.refs_3_), channel_id=1, source_target_pairs={{0,4},{4,0},{8,12},{12,8},{16,20},{20,16},{24,28},{28,24},{1,5},{5... | collective-permute-start | bytes 442376 | tf_op jit(solution)/shard_map/ppermute | solution.py:207
  72.7 15.4 %collective-permute-start.13 = (bf16[512,384]{1,0:T(8,128)(2,1)S(1)}, bf16[512,384]{1,0:T(8,128)(2,1)S(1)}, u32[]{:S(2)}, u32[]{:S(2)}) collective-permute-start(bf16[512,384]{1,0:T(8,128)(2,1)S(1)} %get-tuple-element.46), channel_id=1, source_target_pairs={{4,0},{12,8},{16,12},{20,16},{28,24},{5,1},{13,9},{17,13},{21,17},... | collective-permute-start | bytes 1179656 | tf_op jit(solution)/shard_map/ppermute | solution.py:221
  76.5 12.1 %collective-permute-start.16 = (bf16[512,384]{1,0:T(8,128)(2,1)S(1)}, bf16[512,384]{1,0:T(8,128)(2,1)S(1)}, u32[]{:S(2)}, u32[]{:S(2)}) collective-permute-start(bf16[512,384]{1,0:T(8,128)(2,1)S(1)} %add_convert_fusion.1), channel_id=1, source_target_pairs={{16,8},{17,9},{18,10},{19,11}} | collective-permute-start | bytes 1179656 | tf_op jit(solution)/shard_map/ppermute | solution.py:221
  83.2 9.3 %collective-permute-start.21 = (bf16[2,192,384]{2,1,0:T(8,128)(2,1)S(1)}, bf16[2,192,384]{2,1,0:T(8,128)(2,1)S(1)}, u32[]{:S(2)}, u32[]{:S(2)}) collective-permute-start(bf16[2,192,384]{2,1,0:T(8,128)(2,1)S(1)} %pad_maximum_fusion.2), channel_id=1, source_target_pairs={{0,4},{4,0},{8,12},{12,8},{16,20},{20,16},{24,28},{28,24},{1,5},{5... | collective-permute-start | bytes 884744 | tf_op jit(solution)/shard_map/ppermute | solution.py:207
  83.2 9.3 %collective-permute-start.22 = (bf16[2,192,384]{2,1,0:T(8,128)(2,1)S(1)}, bf16[2,192,384]{2,1,0:T(8,128)(2,1)S(1)}, u32[]{:S(2)}, u32[]{:S(2)}) collective-permute-start(bf16[2,192,384]{2,1,0:T(8,128)(2,1)S(1)} %pad_maximum_fusion.3), channel_id=1, source_target_pairs={{0,8},{4,12},{8,0},{12,4},{16,24},{20,28},{24,16},{28,20},{1,9},{5... | collective-permute-start | bytes 884744 | tf_op jit(solution)/shard_map/ppermute | solution.py:207
  83.4 19.0 %collective-permute-start.20 = (bf16[512,384]{1,0:T(8,128)(2,1)S(1)}, bf16[512,384]{1,0:T(8,128)(2,1)S(1)}, u32[]{:S(2)}, u32[]{:S(2)}) collective-permute-start(bf16[512,384]{1,0:T(8,128)(2,1)S(1)} %add_convert_fusion), channel_id=1, source_target_pairs={{4,0},{12,8},{16,12},{20,16},{28,24},{5,1},{13,9},{17,13},{21,17},... | collective-permute-start | bytes 1179656 | tf_op jit(solution)/shard_map/ppermute | solution.py:221
  88.1 15.1 %collective-permute-start.12 = (bf16[512,384]{1,0:T(8,128)(2,1)S(1)}, bf16[512,384]{1,0:T(8,128)(2,1)S(1)}, u32[]{:S(2)}, u32[]{:S(2)}) collective-permute-start(bf16[512,384]{1,0:T(8,128)(2,1)S(1)} %fusion.5), channel_id=1, source_target_pairs={{0,2},{1,3},{2,0},{3,1},{4,6},{5,7},{6,4},{7,5},{8,10},{9,11},{10,... | collective-permute-start | bytes 1179656 | tf_op jit(solution)/shard_map/ppermute | solution.py:207

commit v8 on v7

--- a/solution.py
+++ b/solution.py
@@ -348,7 +348,7 @@
         home_k = send(merged, [(lower, source)]).astype(F32)
         home_v = send(merged, [(upper, source + 1)])
         if frames == 8:
-            home_v = lax.optimization_barrier((home_v, other_a, other_b))[0]
+            home_v = lax.optimization_barrier((home_v, other_a))[0]
         from_v = send((near_dv.astype(F32) + home_v.astype(F32)).astype(BF16), back(near_pairs))
         key_total = own_grad[0] + from_k.astype(F32) + home_k
         key_total, from_v = lax.optimization_barrier((key_total.astype(BF16), from_v))

time: 104 us -> 104 us (level)
  no operation moved by 1% of the time
where the time goes in v8:
time: 104 us
  waiting for transfers between devices  45.2 us (43%)
  starting transfers between devices  31 us (30%)
  Pallas kernels  22 us (21%)
  other arithmetic  4.52 us (4%)
    ppermute x14, waiting for transfers between devices, swap(): lax.ppermute(array, axis, [(i, i ^ bit) for i in range(lax.axis_size(axis...  27.5 us
    ppermute x9, starting transfers between devices, send(): return lax.ppermute(array, 'tm', pairs)  18.3 us
    ppermute x9, waiting for transfers between devices, send(): return lax.ppermute(array, 'tm', pairs)  17.6 us
    ppermute x14, starting transfers between devices, swap(): lax.ppermute(array, axis, [(i, i ^ bit) for i in range(lax.axis_size(axis...  12.7 us
    pallas_call x1, Pallas kernels, local(): pl.pallas_call(functools.partial(backward_kernel, count, far_frames[0] if...  8.46 us
    pallas_call x1, Pallas kernels, local(): pl.pallas_call(functools.partial(far_kernel, count), grid=(heads,), out_s...  5.15 us
    pallas_call x1, Pallas kernels, local(): pl.pallas_call(near_kernel, grid=(heads,), out_shape=(part_shape, stat_sh...  4.51 us
  transfers between devices with their start and end apart: 23, of which 11 were waited for; matrix products, arithmetic and copies ran while one was open for 2% of the time, Pallas kernels for 16%

profile of v8, /device:TPU:12, one launch (start us, length us, event | category | flops | bytes accessed | tf_op | source)
XLA Modules:
  0.0 104.0 jit_solution(8767364817206034560)
XLA Ops:
  0.7 1.3 %pad_maximum_fusion = bf16[2,512,384]{2,1,0:T(8,128)(2,1)S(1)} fusion(bf16[1,512,384]{2,1,0:T(8,128)(2,1)} %bitcast.45, bf16[1,512,384]{2,1,0:T(8,128)(2,1)} %bitcast.44), kind=kLoop, calls=%fused_computation.5 | loop fusion | flops 393216 | bytes 1572864 | tf_op jit(solution)/shard_map/stack | solution.py:226
  2.0 3.6 %collective-permute-start = (bf16[2,512,384]{2,1,0:T(8,128)(2,1)S(1)}, bf16[2,512,384]{2,1,0:T(8,128)(2,1)S(1)}, u32[]{:S(2)}, u32[]{:S(2)}) collective-permute-start(bf16[2,512,384]{2,1,0:T(8,128)(2,1)S(1)} %pad_maximum_fusion), channel_id=1, source_target_pairs={{0,4},{8,12},{12,16},{16,20},{24,28},{1,5},{9,13},{13,17},{17,21},... | collective-permute-start | bytes 2359304 | tf_op jit(solution)/shard_map/ppermute | solution.py:221
  5.6 1.6 %collective-permute-start.5 = (bf16[512,384]{1,0:T(8,128)(2,1)S(1)}, bf16[512,384]{1,0:T(8,128)(2,1)S(1)}, u32[]{:S(2)}, u32[]{:S(2)}) collective-permute-start(bf16[512,384]{1,0:T(8,128)(2,1)S(1)} %copy-done.4), channel_id=1, source_target_pairs={{0,2},{1,3},{2,0},{3,1},{4,6},{5,7},{6,4},{7,5},{8,10},{9,11},{10,... | collective-permute-start | bytes 1179656 | tf_op jit(solution)/shard_map/ppermute | solution.py:207
  7.1 0.7 collective-permute-start.1
  7.9 0.1 collective-permute-start.4
  7.9 0.7 collective-permute-start.2
  8.6 7.6 %collective-permute-done.5.third.rest_8_ = bf16[512,384]{1,0:T(8,128)(2,1)S(1)} collective-permute-done((bf16[512,384]{1,0:T(8,128)(2,1)S(1)}, bf16[512,384]{1,0:T(8,128)(2,1)S(1)}, u32[]{:S(2)}, u32[]{:S(2)}) %collective-permute-start.5) | collective-permute-done | bytes 393248 | tf_op jit(solution)/shard_map/ppermute | solution.py:207
  16.2 7.1 %collective-permute-done.prev = bf16[2,512,384]{2,1,0:T(8,128)(2,1)S(1)} collective-permute-done((bf16[2,512,384]{2,1,0:T(8,128)(2,1)S(1)}, bf16[2,512,384]{2,1,0:T(8,128)(2,1)S(1)}, u32[]{:S(2)}, u32[]{:S(2)}) %collective-permute-start) | collective-permute-done | bytes 786464 | tf_op jit(solution)/shard_map/ppermute | solution.py:221
  23.4 3.5 %collective-permute-start.3 = (bf16[512,384]{1,0:T(8,128)(2,1)S(1)}, bf16[512,384]{1,0:T(8,128)(2,1)S(1)}, u32[]{:S(2)}, u32[]{:S(2)}) collective-permute-start(bf16[512,384]{1,0:T(8,128)(2,1)S(1)} %slice_bitcast_fusion.1), channel_id=1, source_target_pairs={{12,20},{13,21},{14,22},{15,23}} | collective-permute-start | bytes 1179656 | tf_op jit(solution)/shard_map/ppermute | solution.py:221
  26.9 4.5 %near.1 = (f32[3,128,512]{2,1,0:T(8,128)S(1)}, f32[3,8,512]{2,1,0:T(8,128)S(1)}) custom-call(s32[8]{0:T(128)S(1)} %copy-done.5, bf16[512,384]{1,0:T(8,128)(2,1)S(1)} %copy-done.3, bf16[512,384]{1,0:T(8,128)(2,1)S(1)} %copy-done, bf16[512,384]{1,0:T(8,128)(2,1)S(1)} %copy-done.1, bf16[2,512,384]{2,1,0:T(8,128)(2,1)S(1)} %collective-permute-done.prev), custom_call_target="tpu_custom_call" | custom-call | tf_op jit(solution)/shard_map/near/pallas_call | solution.py:271
  31.5 1.1 %cotangent.1.rest_5_.rest_3_ = bf16[512,384]{1,0:T(8,128)(2,1)S(1)} custom-call(bf16[512,384]{1,0:T(8,128)(2,1)S(1)} %copy-done.4, bf16[512,384]{1,0:T(8,128)(2,1)S(1)} %collective-permute-done.4.second.rest_7_, bf16[512,384]{1,0:T(8,128)(2,1)S(1)} %collective-permute-done.5.third.rest_8_, bf16[512,384]{1,0:T(8,128)(2,1)S(1)} %collective-permute-done.6.fourth.rest_9_, ...), custom_call_target="tpu_custom_call" | custom-call | tf_op jit(solution)/shard_map/cotangent/pallas_call | solution.py:250
  32.6 1.7 %collective-permute-done.3.rest_2_ = bf16[512,384]{1,0:T(8,128)(2,1)S(1)} collective-permute-done((bf16[512,384]{1,0:T(8,128)(2,1)S(1)}, bf16[512,384]{1,0:T(8,128)(2,1)S(1)}, u32[]{:S(2)}, u32[]{:S(2)}) %collective-permute-start.3) | collective-permute-done | bytes 393248 | tf_op jit(solution)/shard_map/ppermute | solution.py:221
  34.3 5.1 %far.1 = (bf16[512,384]{1,0:T(8,128)(2,1)S(1)}, f32[3,8,512]{2,1,0:T(8,128)S(1)}, f32[2,384,384]{2,1,0:T(8,128)S(1)}, bf16[2,384,384]{2,1,0:T(8,128)(2,1)S(1)}) custom-call(s32[8]{0:T(128)S(1)} %copy-done.5, bf16[512,384]{1,0:T(8,128)(2,1)S(1)} %copy-done.3, bf16[512,384]{1,0:T(8,128)(2,1)S(1)} %copy-done, bf16[512,384]{1,0:T(8,128)(2,1)S(1)} %copy-done.1, ...), custom_call_target="tpu_custom_call" | custom-call | tf_op jit(solution)/shard_map/far/pallas_call | solution.py:283
  39.5 0.1 fusion.12
  39.6 0.1 collective-permute-start.8
  39.6 1.5 %collective-permute-start.7 = (bf16[2,192,384]{2,1,0:T(8,128)(2,1)S(1)}, bf16[2,192,384]{2,1,0:T(8,128)(2,1)S(1)}, u32[]{:S(2)}, u32[]{:S(2)}) collective-permute-start(bf16[2,192,384]{2,1,0:T(8,128)(2,1)S(1)} %get-tuple-element.58), channel_id=1, source_target_pairs={{0,4},{4,0},{8,12},{12,8},{16,20},{20,16},{24,28},{28,24},{1,5},{5... | collective-permute-start | bytes 884744 | tf_op jit(solution)/shard_map/ppermute | solution.py:207
  41.2 8.5 %backward.1 = (bf16[512,384]{1,0:T(8,128)(2,1)}, f32[2,512,384]{2,1,0:T(8,128)S(1)}, bf16[512,384]{1,0:T(8,128)(2,1)S(1)}, bf16[512,384]{1,0:T(8,128)(2,1)S(1)},...) custom-call(s32[8]{0:T(128)S(1)} %copy-done.5, bf16[512,384]{1,0:T(8,128)(2,1)S(1)} %copy-done.3, ...), custom_call_target="tpu_custom_call" | custom-call | tf_op jit(solution)/shard_map/backward/pallas_call | solution.py:299
  49.6 0.1 convert_add_fusion.2
  49.8 0.6 collective-permute-start.10
  50.4 2.0 %collective-permute-start.9 = (bf16[192,384]{1,0:T(8,128)(2,1)S(1)}, bf16[192,384]{1,0:T(8,128)(2,1)S(1)}, u32[]{:S(2)}, u32[]{:S(2)}) collective-permute-start(bf16[192,384]{1,0:T(8,128)(2,1)S(1)} %fusion.10), channel_id=1, source_target_pairs={{0,8},{4,12},{8,0},{12,4},{16,24},{20,28},{24,16},{28,20},{1,9},{5... | collective-permute-start | bytes 442376 | tf_op jit(solution)/shard_map/ppermute | solution.py:207
  52.4 2.5 %collective-permute-done.10 = bf16[192,384]{1,0:T(8,128)(2,1)S(1)} collective-permute-done((bf16[192,384]{1,0:T(8,128)(2,1)S(1)}, bf16[192,384]{1,0:T(8,128)(2,1)S(1)}, u32[]{:S(2)}, u32[]{:S(2)}) %collective-permute-start.10) | collective-permute-done | bytes 147488 | tf_op jit(solution)/shard_map/ppermute | solution.py:207
  55.0 0.6 collective-permute-done.9
  55.7 4.8 %collective-permute-start.14 = (bf16[384,384]{1,0:T(8,128)(2,1)S(1)}, bf16[384,384]{1,0:T(8,128)(2,1)S(1)}, u32[]{:S(2)}, u32[]{:S(2)}) collective-permute-start(bf16[384,384]{1,0:T(8,128)(2,1)S(1)} %pad_maximum_fusion.1), channel_id=1, source_target_pairs={{0,16},{4,20},{8,24},{12,28},{16,0},{20,4},{24,8},{28,12},{1,17},{... | collective-permute-start | bytes 884744 | tf_op jit(solution)/shard_map/ppermute | solution.py:207
  60.5 0.7 collective-permute-start.15
  61.2 1.1 %output.1 = (f32[2,512,384]{2,1,0:T(8,128)S(1)}, bf16[2,512,384]{2,1,0:T(8,128)(2,1)S(1)}) custom-call(bf16[512,384]{1,0:T(8,128)(2,1)S(1)} %get-tuple-element.41.attended, bf16[384,1536]{1,0:T(8,128)(2,1)S(1)} %copy-done.2), custom_call_target="tpu_custom_call" | custom-call | tf_op jit(solution)/shard_map/output/pallas_call | solution.py:376
  62.3 0.1 collective-permute-start.11
  62.4 7.3 %collective-permute-done.14 = bf16[384,384]{1,0:T(8,128)(2,1)S(1)} collective-permute-done((bf16[384,384]{1,0:T(8,128)(2,1)S(1)}, bf16[384,384]{1,0:T(8,128)(2,1)S(1)}, u32[]{:S(2)}, u32[]{:S(2)}) %collective-permute-start.14) | collective-permute-done | bytes 294944 | tf_op jit(solution)/shard_map/ppermute | solution.py:207
  69.7 0.1 add_convert_fusion.2
  69.8 0.1 add_convert_fusion.1
  69.9 1.3 %collective-permute-start.17 = (bf16[512,384]{1,0:T(8,128)(2,1)S(1)}, bf16[512,384]{1,0:T(8,128)(2,1)S(1)}, u32[]{:S(2)}, u32[]{:S(2)}) collective-permute-start(bf16[512,384]{1,0:T(8,128)(2,1)S(1)} %add_convert_fusion.1), channel_id=1, source_target_pairs={{20,12},{21,13},{22,14},{23,15}} | collective-permute-start | bytes 1179656 | tf_op jit(solution)/shard_map/ppermute | solution.py:221
  71.3 0.8 collective-permute-start.18
  72.0 0.6 collective-permute-start.21
  72.7 3.3 %collective-permute-start.13 = (bf16[512,384]{1,0:T(8,128)(2,1)S(1)}, bf16[512,384]{1,0:T(8,128)(2,1)S(1)}, u32[]{:S(2)}, u32[]{:S(2)}) collective-permute-start(bf16[512,384]{1,0:T(8,128)(2,1)S(1)} %get-tuple-element.46), channel_id=1, source_target_pairs={{4,0},{12,8},{16,12},{20,16},{28,24},{5,1},{13,9},{17,13},{21,17},... | collective-permute-start | bytes 1179656 | tf_op jit(solution)/shard_map/ppermute | solution.py:221
  76.0 0.5 collective-permute-done.18.refs_1_
  76.5 0.7 collective-permute-start.16
  77.2 5.9 %collective-permute-done.21.refs_4_ = bf16[192,384]{1,0:T(8,128)(2,1)S(1)} collective-permute-done((bf16[192,384]{1,0:T(8,128)(2,1)S(1)}, bf16[192,384]{1,0:T(8,128)(2,1)S(1)}, u32[]{:S(2)}, u32[]{:S(2)}) %collective-permute-start.21) | collective-permute-done | bytes 147488 | tf_op jit(solution)/shard_map/ppermute | solution.py:207
  83.2 0.1 collective-permute-start.22
  83.3 0.1 add_convert_fusion
  83.4 3.9 %collective-permute-start.19 = (bf16[512,384]{1,0:T(8,128)(2,1)S(1)}, bf16[512,384]{1,0:T(8,128)(2,1)S(1)}, u32[]{:S(2)}, u32[]{:S(2)}) collective-permute-start(bf16[512,384]{1,0:T(8,128)(2,1)S(1)} %add_convert_fusion), channel_id=1, source_target_pairs={{4,0},{12,8},{16,12},{20,16},{28,24},{5,1},{13,9},{17,13},{21,17},... | collective-permute-start | bytes 1179656 | tf_op jit(solution)/shard_map/ppermute | solution.py:221
  87.3 0.1 convert_add_fusion
  87.5 0.5 collective-permute-done.13
  88.1 0.5 collective-permute-start.12
  88.6 0.9 fusion.4
  89.5 3.0 %collective-permute-done.20.refs_2_ = bf16[2,192,384]{2,1,0:T(8,128)(2,1)S(1)} collective-permute-done((bf16[2,192,384]{2,1,0:T(8,128)(2,1)S(1)}, bf16[2,192,384]{2,1,0:T(8,128)(2,1)S(1)}, u32[]{:S(2)}, u32[]{:S(2)}) %collective-permute-start.20) | collective-permute-done | bytes 294944 | tf_op jit(solution)/shard_map/ppermute | solution.py:207
  92.5 1.6 %assemble.1 = f32[384,1536]{1,0:T(8,128)} custom-call(bf16[192,384]{1,0:T(8,128)(2,1)S(1)} %get-tuple-element.62.refs_0_, bf16[192,384]{1,0:T(8,128)(2,1)S(1)} %collective-permute-done.18.refs_1_, bf16[2,192,384]{2,1,0:T(8,128)(2,1)S(1)} %collective-permute-done.20.refs_2_, bf16[192,384]{1,0:T(8,128)(2,1)S(1)} %get-tuple-element.61.refs_3_, ...), custom_call_target="tpu_custom_call" | custom-call | tf_op jit(solution)/shard_map/assemble/pallas_call | solution.py:336
  94.1 8.3 %collective-permute-done.19 = bf16[512,384]{1,0:T(8,128)(2,1)S(1)} collective-permute-done((bf16[512,384]{1,0:T(8,128)(2,1)S(1)}, bf16[512,384]{1,0:T(8,128)(2,1)S(1)}, u32[]{:S(2)}, u32[]{:S(2)}) %collective-permute-start.19) | collective-permute-done | bytes 393248 | tf_op jit(solution)/shard_map/ppermute | solution.py:221
  102.4 0.8 fusion.2
  103.2 0.8 fusion.1
  (36 shorter events, 0.4 us)
Async XLA Ops:
  0.6 26.2 %copy-start.1 = (bf16[512,384]{1,0:T(8,128)(2,1)S(1)}, bf16[512,384]{1,0:T(8,128)(2,1)}, u32[]{:S(2)}) copy-start(bf16[512,384]{1,0:T(8,128)(2,1)} %v.5) | copy-start | bytes 1179652
  0.6 7.3 %copy-start = (bf16[512,384]{1,0:T(8,128)(2,1)S(1)}, bf16[512,384]{1,0:T(8,128)(2,1)}, u32[]{:S(2)}) copy-start(bf16[512,384]{1,0:T(8,128)(2,1)} %k.5) | copy-start | bytes 1179652
  0.7 4.9 %copy-start.4 = (bf16[512,384]{1,0:T(8,128)(2,1)S(1)}, bf16[512,384]{1,0:T(8,128)(2,1)}, u32[]{:S(2)}) copy-start(bf16[512,384]{1,0:T(8,128)(2,1)} %rest_6_.1) | copy-start | bytes 1179652
  0.7 26.2 %copy-start.5 = (s32[8]{0:T(128)S(1)}, s32[8]{0:T(128)}, u32[]{:S(2)}) copy-start(s32[8]{0:T(128)} %anchor.5) | copy-start | bytes 100
  0.7 26.2 %copy-start.3 = (bf16[512,384]{1,0:T(8,128)(2,1)S(1)}, bf16[512,384]{1,0:T(8,128)(2,1)}, u32[]{:S(2)}) copy-start(bf16[512,384]{1,0:T(8,128)(2,1)} %q.5) | copy-start | bytes 1179652
  2.0 29.4 %copy-start.2 = (bf16[384,1536]{1,0:T(8,128)(2,1)S(1)}, bf16[384,1536]{1,0:T(8,128)(2,1)}, u32[]{:S(2)}) copy-start(bf16[384,1536]{1,0:T(8,128)(2,1)} %weight.3) | copy-start | bytes 3538948
  2.0 21.3 %collective-permute-start = (bf16[2,512,384]{2,1,0:T(8,128)(2,1)S(1)}, bf16[2,512,384]{2,1,0:T(8,128)(2,1)S(1)}, u32[]{:S(2)}, u32[]{:S(2)}) collective-permute-start(bf16[2,512,384]{2,1,0:T(8,128)(2,1)S(1)} %pad_maximum_fusion), channel_id=1, source_target_pairs={{0,4},{8,12},{12,16},{16,20},{24,28},{1,5},{9,13},{13,17},{17,21},... | collective-permute-start | bytes 2359304 | tf_op jit(solution)/shard_map/ppermute | solution.py:221
  5.6 10.6 %collective-permute-start.5 = (bf16[512,384]{1,0:T(8,128)(2,1)S(1)}, bf16[512,384]{1,0:T(8,128)(2,1)S(1)}, u32[]{:S(2)}, u32[]{:S(2)}) collective-permute-start(bf16[512,384]{1,0:T(8,128)(2,1)S(1)} %copy-done.4), channel_id=1, source_target_pairs={{0,2},{1,3},{2,0},{3,1},{4,6},{5,7},{6,4},{7,5},{8,10},{9,11},{10,... | collective-permute-start | bytes 1179656 | tf_op jit(solution)/shard_map/ppermute | solution.py:207
  7.1 25.5 %collective-permute-start.1 = (bf16[2,512,384]{2,1,0:T(8,128)(2,1)S(1)}, bf16[2,512,384]{2,1,0:T(8,128)(2,1)S(1)}, u32[]{:S(2)}, u32[]{:S(2)}) collective-permute-start(bf16[2,512,384]{2,1,0:T(8,128)(2,1)S(1)} %pad_maximum_fusion), channel_id=1, source_target_pairs={{8,16},{9,17},{10,18},{11,19}} | collective-permute-start | bytes 2359304 | tf_op jit(solution)/shard_map/ppermute | solution.py:221
  7.9 23.6 %collective-permute-start.4 = (bf16[512,384]{1,0:T(8,128)(2,1)S(1)}, bf16[512,384]{1,0:T(8,128)(2,1)S(1)}, u32[]{:S(2)}, u32[]{:S(2)}) collective-permute-start(bf16[512,384]{1,0:T(8,128)(2,1)S(1)} %copy-done.4), channel_id=1, source_target_pairs={{0,1},{1,0},{2,3},{3,2},{4,5},{5,4},{6,7},{7,6},{8,9},{9,8},{10,11... | collective-permute-start | bytes 1179656 | tf_op jit(solution)/shard_map/ppermute | solution.py:207
  7.9 24.7 %collective-permute-start.2 = (bf16[512,384]{1,0:T(8,128)(2,1)S(1)}, bf16[512,384]{1,0:T(8,128)(2,1)S(1)}, u32[]{:S(2)}, u32[]{:S(2)}) collective-permute-start(bf16[512,384]{1,0:T(8,128)(2,1)S(1)} %copy-done), channel_id=1, source_target_pairs={{8,20},{9,21},{10,22},{11,23}} | collective-permute-start | bytes 1179656 | tf_op jit(solution)/shard_map/ppermute | solution.py:221
  16.2 15.2 %collective-permute-start.6 = (bf16[512,384]{1,0:T(8,128)(2,1)S(1)}, bf16[512,384]{1,0:T(8,128)(2,1)S(1)}, u32[]{:S(2)}, u32[]{:S(2)}) collective-permute-start(bf16[512,384]{1,0:T(8,128)(2,1)S(1)} %collective-permute-done.5.third.rest_8_), channel_id=1, source_target_pairs={{0,1},{1,0},{2,3},{3,2},{4,5},{5,4},{6,7},{7,6},{8,9},{9,8},{10,11... | collective-permute-start | bytes 1179656 | tf_op jit(solution)/shard_map/ppermute | solution.py:207
  23.4 11.0 %collective-permute-start.3 = (bf16[512,384]{1,0:T(8,128)(2,1)S(1)}, bf16[512,384]{1,0:T(8,128)(2,1)S(1)}, u32[]{:S(2)}, u32[]{:S(2)}) collective-permute-start(bf16[512,384]{1,0:T(8,128)(2,1)S(1)} %slice_bitcast_fusion.1), channel_id=1, source_target_pairs={{12,20},{13,21},{14,22},{15,23}} | collective-permute-start | bytes 1179656 | tf_op jit(solution)/shard_map/ppermute | solution.py:221
  39.6 10.1 %collective-permute-start.8 = (bf16[2,192,384]{2,1,0:T(8,128)(2,1)S(1)}, bf16[2,192,384]{2,1,0:T(8,128)(2,1)S(1)}, u32[]{:S(2)}, u32[]{:S(2)}) collective-permute-start(bf16[2,192,384]{2,1,0:T(8,128)(2,1)S(1)} %get-tuple-element.57), channel_id=1, source_target_pairs={{0,8},{4,12},{8,0},{12,4},{16,24},{20,28},{24,16},{28,20},{1,9},{5... | collective-permute-start | bytes 884744 | tf_op jit(solution)/shard_map/ppermute | solution.py:207
  39.6 10.0 %collective-permute-start.7 = (bf16[2,192,384]{2,1,0:T(8,128)(2,1)S(1)}, bf16[2,192,384]{2,1,0:T(8,128)(2,1)S(1)}, u32[]{:S(2)}, u32[]{:S(2)}) collective-permute-start(bf16[2,192,384]{2,1,0:T(8,128)(2,1)S(1)} %get-tuple-element.58), channel_id=1, source_target_pairs={{0,4},{4,0},{8,12},{12,8},{16,20},{20,16},{24,28},{28,24},{1,5},{5... | collective-permute-start | bytes 884744 | tf_op jit(solution)/shard_map/ppermute | solution.py:207
  49.8 5.2 %collective-permute-start.10 = (bf16[192,384]{1,0:T(8,128)(2,1)S(1)}, bf16[192,384]{1,0:T(8,128)(2,1)S(1)}, u32[]{:S(2)}, u32[]{:S(2)}) collective-permute-start(bf16[192,384]{1,0:T(8,128)(2,1)S(1)} %fusion.11), channel_id=1, source_target_pairs={{0,4},{4,0},{8,12},{12,8},{16,20},{20,16},{24,28},{28,24},{1,5},{5... | collective-permute-start | bytes 442376 | tf_op jit(solution)/shard_map/ppermute | solution.py:207
  50.4 5.2 %collective-permute-start.9 = (bf16[192,384]{1,0:T(8,128)(2,1)S(1)}, bf16[192,384]{1,0:T(8,128)(2,1)S(1)}, u32[]{:S(2)}, u32[]{:S(2)}) collective-permute-start(bf16[192,384]{1,0:T(8,128)(2,1)S(1)} %fusion.10), channel_id=1, source_target_pairs={{0,8},{4,12},{8,0},{12,4},{16,24},{20,28},{24,16},{28,20},{1,9},{5... | collective-permute-start | bytes 442376 | tf_op jit(solution)/shard_map/ppermute | solution.py:207
  55.7 14.0 %collective-permute-start.14 = (bf16[384,384]{1,0:T(8,128)(2,1)S(1)}, bf16[384,384]{1,0:T(8,128)(2,1)S(1)}, u32[]{:S(2)}, u32[]{:S(2)}) collective-permute-start(bf16[384,384]{1,0:T(8,128)(2,1)S(1)} %pad_maximum_fusion.1), channel_id=1, source_target_pairs={{0,16},{4,20},{8,24},{12,28},{16,0},{20,4},{24,8},{28,12},{1,17},{... | collective-permute-start | bytes 884744 | tf_op jit(solution)/shard_map/ppermute | solution.py:207
  60.5 9.3 %collective-permute-start.15 = (bf16[512,384]{1,0:T(8,128)(2,1)S(1)}, bf16[512,384]{1,0:T(8,128)(2,1)S(1)}, u32[]{:S(2)}, u32[]{:S(2)}) collective-permute-start(bf16[512,384]{1,0:T(8,128)(2,1)S(1)} %get-tuple-element.40), channel_id=1, source_target_pairs={{16,20},{20,16},{17,21},{21,17},{18,22},{22,18},{19,23},{23,19}} | collective-permute-start | bytes 1179656 | tf_op jit(solution)/shard_map/ppermute | solution.py:221
  62.3 21.1 %collective-permute-start.11 = (bf16[2,512,384]{2,1,0:T(8,128)(2,1)S(1)}, bf16[2,512,384]{2,1,0:T(8,128)(2,1)S(1)}, u32[]{:S(2)}, u32[]{:S(2)}) collective-permute-start(bf16[2,512,384]{2,1,0:T(8,128)(2,1)S(1)} %get-tuple-element.43), channel_id=1, source_target_pairs={{0,1},{1,0},{2,3},{3,2},{4,5},{5,4},{6,7},{7,6},{8,9},{9,8},{10,11... | collective-permute-start | bytes 2359304 | tf_op jit(solution)/shard_map/ppermute | solution.py:207
  69.9 13.3 %collective-permute-start.17 = (bf16[512,384]{1,0:T(8,128)(2,1)S(1)}, bf16[512,384]{1,0:T(8,128)(2,1)S(1)}, u32[]{:S(2)}, u32[]{:S(2)}) collective-permute-start(bf16[512,384]{1,0:T(8,128)(2,1)S(1)} %add_convert_fusion.1), channel_id=1, source_target_pairs={{20,12},{21,13},{22,14},{23,15}} | collective-permute-start | bytes 1179656 | tf_op jit(solution)/shard_map/ppermute | solution.py:221
  71.3 5.2 %collective-permute-start.18 = (bf16[192,384]{1,0:T(8,128)(2,1)S(1)}, bf16[192,384]{1,0:T(8,128)(2,1)S(1)}, u32[]{:S(2)}, u32[]{:S(2)}) collective-permute-start(bf16[192,384]{1,0:T(8,128)(2,1)S(1)} %get-tuple-element.62.refs_0_), channel_id=1, source_target_pairs={{0,8},{4,12},{8,0},{12,4},{16,24},{20,28},{24,16},{28,20},{1,9},{5... | collective-permute-start | bytes 442376 | tf_op jit(solution)/shard_map/ppermute | solution.py:207
  72.0 11.1 %collective-permute-start.21 = (bf16[192,384]{1,0:T(8,128)(2,1)S(1)}, bf16[192,384]{1,0:T(8,128)(2,1)S(1)}, u32[]{:S(2)}, u32[]{:S(2)}) collective-permute-start(bf16[192,384]{1,0:T(8,128)(2,1)S(1)} %get-tuple-element.61.refs_3_), channel_id=1, source_target_pairs={{0,4},{4,0},{8,12},{12,8},{16,20},{20,16},{24,28},{28,24},{1,5},{5... | collective-permute-start | bytes 442376 | tf_op jit(solution)/shard_map/ppermute | solution.py:207
  72.7 15.4 %collective-permute-start.13 = (bf16[512,384]{1,0:T(8,128)(2,1)S(1)}, bf16[512,384]{1,0:T(8,128)(2,1)S(1)}, u32[]{:S(2)}, u32[]{:S(2)}) collective-permute-start(bf16[512,384]{1,0:T(8,128)(2,1)S(1)} %get-tuple-element.46), channel_id=1, source_target_pairs={{4,0},{12,8},{16,12},{20,16},{28,24},{5,1},{13,9},{17,13},{21,17},... | collective-permute-start | bytes 1179656 | tf_op jit(solution)/shard_map/ppermute | solution.py:221
  76.5 12.1 %collective-permute-start.16 = (bf16[512,384]{1,0:T(8,128)(2,1)S(1)}, bf16[512,384]{1,0:T(8,128)(2,1)S(1)}, u32[]{:S(2)}, u32[]{:S(2)}) collective-permute-start(bf16[512,384]{1,0:T(8,128)(2,1)S(1)} %add_convert_fusion.1), channel_id=1, source_target_pairs={{16,8},{17,9},{18,10},{19,11}} | collective-permute-start | bytes 1179656 | tf_op jit(solution)/shard_map/ppermute | solution.py:221
  83.2 9.3 %collective-permute-start.20 = (bf16[2,192,384]{2,1,0:T(8,128)(2,1)S(1)}, bf16[2,192,384]{2,1,0:T(8,128)(2,1)S(1)}, u32[]{:S(2)}, u32[]{:S(2)}) collective-permute-start(bf16[2,192,384]{2,1,0:T(8,128)(2,1)S(1)} %pad_maximum_fusion.2), channel_id=1, source_target_pairs={{0,4},{4,0},{8,12},{12,8},{16,20},{20,16},{24,28},{28,24},{1,5},{5... | collective-permute-start | bytes 884744 | tf_op jit(solution)/shard_map/ppermute | solution.py:207
  83.2 9.3 %collective-permute-start.22 = (bf16[2,192,384]{2,1,0:T(8,128)(2,1)S(1)}, bf16[2,192,384]{2,1,0:T(8,128)(2,1)S(1)}, u32[]{:S(2)}, u32[]{:S(2)}) collective-permute-start(bf16[2,192,384]{2,1,0:T(8,128)(2,1)S(1)} %pad_maximum_fusion.3), channel_id=1, source_target_pairs={{0,8},{4,12},{8,0},{12,4},{16,24},{20,28},{24,16},{28,20},{1,9},{5... | collective-permute-start | bytes 884744 | tf_op jit(solution)/shard_map/ppermute | solution.py:207
  83.4 19.0 %collective-permute-start.19 = (bf16[512,384]{1,0:T(8,128)(2,1)S(1)}, bf16[512,384]{1,0:T(8,128)(2,1)S(1)}, u32[]{:S(2)}, u32[]{:S(2)}) collective-permute-start(bf16[512,384]{1,0:T(8,128)(2,1)S(1)} %add_convert_fusion), channel_id=1, source_target_pairs={{4,0},{12,8},{16,12},{20,16},{28,24},{5,1},{13,9},{17,13},{21,17},... | collective-permute-start | bytes 1179656 | tf_op jit(solution)/shard_map/ppermute | solution.py:221
  88.1 15.1 %collective-permute-start.12 = (bf16[512,384]{1,0:T(8,128)(2,1)S(1)}, bf16[512,384]{1,0:T(8,128)(2,1)S(1)}, u32[]{:S(2)}, u32[]{:S(2)}) collective-permute-start(bf16[512,384]{1,0:T(8,128)(2,1)S(1)} %fusion.5), channel_id=1, source_target_pairs={{0,2},{1,3},{2,0},{3,1},{4,6},{5,7},{6,4},{7,5},{8,10},{9,11},{10,... | collective-permute-start | bytes 1179656 | tf_op jit(solution)/shard_map/ppermute | solution.py:207
